TPU v7x, 512 devices: a whole 4x8x8 slice. The times are simulated.
512 devices in a mesh: mem: 8 (over z_lo, core), space: 64 (over z_hi, x, y).
Axes of the slice: x: 4, y: 8, z: 8 (z_hi: 2, z_lo: 4; z = z_hi * 4 + z_lo), core: 2. Of those that a mesh axis runs over, the one named last changes fastest.
Arguments:
- log_perm: float32 [128, 128, 2048], P('space', 'mem'), may hold values from -2 to 2
- concentration: float32 [128, 128, 2048], P('space', 'mem'), may hold values from -6 to 6
- well_cells: int32 [128], replicated, may hold values from 0 to 262143
- obs_data: float32 [128], replicated, may hold values from -6 to 6
- obs_var: float32 [128], replicated, may hold values from 0.05 to 0.5
- obs_noise: float32 [128, 128], P('mem'), may hold values from -6 to 6
Outputs:
- forecast: float32 [128, 128, 2048], P('space', 'mem')
- updated_log_perm: float32 [128, 128, 2048], P('space', 'mem')
Inputs may be any that keep to these rules, and one draw needn't show every extreme that they name: `well_cells`: cells flattened as row times 2048 plus column.
All inputs are finite; a program needn't handle non-finite values.
Results may differ from a plain program's by a relative error of at most 0.0034.
Values may be sent and summed in bfloat16 or wider, within the bound.
No kernel may reach another device: no remote copies, remote signals or barrier semaphores. Data moves between devices by JAX's collectives and lax.ppermute only.
A program may use at most 128 MiB of HBM per device.

v0:
```python
import jax
import jax.numpy as jnp
from jax import lax
from jax.sharding import PartitionSpec as P

time_step = 0.03
inflation = 4.0


def with_halo(block, sides, width):
    for axis, dim in sides:
        count = lax.axis_size(axis)
        forward = [(i, i + 1) for i in range(count - 1)]
        backward = [(target, source) for source, target in forward]
        low = lax.ppermute(
            lax.slice_in_dim(block, block.shape[dim] - width, None, axis=dim), axis, forward
        )
        high = lax.ppermute(lax.slice_in_dim(block, 0, width, axis=dim), axis, backward)
        block = jnp.concatenate([low, block, high], axis=dim)
    return block


def advance(conc_ext, conduct_ext):
    conc_pad = jnp.pad(conc_ext, ((0, 0), (0, 0), (1, 1)))
    cond_pad = jnp.pad(conduct_ext, ((0, 0), (0, 0), (1, 1)))
    centre = conc_pad[1:-1, :, 1:-1]
    centre_cond = cond_pad[1:-1, :, 1:-1]
    inflow = jnp.zeros_like(centre)
    sides = (
        (conc_pad[:-2, :, 1:-1], cond_pad[:-2, :, 1:-1]),
        (conc_pad[2:, :, 1:-1], cond_pad[2:, :, 1:-1]),
        (conc_pad[1:-1, :, :-2], cond_pad[1:-1, :, :-2]),
        (conc_pad[1:-1, :, 2:], cond_pad[1:-1, :, 2:]),
    )
    for conc_side, cond_side in sides:
        inflow = inflow + 0.5 * (centre_cond + cond_side) * (conc_side - centre)
    return centre + time_step * inflow


def cholesky_solve(matrix, target):
    factor = jnp.linalg.cholesky(matrix)
    middle = lax.linalg.triangular_solve(factor, target, left_side=True, lower=True)
    return lax.linalg.triangular_solve(factor, middle, left_side=True, lower=True, transpose_a=True)


def transform(predicted, noise_all, obs_data, obs_var):
    members = predicted.shape[0]
    anomaly = predicted - jnp.mean(predicted, axis=0, keepdims=True)
    covariance = jnp.dot(
        anomaly.T, anomaly, precision=lax.Precision.HIGHEST, preferred_element_type=jnp.float32
    ) / (members - 1) + inflation * jnp.diag(obs_var)
    innovation = obs_data[None, :] + jnp.sqrt(inflation * obs_var)[None, :] * noise_all - predicted
    solved = cholesky_solve(covariance, innovation.T)
    weights = jnp.dot(
        anomaly, solved, precision=lax.Precision.HIGHEST, preferred_element_type=jnp.float32
    ) / (members - 1)
    centred = weights - jnp.mean(weights, axis=0, keepdims=True)
    return centred.astype(jnp.bfloat16)


def local(log_perm, concentration, well_cells, obs_data, obs_var, obs_noise):
    row_count, member_dev, col_count = log_perm.shape
    tile_index = lax.axis_index("space")
    group_index = lax.axis_index("mem")
    conduct = jnp.exp(log_perm)
    tracer = concentration
    for repeat in range(2):
        padded = with_halo(jnp.stack([tracer, conduct]), (("space", 1),), 1)
        tracer = advance(padded[0], padded[1])
    first_cell = tile_index * (row_count * col_count)
    local_cell = well_cells - first_cell
    inside_tile = (local_cell >= 0) & (local_cell < row_count * col_count)
    clipped = jnp.clip(local_cell, 0, row_count * col_count - 1)
    picked = tracer[clipped // col_count, :, clipped % col_count]
    picked = jnp.where(inside_tile[:, None], picked, 0.0).T
    summed = lax.psum(picked, "space")
    predicted, noise_all = (
        lax.all_gather(summed, "mem", axis=0, tiled=True),
        lax.all_gather(obs_noise, "mem", axis=0, tiled=True),
    )
    centred = transform(predicted, noise_all, obs_data, obs_var)
    perm_low = log_perm.astype(jnp.bfloat16)
    my_columns = lax.dynamic_slice_in_dim(centred, group_index * member_dev, member_dev, 1)
    increment = jnp.einsum(
        "xiy,ij->xjy",
        lax.all_gather(perm_low, "mem", axis=1, tiled=True),
        my_columns,
        preferred_element_type=jnp.float32,
    )
    return (tracer, log_perm + increment)


def solution(mesh):
    return jax.shard_map(
        local,
        mesh=mesh,
        in_specs=(P("space", "mem", None), P("space", "mem", None), P(), P(), P(), P("mem", None)),
        out_specs=(P("space", "mem", None), P("space", "mem", None)),
        check_vma=False,
    )
```

profile of v0, /device:TPU:1, one launch (start us, length us, event | category | flops | bytes accessed | tf_op | source)
XLA Modules:
  0.0 537.2 jit_solution(17036058877172273697)
XLA Ops:
  7.2 1.0 exponential_bitcast_fusion
  8.2 1.0 fusion.10
  9.2 1.3 collective-permute-start.1
  10.5 4.7 collective-permute-start
  15.2 0.7 fusion.75
  15.9 1.1 collective-permute-done.1
  17.0 1.5 collective-permute-done
  18.5 1.0 fusion.2
  19.8 0.6 copy-done.1
  20.5 0.9 fusion.79
  21.5 1.3 collective-permute-start.3
  22.8 4.7 collective-permute-start.2
  27.6 21.4 %all_gather.10 = f32[128,128]{1,0:T(8,128)S(1)} all-gather(f32[16,128]{1,0:T(8,128)S(1)} %copy-done.3), channel_id=1, replica_groups=mesh['mem'=8,'space'=64] {'mem'}, dimensions={0}, use_global_device_ids=true | all-gather | bytes 73728 | tf_op jit(solution)/shard_map/all_gather | solution.py:79
  49.4 0.4 fusion.29
  49.8 0.6 copy.44
  50.4 1.2 gather_fusion
  51.7 382.8 %psum.7 = f32[16,128]{0,1:T(8,128)S(1)} all-reduce(f32[16,128]{0,1:T(8,128)S(1)} %select_bitcast_fusion), channel_id=1, replica_groups=mesh['mem'=8,'space'=64] {'space'}, use_global_device_ids=true, to_apply=%region_0.1 | all-reduce | flops 2048 | bytes 16384 | tf_op jit(solution)/shard_map/psum | solution.py:76
  434.5 69.2 %all_gather.9 = f32[128,128]{1,0:T(8,128)S(1)} all-gather(f32[16,128]{1,0:T(8,128)S(1)} %copy.45), channel_id=1, replica_groups=mesh['mem'=8,'space'=64] {'mem'}, dimensions={0}, use_global_device_ids=true | all-gather | bytes 73728 | tf_op jit(solution)/shard_map/all_gather | solution.py:78
  504.3 11.7 %cholesky.16 = f32[128,128]{1,0:T(8,128)S(1)} custom-call(f32[128,128]{1,0:T(8,128)S(1)} %fusion.59), custom_call_target="Cholesky" | custom-call | tf_op jit(solution)/shard_map/jit(cholesky)/cholesky | solution.py:41
  516.0 0.7 compare_reduce_fusion
  516.7 0.6 fusion.53
  517.3 9.8 %custom-call.8 = f32[1,128,128]{1,2,0:T(8,128)S(1)} custom-call(f32[1,128,128]{2,1,0:T(8,128)S(1)} %fusion.53), custom_call_target="InvertDiagBlocksLowerTriangular" | custom-call | tf_op jit(solution)/shard_map/triangular_solve | solution.py:43
  527.7 0.4 fusion.80
  528.1 2.2 fusion
  (38 shorter events, 2.0 us)
Async XLA Ops:
  7.2 521.0 %all-gather.2.cloned.1.call-start = ((), (), s32[]{:S(2)}) async-start(), calls=%async_computation | async-start | bytes 1179648 | tf_op jit(solution)/shard_map/all_gather | solution.py:86
  9.2 7.8 %collective-permute-start.1 = (f32[2,1,16,2048]{3,2,1,0:T(8,128)S(1)}, f32[2,1,16,2048]{3,2,1,0:T(8,128)S(1)}, u32[]{:S(2)}, u32[]{:S(2)}) collective-permute-start(f32[2,1,16,2048]{3,2,1,0:T(8,128)S(1)} %get-tuple-element.17), channel_id=1, source_target_pairs={{1,0},{2,1},{3,2},{4,3},{5,4},{6,5},{7,6},{8,7},{9,8},{10,9},{11,1... | collective-permute-start | bytes 786440 | tf_op jit(solution)/shard_map/ppermute | solution.py:18
  10.5 8.0 %collective-permute-start = (f32[2,1,16,2048]{3,2,1,0:T(8,128)S(1)}, f32[2,1,16,2048]{3,2,1,0:T(8,128)S(1)}, u32[]{:S(2)}, u32[]{:S(2)}) collective-permute-start(f32[2,1,16,2048]{3,2,1,0:T(8,128)S(1)} %get-tuple-element.16), channel_id=1, source_target_pairs={{0,1},{1,2},{2,3},{3,4},{4,5},{5,6},{6,7},{7,8},{8,9},{9,10},{10,1... | collective-permute-start | bytes 786440 | tf_op jit(solution)/shard_map/ppermute | solution.py:15
  15.9 3.7 copy-start
  19.5 1.0 copy-start.1
  19.8 7.7 %copy-start.6 = (s32[128]{0:T(128)S(1)}, s32[128]{0:T(128)}, u32[]{:S(2)}) copy-start(s32[128]{0:T(128)} %param.8) | copy-start | bytes 1540
  19.8 7.7 %copy-start.3 = (f32[16,128]{1,0:T(8,128)S(1)}, f32[16,128]{1,0:T(8,128)}, u32[]{:S(2)}) copy-start(f32[16,128]{1,0:T(8,128)} %param.11) | copy-start | bytes 24580
  19.8 29.1 %copy-start.4 = (f32[128]{0:T(128)S(1)}, f32[128]{0:T(128)}, u32[]{:S(2)}) copy-start(f32[128]{0:T(128)} %param.10) | copy-start | bytes 1540
  21.5 27.5 %collective-permute-start.3 = (f32[2,1,16,2048]{3,2,1,0:T(8,128)S(1)}, f32[2,1,16,2048]{3,2,1,0:T(8,128)S(1)}, u32[]{:S(2)}, u32[]{:S(2)}) collective-permute-start(f32[2,1,16,2048]{3,2,1,0:T(8,128)S(1)} %get-tuple-element.13), channel_id=1, source_target_pairs={{1,0},{2,1},{3,2},{4,3},{5,4},{6,5},{7,6},{8,7},{9,8},{10,9},{11,1... | collective-permute-start | bytes 786440 | tf_op jit(solution)/shard_map/ppermute | solution.py:18
  22.8 26.3 %collective-permute-start.2 = (f32[2,1,16,2048]{3,2,1,0:T(8,128)S(1)}, f32[2,1,16,2048]{3,2,1,0:T(8,128)S(1)}, u32[]{:S(2)}, u32[]{:S(2)}) collective-permute-start(f32[2,1,16,2048]{3,2,1,0:T(8,128)S(1)} %get-tuple-element.12), channel_id=1, source_target_pairs={{0,1},{1,2},{2,3},{3,4},{4,5},{5,6},{6,7},{7,8},{8,9},{9,10},{10,1... | collective-permute-start | bytes 786440 | tf_op jit(solution)/shard_map/ppermute | solution.py:15
  49.7 477.7 %copy-start.2 = (f32[2,16,2048]{2,1,0:T(8,128)}, f32[2,16,2048]{2,1,0:T(8,128)S(1)}, u32[]{:S(2)}) copy-start(f32[2,16,2048]{2,1,0:T(8,128)S(1)} %fusion.29) | copy-start | bytes 786436
  49.7 477.4 %copy-start.5 = (f32[128]{0:T(128)S(1)}, f32[128]{0:T(128)}, u32[]{:S(2)}) copy-start(f32[128]{0:T(128)} %param.9) | copy-start | bytes 1540
Sparse Core Ops, SparseCore 0:
  49.1 50.8 all-gather.1
where the time goes:
time: 547 us; the launch traced here: 537 us
  blocking collectives  473 us (86%)
  other arithmetic  27.6 us (5%)
  between operations  14.3 us (3%)
  starting transfers between devices  12 us (2%)
    psum x1, blocking collectives, local(): summed = lax.psum(picked, 'space')  383 us
    all_gather x1, blocking collectives, local(): lax.all_gather(summed, 'mem', axis=0, tiled=True)  69.2 us
    all_gather x1, blocking collectives, local(): lax.all_gather(obs_noise, 'mem', axis=0, tiled=True)  21.4 us
    another operation x3, other arithmetic, cholesky_solve(): factor = jnp.linalg.cholesky(matrix)  12.4 us
  transfers between devices with their start and end apart: 5, of which 2 were waited for; matrix products, arithmetic and copies ran while one was open for 5% of the time, Pallas kernels for 0%

commit v1 on v0

v1 whole, which is shorter than its diff:
```python
import jax
import jax.numpy as jnp
from jax import lax
from jax.experimental import pallas as pl
from jax.experimental.pallas import tpu as pltpu
from jax.sharding import Mesh, PartitionSpec as P

F32, BF16 = jnp.float32, jnp.bfloat16
time_step = 0.03
inflation = 4.0
HIGH = lax.Precision.HIGHEST
TN = (((0,), (0,)), ((), ()))
PANEL = 16
MEM = ("z_lo", "core")
SPACE = ("z_hi", "x", "y")
ORDER = (0, 2, 4, 6, 1, 3, 5, 7)
VMEM_LIMIT = 48 * 1024 * 1024

def split3(x):
    hi = x.astype(BF16)
    rest = x - hi.astype(F32)
    mid = rest.astype(BF16)
    low = (rest - mid.astype(F32)).astype(BF16)
    return hi, mid, low


def factor_panel(rows, base):
    height = rows.shape[0]
    index = lax.broadcasted_iota(jnp.int32, (height, 128), 0)
    lanes = rows.shape[1] // 128
    cols = [jnp.broadcast_to(rows[:, base + c : base + c + 1], (height, 128)) for c in range(height)]
    tiles = [rows[:, t * 128 : (t + 1) * 128] for t in range(lanes)]
    for k in range(height):
        scale = lax.rsqrt(cols[k][k : k + 1, :])
        below = cols[k] * scale
        masked = jnp.where(index > k, below, 0.0)
        for c in range(k + 1, height):
            cols[c] = cols[c] - masked * below[c : c + 1, :]
        for t in range(lanes):
            top = tiles[t][k : k + 1, :] * scale
            tiles[t] = jnp.where(index == k, top, tiles[t] - masked * top)
    return jnp.concatenate(tiles, axis=1)


def weights_of(pred, own_noise, obs_data, obs_var, work, solved):
    members = pred.shape[0]
    anomaly = pred - jnp.mean(pred, axis=0, keepdims=True)
    innovation = obs_data + jnp.sqrt(inflation * obs_var) * own_noise - pred[:16]
    cov = lax.dot_general(anomaly, anomaly, TN, precision=HIGH, preferred_element_type=F32) / (members - 1)
    r = lax.broadcasted_iota(jnp.int32, (128, 128), 0)
    c = lax.broadcasted_iota(jnp.int32, (128, 128), 1)
    cov = cov + jnp.where(r == c, jnp.broadcast_to(inflation * obs_var, (128, 128)), 0.0)
    work[:, 0:128] = cov
    work[:, 128:256] = anomaly.T
    padded = jnp.concatenate([innovation, jnp.zeros((112, 128), F32)], axis=0)
    work[:, 256:384] = padded.T
    for p in range(128 // PANEL):
        u = factor_panel(work[p * PANEL : (p + 1) * PANEL, :], p * PANEL)
        solved[p * PANEL : (p + 1) * PANEL, :] = u[:, 128:384]
        if p < 128 // PANEL - 1:
            h, m, l = split3(u)
            left = jnp.concatenate([h, h, m, h, l, m], axis=0)[:, 0:128]
            right = jnp.concatenate([h, m, h, l, h, m], axis=0)
            update = lax.dot_general(left, right, TN, preferred_element_type=F32)
            work[(p + 1) * PANEL :, :] = work[(p + 1) * PANEL :, :] - update[(p + 1) * PANEL :, :]
    w = lax.dot_general(
        solved[:, 128:256], solved[:, 0:128], TN, precision=HIGH, preferred_element_type=F32
    )[:16] / (members - 1)
    return w - jnp.mean(w, axis=1, keepdims=True)


def along_row(conc, link, left_edge):
    width = conc.shape[1]
    lane = lax.broadcasted_iota(jnp.int32, conc.shape, 1)
    right = jnp.where(lane == width - 1, 0.0, pltpu.roll(conc, width - 1, 1))
    flux = link * (right - conc)
    from_left = jnp.where(lane == 0, left_edge * conc, pltpu.roll(flux, 1, 1))
    return flux - from_left


def link_right(conduct):
    width = conduct.shape[1]
    lane = lax.broadcasted_iota(jnp.int32, conduct.shape, 1)
    return 0.5 * (conduct + jnp.where(lane == width - 1, 0.0, pltpu.roll(conduct, width - 1, 1)))


def prepare_kernel(perm_ref, conc_ref, up_ref, down_ref, low_ref, part_ref, conduct_ref):
    perm0, perm1 = perm_ref[0], perm_ref[1]
    conc0, conc1 = conc_ref[0], conc_ref[1]
    low_ref[0], low_ref[1] = perm0.astype(BF16), perm1.astype(BF16)
    cond0, cond1 = jnp.exp(perm0), jnp.exp(perm1)
    conduct_ref[0], conduct_ref[1] = cond0, cond1
    between = 0.5 * (cond0 + cond1) * (conc1 - conc0)
    part0 = conc0 + time_step * (along_row(conc0, link_right(cond0), 0.5 * cond0) + between)
    part1 = conc1 + time_step * (along_row(conc1, link_right(cond1), 0.5 * cond1) - between)
    part_ref[0], part_ref[1] = part0, part1
    down_ref[0], down_ref[1], down_ref[2] = conc0.astype(BF16), cond0.astype(BF16), part0.astype(BF16)
    up_ref[0], up_ref[1], up_ref[2] = conc1.astype(BF16), cond1.astype(BF16), part1.astype(BF16)


def prepare(log_perm, conc):
    rows, members, width = log_perm.shape
    edge = jax.ShapeDtypeStruct((3, members, width), BF16)
    full = jax.ShapeDtypeStruct(log_perm.shape, F32)
    return pl.pallas_call(
        prepare_kernel,
        out_shape=(edge, edge, jax.ShapeDtypeStruct(log_perm.shape, BF16), full, full),
        cost_estimate=pl.CostEstimate(flops=2_000_000, bytes_accessed=1_600_000, transcendentals=65536),
        compiler_params=pltpu.CompilerParams(vmem_limit_bytes=VMEM_LIMIT),
        name="prepare",
    )(log_perm, conc)


def advance_kernel(place_ref, conc_ref, conduct_ref, part_ref, above_ref, below_ref, wells_ref, out_ref, picked_ref):
    strip = place_ref[0]
    conc0, conc1 = conc_ref[0], conc_ref[1]
    cond0, cond1 = conduct_ref[0], conduct_ref[1]
    conc_a, cond_a, part_a = [above_ref[i].astype(F32) for i in range(3)]
    conc_b, cond_b, part_b = [below_ref[i].astype(F32) for i in range(3)]
    link_a = 0.5 * (cond0 + cond_a)
    link_b = 0.5 * (cond1 + cond_b)
    gain_a = time_step * (link_a * (conc_a - conc0))
    gain_b = time_step * (link_b * (conc_b - conc1))
    once0, once1 = part_ref[0] + gain_a, part_ref[1] + gain_b
    once_a = jnp.where(strip == 0, 0.0, part_a - gain_a)
    once_b = jnp.where(strip == STRIPS - 1, 0.0, part_b - gain_b)
    between = 0.5 * (cond0 + cond1) * (once1 - once0)
    twice0 = once0 + time_step * (
        along_row(once0, link_right(cond0), 0.5 * cond0) + between + link_a * (once_a - once0)
    )
    twice1 = once1 + time_step * (
        along_row(once1, link_right(cond1), 0.5 * cond1) - between + link_b * (once_b - once1)
    )
    out_ref[0], out_ref[1] = twice0, twice1
    members, width = twice0.shape
    chunk = 256
    total = jnp.zeros((3 * members, 128), F32)
    for row, values in enumerate((twice0, twice1)):
        pieces = jnp.concatenate(split3(values), axis=0)
        column = wells_ref[...] - (2 * strip + row) * width
        for start in range(0, width, chunk):
            here = lax.broadcasted_iota(jnp.int32, (chunk, 128), 0) + start
            chosen = jnp.where(here == column, 1.0, 0.0).astype(BF16)
            total = total + jnp.dot(pieces[:, start : start + chunk], chosen, preferred_element_type=F32)
    picked = total[:members] + total[members : 2 * members] + total[2 * members :]
    for copy in range(picked_ref.shape[0]):
        picked_ref[copy] = picked


def advance(place, conc, conduct, part, above, below, wells, copies):
    vmem = pl.BlockSpec(memory_space=pltpu.VMEM)
    return pl.pallas_call(
        advance_kernel,
        out_shape=(
            jax.ShapeDtypeStruct(conc.shape, F32),
            jax.ShapeDtypeStruct((copies, conc.shape[1], 128), F32),
        ),
        in_specs=[pl.BlockSpec(memory_space=pltpu.SMEM)] + [vmem] * 6,
        out_specs=(vmem, vmem),
        cost_estimate=pl.CostEstimate(flops=60_000_000, bytes_accessed=1_800_000, transcendentals=0),
        compiler_params=pltpu.CompilerParams(vmem_limit_bytes=VMEM_LIMIT),
        name="advance",
    )(place, conc, conduct, part, above, below, wells)


def update_kernel(place_ref, found_ref, noise_ref, data_ref, var_ref, perm_ref, even_ref, odd_ref, out_ref, pred, work, solved, low, sem):
    group = place_ref[1]
    copies = []
    for position in range(8):
        source = (even_ref if position < 4 else odd_ref).at[position % 4]
        for row in range(2):
            copies.append(
                pltpu.make_async_copy(source.at[row], low.at[row, pl.ds(position * 16, 16)], sem.at[position, row])
            )
    for copy in copies:
        copy.start()
    for position, flip in enumerate(ORDER):
        block = lax.bitwise_xor(group, flip)
        pred[pl.ds(position * 16, 16), :] = found_ref[2 * block] + found_ref[2 * block + 1]
    centred = weights_of(pred[...], noise_ref[...], data_ref[...], var_ref[...], work, solved).astype(BF16)
    for copy in copies:
        copy.wait()
    for row in range(2):
        out_ref[row] = perm_ref[row] + jnp.dot(centred, low[row], preferred_element_type=F32)


def update(place, found, noise, obs_data, obs_var, log_perm, even, odd):
    vmem = pl.BlockSpec(memory_space=pltpu.VMEM)
    anywhere = pl.BlockSpec(memory_space=pl.ANY)
    rows, members, width = log_perm.shape
    return pl.pallas_call(
        update_kernel,
        out_shape=jax.ShapeDtypeStruct(log_perm.shape, F32),
        in_specs=[pl.BlockSpec(memory_space=pltpu.SMEM)] + [vmem] * 5 + [anywhere] * 2,
        out_specs=vmem,
        scratch_shapes=[
            pltpu.VMEM((128, 128), F32),
            pltpu.VMEM((128, 384), F32),
            pltpu.VMEM((128, 256), F32),
            pltpu.VMEM((rows, 128, width), BF16),
            pltpu.SemaphoreType.DMA((8, 2)),
        ],
        cost_estimate=pl.CostEstimate(flops=200_000_000, bytes_accessed=1_700_000, transcendentals=128),
        compiler_params=pltpu.CompilerParams(vmem_limit_bytes=VMEM_LIMIT),
        name="update",
    )(place, found, noise, obs_data, obs_var, log_perm, even, odd)


STRIPS = 64


def shifted(value, shift):
    pairs = [(i, i + shift) for i in range(STRIPS) if 0 <= i + shift < STRIPS]
    return lax.ppermute(value, SPACE, pairs)


def swapped(value, axis, flip):
    return lax.ppermute(value, axis, [(i, i ^ flip) for i in range(lax.axis_size(axis))])


def local(log_perm, concentration, well_cells, obs_data, obs_var, obs_noise):
    place = jnp.stack([lax.axis_index(SPACE), lax.axis_index(MEM)]).astype(jnp.int32)
    up, down, low, part, conduct = prepare(log_perm, concentration)
    above, below = shifted(up, 1), shifted(down, -1)
    two = jnp.stack([low, swapped(low, "z_lo", 1)])
    even = jnp.concatenate([two, swapped(two, "z_lo", 2)])
    odd = swapped(even, "core", 1)
    tracer, picked = advance(place, concentration, conduct, part, above, below, well_cells[None], 32)
    found = lax.all_to_all(picked, ("x", "y"), 0, 0, tiled=True)
    found = jnp.broadcast_to(jnp.sum(found, axis=0)[None], (16, 16, 128))
    found = lax.all_to_all(found, ("z_lo", "core", "z_hi"), 0, 0, tiled=True)
    updated = update(place, found, obs_noise, obs_data[None], obs_var[None], log_perm, even, odd)
    return (tracer, updated)


def solution(mesh):
    fine = Mesh(mesh.devices.reshape(4, 2, 2, 4, 8), MEM + SPACE)
    return jax.shard_map(
        local,
        mesh=fine,
        in_specs=(P(SPACE, MEM, None), P(SPACE, MEM, None), P(), P(), P(), P(MEM, None)),
        out_specs=(P(SPACE, MEM, None), P(SPACE, MEM, None)),
        check_vma=False,
    )
```

time: 547 us -> 86.9 us (0.16); the launches traced: 537 us -> 86.5 us
  blocking collectives: 473 us -> 0 us
  starting transfers between devices: 12 us -> 51.1 us
  other arithmetic: 27.6 us -> 0.19 us
  waiting for transfers between devices: 2.62 us -> 21.2 us
  between operations: 14.3 us -> 0.75 us
  Pallas kernels: 0 us -> 9.32 us
    psum x1 -> x0, blocking collectives: 383 us -> none  [local(): summed = lax.psum(picked, 'space')]
    all_gather x2 -> x0, blocking collectives: 90.6 us -> none  [the longest x1 69.2 us: local(): lax.all_gather(summed, 'mem', axis=0, tiled=True)]
    all_to_all x0 -> x2, starting transfers between devices: none -> 29.9 us  [the longest x1 21.4 us: local(): found = lax.all_to_all(picked, ('x', 'y'), 0, 0, tiled=True)]
    another operation x7 -> x2, other arithmetic: 23.9 us -> 0.1 us  [the longest x1 0.08 us: local(): jnp.stack([lax.axis_index(SPACE), lax.axis_index(MEM)]).astype(jnp.int32)]
    all_to_all x0 -> x2, waiting for transfers between devices: none -> 13.5 us  [the longest x1 8.95 us: local(): found = lax.all_to_all(found, ('z_lo', 'core', 'z_hi'), 0, 0, tiled=True)]
    pallas_call x0 -> x3, Pallas kernels: none -> 9.32 us  [the longest x1 7.05 us: update(): pl.pallas_call(update_kernel, out_shape=jax.ShapeDtypeStruct(log_perm.sha...]
    ppermute x4 -> x5, starting transfers between devices: 12 us -> 21.2 us  [the longest x3 16.7 us: swapped(): lax.ppermute(value, axis, [(i, i ^ flip) for i in range(lax.axis_size(axi...]
  transfers between devices with their start and end apart: 5 -> 7, of which waited for: 2 -> 5; matrix products, arithmetic and copies ran while one was open for 5% -> 1% of each run, Pallas kernels for 0% -> 2%
where the time goes in v1:
time: 86.9 us; the launch traced here: 86.5 us
  starting transfers between devices  51.1 us (59%)
  waiting for transfers between devices  21.2 us (24%)
  Pallas kernels  9.32 us (11%)
  local copies, waits for them, and re-layouts  3.89 us (4%)
    all_to_all x1, starting transfers between devices, local(): found = lax.all_to_all(picked, ('x', 'y'), 0, 0, tiled=True)  21.4 us
    ppermute x3, starting transfers between devices, swapped(): lax.ppermute(value, axis, [(i, i ^ flip) for i in range(lax.axis_size(axi...  16.7 us
    all_to_all x1, waiting for transfers between devices, local(): found = lax.all_to_all(found, ('z_lo', 'core', 'z_hi'), 0, 0, tiled=True)  8.95 us
    all_to_all x1, starting transfers between devices, local(): found = lax.all_to_all(found, ('z_lo', 'core', 'z_hi'), 0, 0, tiled=True)  8.5 us
    pallas_call x1, Pallas kernels, update(): pl.pallas_call(update_kernel, out_shape=jax.ShapeDtypeStruct(log_perm.sha...  7.05 us
    ppermute x2, waiting for transfers between devices, shifted(): return lax.ppermute(value, SPACE, pairs)  5.32 us
    all_to_all x1, waiting for transfers between devices, local(): found = lax.all_to_all(picked, ('x', 'y'), 0, 0, tiled=True)  4.58 us
    ppermute x2, starting transfers between devices, shifted(): return lax.ppermute(value, SPACE, pairs)  4.5 us
  transfers between devices with their start and end apart: 7, of which 5 were waited for; matrix products, arithmetic and copies ran while one was open for 1% of the time, Pallas kernels for 2%

profile of v1, /device:TPU:1, one launch (start us, length us, event | category | flops | bytes accessed | tf_op | source)
XLA Modules:
  0.0 86.5 jit_solution(9127553519598280730)
XLA Ops:
  0.6 0.0 copy-start
  0.6 0.9 %copy-done = f32[2,16,2048]{2,1,0:T(8,128)S(1)} copy-done((f32[2,16,2048]{2,1,0:T(8,128)S(1)}, f32[2,16,2048]{2,1,0:T(8,128)}, u32[]{:S(2)}) %copy-start) | copy-done | bytes 262168
  1.6 0.9 %copy-done.2 = f32[2,16,2048]{2,1,0:T(8,128)S(1)} copy-done((f32[2,16,2048]{2,1,0:T(8,128)S(1)}, f32[2,16,2048]{2,1,0:T(8,128)}, u32[]{:S(2)}) %copy-start.2) | copy-done | bytes 262168
  2.5 0.4 prepare.1
  2.9 4.8 %collective-permute-start.2 = (bf16[2,16,2048]{2,1,0:T(8,128)(2,1)S(1)}, bf16[2,16,2048]{2,1,0:T(8,128)(2,1)S(1)}, u32[]{:S(2)}, u32[]{:S(2)}) collective-permute-start(bf16[2,16,2048]{2,1,0:T(8,128)(2,1)S(1)} %get-tuple-element.15), channel_id=1, source_target_pairs={{0,128},{128,0},{256,384},{384,256},{1,129},{129,1},{257,385},{385... | collective-permute-start | bytes 393224 | tf_op jit(solution)/shard_map/ppermute | solution.py:218
  7.7 2.3 %collective-permute-done.2 = bf16[2,16,2048]{2,1,0:T(8,128)(2,1)S(1)} collective-permute-done((bf16[2,16,2048]{2,1,0:T(8,128)(2,1)S(1)}, bf16[2,16,2048]{2,1,0:T(8,128)(2,1)S(1)}, u32[]{:S(2)}, u32[]{:S(2)}) %collective-permute-start.2) | collective-permute-done | bytes 131104 | tf_op jit(solution)/shard_map/ppermute | solution.py:218
  10.1 6.8 %collective-permute-start.3 = (bf16[2,2,16,2048]{3,2,1,0:T(8,128)(2,1)S(1)}, bf16[2,2,16,2048]{3,2,1,0:T(8,128)(2,1)S(1)}, u32[]{:S(2)}, u32[]{:S(2)}) collective-permute-start(bf16[2,2,16,2048]{3,2,1,0:T(8,128)(2,1)S(1)} %pad_maximum_fusion.1), channel_id=1, source_target_pairs={{0,256},{128,384},{256,0},{384,128},{1,257},{129,385},{257,1},{385... | collective-permute-start | bytes 786440 | tf_op jit(solution)/shard_map/ppermute | solution.py:218
  16.9 3.2 %collective-permute-start = (bf16[3,16,2048]{2,1,0:T(8,128)(2,1)S(1)}, bf16[3,16,2048]{2,1,0:T(8,128)(2,1)S(1)}, u32[]{:S(2)}, u32[]{:S(2)}) collective-permute-start(bf16[3,16,2048]{2,1,0:T(8,128)(2,1)S(1)} %get-tuple-element.11), channel_id=1, source_target_pairs={{0,1},{1,2},{2,3},{3,4},{4,5},{5,6},{6,7},{7,8},{8,9},{9,10},{10,1... | collective-permute-start | bytes 589832 | tf_op jit(solution)/shard_map/ppermute | solution.py:214
  20.1 1.3 %collective-permute-start.1 = (bf16[3,16,2048]{2,1,0:T(8,128)(2,1)S(1)}, bf16[3,16,2048]{2,1,0:T(8,128)(2,1)S(1)}, u32[]{:S(2)}, u32[]{:S(2)}) collective-permute-start(bf16[3,16,2048]{2,1,0:T(8,128)(2,1)S(1)} %get-tuple-element.12), channel_id=1, source_target_pairs={{1,0},{2,1},{3,2},{4,3},{5,4},{6,5},{7,6},{8,7},{9,8},{10,9},{11,1... | collective-permute-start | bytes 589832 | tf_op jit(solution)/shard_map/ppermute | solution.py:214
  21.5 0.1 pad_add_fusion.place_ref
  21.5 1.2 %collective-permute-done.above_ref = bf16[3,16,2048]{2,1,0:T(8,128)(2,1)S(1)} collective-permute-done((bf16[3,16,2048]{2,1,0:T(8,128)(2,1)S(1)}, bf16[3,16,2048]{2,1,0:T(8,128)(2,1)S(1)}, u32[]{:S(2)}, u32[]{:S(2)}) %collective-permute-start) | collective-permute-done | bytes 196640 | tf_op jit(solution)/shard_map/ppermute | solution.py:214
  22.7 4.1 %collective-permute-done.1.below_ref = bf16[3,16,2048]{2,1,0:T(8,128)(2,1)S(1)} collective-permute-done((bf16[3,16,2048]{2,1,0:T(8,128)(2,1)S(1)}, bf16[3,16,2048]{2,1,0:T(8,128)(2,1)S(1)}, u32[]{:S(2)}, u32[]{:S(2)}) %collective-permute-start.1) | collective-permute-done | bytes 196640 | tf_op jit(solution)/shard_map/ppermute | solution.py:214
  26.9 0.7 copy-done.5
  27.5 1.9 %advance.1 = (f32[2,16,2048]{2,1,0:T(8,128)}, f32[32,16,128]{2,1,0:T(8,128)}) custom-call(s32[2]{0:T(128)S(1)} %pad_add_fusion.place_ref, f32[2,16,2048]{2,1,0:T(8,128)S(1)} %copy-done.1, f32[2,16,2048]{2,1,0:T(8,128)S(1)} %get-tuple-element.9.conduct_ref, f32[2,16,2048]{2,1,0:T(8,128)S(1)} %get-tuple-element.10.part_ref, ...), custom_call_target="tpu_custom_call" | custom-call | flops 60000000 | bytes 1800000 | tf_op jit(solution)/shard_map/advance/pallas_call | solution.py:152
  29.4 21.4 %all-to-all-start = ((f32[32,16,128]{2,1,0:T(8,128)}), f32[32,16,128]{2,1,0:T(8,128)S(1)}, u32[]{:S(2)}, u32[]{:S(2)}) async-start(f32[32,16,128]{2,1,0:T(8,128)} %get-tuple-element.14), calls=%async_computation | async-start | bytes 524288 | tf_op jit(solution)/shard_map/all_to_all | solution.py:229
  50.8 0.1 pad_maximum_fusion.even_ref
  50.9 5.1 %collective-permute-start.4 = (bf16[4,2,16,2048]{3,2,1,0:T(8,128)(2,1)S(1)}, bf16[4,2,16,2048]{3,2,1,0:T(8,128)(2,1)S(1)}, u32[]{:S(2)}, u32[]{:S(2)}) collective-permute-start(bf16[4,2,16,2048]{3,2,1,0:T(8,128)(2,1)S(1)} %pad_maximum_fusion.even_ref), channel_id=1, source_target_pairs={{0,64},{64,0},{1,65},{65,1},{2,66},{66,2},{3,67},{67,3},{4,68},{68... | collective-permute-start | bytes 1572872 | tf_op jit(solution)/shard_map/ppermute | solution.py:218
  56.0 4.6 %all-to-all-done = f32[32,16,128]{2,1,0:T(8,128)S(1)} async-done(((f32[32,16,128]{2,1,0:T(8,128)}), f32[32,16,128]{2,1,0:T(8,128)S(1)}, u32[]{:S(2)}, u32[]{:S(2)}) %all-to-all-start) | async-done | bytes 262176 | tf_op jit(solution)/shard_map/all_to_all | solution.py:229
  60.6 0.7 broadcast_in_dim.16
  61.3 8.5 %all-to-all-start.1 = ((f32[16,16,128]{2,1,0:T(8,128)}), f32[16,16,128]{2,1,0:T(8,128)S(1)}, u32[]{:S(2)}, u32[]{:S(2)}) async-start(f32[16,16,128]{2,1,0:T(8,128)} %broadcast_in_dim.16), calls=%async_computation.1 | async-start | bytes 262144 | tf_op jit(solution)/shard_map/all_to_all | solution.py:231
  69.8 8.9 %all-to-all-done.1.found_ref = f32[16,16,128]{2,1,0:T(8,128)S(1)} async-done(((f32[16,16,128]{2,1,0:T(8,128)}), f32[16,16,128]{2,1,0:T(8,128)S(1)}, u32[]{:S(2)}, u32[]{:S(2)}) %all-to-all-start.1) | async-done | bytes 131104 | tf_op jit(solution)/shard_map/all_to_all | solution.py:231
  78.7 0.6 copy-done.6
  79.4 0.0 copy-done.7
  79.4 7.1 %update.1 = f32[2,16,2048]{2,1,0:T(8,128)} custom-call(s32[2]{0:T(128)S(1)} %pad_add_fusion.place_ref, f32[16,16,128]{2,1,0:T(8,128)S(1)} %all-to-all-done.1.found_ref, f32[16,128]{1,0:T(8,128)S(1)} %copy-done.4, f32[1,128]{1,0:T(1,128)S(1)} %bitcast.10, f32[1,128]{1,0:T(1,128)S(1)} %bitcast.11, f32[2,16,2048]{2,1,0:T(8,128)S(1)} %copy-done.3, ...), custom_call_target="tpu_custom_call" | custom-call | flops 200000000 | bytes 1700000 | tf_op jit(solution)/shard_map/update/pallas_call | solution.py:191
  (14 shorter events, 0.1 us)
Async XLA Ops:
  0.6 1.0 %copy-start = (f32[2,16,2048]{2,1,0:T(8,128)S(1)}, f32[2,16,2048]{2,1,0:T(8,128)}, u32[]{:S(2)}) copy-start(f32[2,16,2048]{2,1,0:T(8,128)} %conc_ref.3) | copy-start | bytes 786436
  1.6 0.9 %copy-start.2 = (f32[2,16,2048]{2,1,0:T(8,128)S(1)}, f32[2,16,2048]{2,1,0:T(8,128)}, u32[]{:S(2)}) copy-start(f32[2,16,2048]{2,1,0:T(8,128)} %perm_ref.3) | copy-start | bytes 786436
  2.9 7.2 %collective-permute-start.2 = (bf16[2,16,2048]{2,1,0:T(8,128)(2,1)S(1)}, bf16[2,16,2048]{2,1,0:T(8,128)(2,1)S(1)}, u32[]{:S(2)}, u32[]{:S(2)}) collective-permute-start(bf16[2,16,2048]{2,1,0:T(8,128)(2,1)S(1)} %get-tuple-element.15), channel_id=1, source_target_pairs={{0,128},{128,0},{256,384},{384,256},{1,129},{129,1},{257,385},{385... | collective-permute-start | bytes 393224 | tf_op jit(solution)/shard_map/ppermute | solution.py:218
  10.1 16.8 %copy-start.1 = (f32[2,16,2048]{2,1,0:T(8,128)S(1)}, f32[2,16,2048]{2,1,0:T(8,128)}, u32[]{:S(2)}) copy-start(f32[2,16,2048]{2,1,0:T(8,128)} %conc_ref.3) | copy-start | bytes 786436
  10.1 40.7 %collective-permute-start.3 = (bf16[2,2,16,2048]{3,2,1,0:T(8,128)(2,1)S(1)}, bf16[2,2,16,2048]{3,2,1,0:T(8,128)(2,1)S(1)}, u32[]{:S(2)}, u32[]{:S(2)}) collective-permute-start(bf16[2,2,16,2048]{3,2,1,0:T(8,128)(2,1)S(1)} %pad_maximum_fusion.1), channel_id=1, source_target_pairs={{0,256},{128,384},{256,0},{384,128},{1,257},{129,385},{257,1},{385... | collective-permute-start | bytes 786440 | tf_op jit(solution)/shard_map/ppermute | solution.py:218
  16.9 5.8 %collective-permute-start = (bf16[3,16,2048]{2,1,0:T(8,128)(2,1)S(1)}, bf16[3,16,2048]{2,1,0:T(8,128)(2,1)S(1)}, u32[]{:S(2)}, u32[]{:S(2)}) collective-permute-start(bf16[3,16,2048]{2,1,0:T(8,128)(2,1)S(1)} %get-tuple-element.11), channel_id=1, source_target_pairs={{0,1},{1,2},{2,3},{3,4},{4,5},{5,6},{6,7},{7,8},{8,9},{9,10},{10,1... | collective-permute-start | bytes 589832 | tf_op jit(solution)/shard_map/ppermute | solution.py:214
  20.1 6.7 %collective-permute-start.1 = (bf16[3,16,2048]{2,1,0:T(8,128)(2,1)S(1)}, bf16[3,16,2048]{2,1,0:T(8,128)(2,1)S(1)}, u32[]{:S(2)}, u32[]{:S(2)}) collective-permute-start(bf16[3,16,2048]{2,1,0:T(8,128)(2,1)S(1)} %get-tuple-element.12), channel_id=1, source_target_pairs={{1,0},{2,1},{3,2},{4,3},{5,4},{6,5},{7,6},{8,7},{9,8},{10,9},{11,1... | collective-permute-start | bytes 589832 | tf_op jit(solution)/shard_map/ppermute | solution.py:214
  26.9 0.7 copy-start.5
  29.4 31.1 %all-to-all-start = ((f32[32,16,128]{2,1,0:T(8,128)}), f32[32,16,128]{2,1,0:T(8,128)S(1)}, u32[]{:S(2)}, u32[]{:S(2)}) async-start(f32[32,16,128]{2,1,0:T(8,128)} %get-tuple-element.14), calls=%async_computation | async-start | bytes 524288 | tf_op jit(solution)/shard_map/all_to_all | solution.py:229
  50.9 18.9 %collective-permute-start.4 = (bf16[4,2,16,2048]{3,2,1,0:T(8,128)(2,1)S(1)}, bf16[4,2,16,2048]{3,2,1,0:T(8,128)(2,1)S(1)}, u32[]{:S(2)}, u32[]{:S(2)}) collective-permute-start(bf16[4,2,16,2048]{3,2,1,0:T(8,128)(2,1)S(1)} %pad_maximum_fusion.even_ref), channel_id=1, source_target_pairs={{0,64},{64,0},{1,65},{65,1},{2,66},{66,2},{3,67},{67,3},{4,68},{68... | collective-permute-start | bytes 1572872 | tf_op jit(solution)/shard_map/ppermute | solution.py:218
  60.6 18.1 %copy-start.3 = (f32[2,16,2048]{2,1,0:T(8,128)S(1)}, f32[2,16,2048]{2,1,0:T(8,128)}, u32[]{:S(2)}) copy-start(f32[2,16,2048]{2,1,0:T(8,128)} %perm_ref.3) | copy-start | bytes 786436
  61.3 17.5 %copy-start.4 = (f32[16,128]{1,0:T(8,128)S(1)}, f32[16,128]{1,0:T(8,128)}, u32[]{:S(2)}) copy-start(f32[16,128]{1,0:T(8,128)} %noise_ref.1) | copy-start | bytes 24580
  61.3 17.5 %all-to-all-start.1 = ((f32[16,16,128]{2,1,0:T(8,128)}), f32[16,16,128]{2,1,0:T(8,128)S(1)}, u32[]{:S(2)}, u32[]{:S(2)}) async-start(f32[16,16,128]{2,1,0:T(8,128)} %broadcast_in_dim.16), calls=%async_computation.1 | async-start | bytes 262144 | tf_op jit(solution)/shard_map/all_to_all | solution.py:231
  78.7 0.7 copy-start.6
  78.7 0.7 copy-start.7

commit v2 on v1

--- a/solution.py
+++ b/solution.py
@@ -84,7 +84,26 @@
     return 0.5 * (conduct + jnp.where(lane == width - 1, 0.0, pltpu.roll(conduct, width - 1, 1)))
 
 
-def prepare_kernel(perm_ref, conc_ref, up_ref, down_ref, low_ref, part_ref, conduct_ref):
+def prepare_kernel(
+    perm_hbm, conc_hbm, wells_hbm, data_hbm, var_hbm, noise_hbm,
+    up_ref, down_ref, low_ref, part_ref, conduct_ref, wells_ref, data_ref, var_ref, noise_ref,
+    perm_ref, conc_ref, sem,
+):
+    main = [
+        pltpu.make_async_copy(source.at[row], target.at[row], sem.at[2 * i + row])
+        for i, (source, target) in enumerate(((perm_hbm, perm_ref), (conc_hbm, conc_ref)))
+        for row in range(2)
+    ]
+    small = [
+        pltpu.make_async_copy(source, target, sem.at[4 + i])
+        for i, (source, target) in enumerate(
+            ((wells_hbm, wells_ref), (data_hbm, data_ref), (var_hbm, var_ref), (noise_hbm, noise_ref))
+        )
+    ]
+    for copy in main + small:
+        copy.start()
+    for copy in main:
+        copy.wait()
     perm0, perm1 = perm_ref[0], perm_ref[1]
     conc0, conc1 = conc_ref[0], conc_ref[1]
     low_ref[0], low_ref[1] = perm0.astype(BF16), perm1.astype(BF16)
@@ -96,19 +115,47 @@
     part_ref[0], part_ref[1] = part0, part1
     down_ref[0], down_ref[1], down_ref[2] = conc0.astype(BF16), cond0.astype(BF16), part0.astype(BF16)
     up_ref[0], up_ref[1], up_ref[2] = conc1.astype(BF16), cond1.astype(BF16), part1.astype(BF16)
-
-
-def prepare(log_perm, conc):
+    for copy in small:
+        copy.wait()
+
+
+def prepare(log_perm, conc, wells, obs_data, obs_var, noise):
     rows, members, width = log_perm.shape
     edge = jax.ShapeDtypeStruct((3, members, width), BF16)
     full = jax.ShapeDtypeStruct(log_perm.shape, F32)
+    small = [jax.ShapeDtypeStruct(a.shape, a.dtype) for a in (wells, obs_data, obs_var, noise)]
     return pl.pallas_call(
         prepare_kernel,
-        out_shape=(edge, edge, jax.ShapeDtypeStruct(log_perm.shape, BF16), full, full),
+        out_shape=(edge, edge, jax.ShapeDtypeStruct(log_perm.shape, BF16), full, full, *small),
+        in_specs=[pl.BlockSpec(memory_space=pltpu.HBM)] * 6,
+        out_specs=[pl.BlockSpec(memory_space=pltpu.VMEM)] * 9,
+        scratch_shapes=[
+            pltpu.VMEM(log_perm.shape, F32),
+            pltpu.VMEM(log_perm.shape, F32),
+            pltpu.SemaphoreType.DMA((8,)),
+        ],
         cost_estimate=pl.CostEstimate(flops=2_000_000, bytes_accessed=1_600_000, transcendentals=65536),
         compiler_params=pltpu.CompilerParams(vmem_limit_bytes=VMEM_LIMIT),
         name="prepare",
-    )(log_perm, conc)
+    )(*[pltpu.with_memory_space_constraint(a, pltpu.HBM) for a in (log_perm, conc, wells, obs_data, obs_var, noise)])
+
+
+def spread_kernel(found_ref, out_ref):
+    total = found_ref[0]
+    for i in range(1, found_ref.shape[0]):
+        total = total + found_ref[i]
+    for copy in range(out_ref.shape[0]):
+        out_ref[copy] = total
+
+
+def spread(found, copies):
+    return pl.pallas_call(
+        spread_kernel,
+        out_shape=jax.ShapeDtypeStruct((copies, *found.shape[1:]), F32),
+        cost_estimate=pl.CostEstimate(flops=65536, bytes_accessed=400_000, transcendentals=0),
+        compiler_params=pltpu.CompilerParams(vmem_limit_bytes=VMEM_LIMIT),
+        name="spread",
+    )(found)
 
 
 def advance_kernel(place_ref, conc_ref, conduct_ref, part_ref, above_ref, below_ref, wells_ref, out_ref, picked_ref):
@@ -220,16 +267,18 @@
 
 def local(log_perm, concentration, well_cells, obs_data, obs_var, obs_noise):
     place = jnp.stack([lax.axis_index(SPACE), lax.axis_index(MEM)]).astype(jnp.int32)
-    up, down, low, part, conduct = prepare(log_perm, concentration)
+    up, down, low, part, conduct, wells, data, var, noise = prepare(
+        log_perm, concentration, well_cells[None], obs_data[None], obs_var[None], obs_noise
+    )
     above, below = shifted(up, 1), shifted(down, -1)
-    two = jnp.stack([low, swapped(low, "z_lo", 1)])
-    even = jnp.concatenate([two, swapped(two, "z_lo", 2)])
+    tracer, picked = advance(place, concentration, conduct, part, above, below, wells, 32)
+    low, picked = lax.optimization_barrier((low, picked))
+    found = lax.all_to_all(picked, ("x", "y"), 0, 0, tiled=True)
+    even = jnp.stack([low] + [swapped(low, "z_lo", flip) for flip in (1, 2, 3)])
+    even, found = lax.optimization_barrier((even, found))
+    found = lax.all_to_all(spread(found, 16), ("z_lo", "core", "z_hi"), 0, 0, tiled=True)
     odd = swapped(even, "core", 1)
-    tracer, picked = advance(place, concentration, conduct, part, above, below, well_cells[None], 32)
-    found = lax.all_to_all(picked, ("x", "y"), 0, 0, tiled=True)
-    found = jnp.broadcast_to(jnp.sum(found, axis=0)[None], (16, 16, 128))
-    found = lax.all_to_all(found, ("z_lo", "core", "z_hi"), 0, 0, tiled=True)
-    updated = update(place, found, obs_noise, obs_data[None], obs_var[None], log_perm, even, odd)
+    updated = update(place, found, noise, data, var, log_perm, even, odd)
     return (tracer, updated)
 
 

time: 86.9 us -> 80.8 us (0.930)
  blocking collectives: 0 us -> 12.9 us
  waiting for transfers between devices: 21.2 us -> 11.8 us
  starting transfers between devices: 51.1 us -> 44.2 us
  local copies, waits for them, and re-layouts: 3.89 us -> 0.01 us
  Pallas kernels: 9.32 us -> 10.6 us
    all_to_all x0 -> x1, blocking collectives: none -> 12.9 us  [local(): lax.all_to_all(spread(found, 16), ('z_lo', 'core', 'z_hi'), 0, 0, tiled=T...]
    all_to_all x1 -> x0, waiting for transfers between devices: 8.95 us -> none  [local(): found = lax.all_to_all(found, ('z_lo', 'core', 'z_hi'), 0, 0, tiled=True)]
    all_to_all x1 -> x0, starting transfers between devices: 8.5 us -> none  [local(): found = lax.all_to_all(found, ('z_lo', 'core', 'z_hi'), 0, 0, tiled=True)]
    all_to_all x1, waiting for transfers between devices: 4.58 us -> 0.01 us  [local(): found = lax.all_to_all(picked, ('x', 'y'), 0, 0, tiled=True)]
    ppermute x3 -> x4, waiting for transfers between devices: 2.35 us -> 6.75 us  [swapped(): lax.ppermute(value, axis, [(i, i ^ flip) for i in range(lax.axis_size(axi...]
    all_to_all x1, starting transfers between devices: 21.4 us -> 25.4 us  [local(): found = lax.all_to_all(picked, ('x', 'y'), 0, 0, tiled=True)]
    unnamed x16 -> x4, local copies, waits for them, and re-layouts: 3.22 us -> 0.01 us
    ppermute x3 -> x4, starting transfers between devices: 16.7 us -> 13.5 us  [swapped(): lax.ppermute(value, axis, [(i, i ^ flip) for i in range(lax.axis_size(axi...]
  transfers between devices with their start and end apart: 7 -> 7, of which waited for: 5 -> 3; matrix products, arithmetic and copies ran while one was open for 1% -> 0% of each run, Pallas kernels for 2% -> 0%
where the time goes in v2:
time: 80.8 us; the launch traced here: 80.4 us
  starting transfers between devices  44.2 us (55%)
  blocking collectives  12.9 us (16%)
  waiting for transfers between devices  11.8 us (15%)
  Pallas kernels  10.6 us (13%)
    all_to_all x1, starting transfers between devices, local(): found = lax.all_to_all(picked, ('x', 'y'), 0, 0, tiled=True)  25.4 us
    ppermute x4, starting transfers between devices, swapped(): lax.ppermute(value, axis, [(i, i ^ flip) for i in range(lax.axis_size(axi...  13.5 us
    all_to_all x1, blocking collectives, local(): lax.all_to_all(spread(found, 16), ('z_lo', 'core', 'z_hi'), 0, 0, tiled=T...  12.9 us
    pallas_call x1, Pallas kernels, update(): pl.pallas_call(update_kernel, out_shape=jax.ShapeDtypeStruct(log_perm.sha...  7.06 us
    ppermute x4, waiting for transfers between devices, swapped(): lax.ppermute(value, axis, [(i, i ^ flip) for i in range(lax.axis_size(axi...  6.75 us
    ppermute x2, starting transfers between devices, shifted(): return lax.ppermute(value, SPACE, pairs)  5.33 us
    ppermute x2, waiting for transfers between devices, shifted(): return lax.ppermute(value, SPACE, pairs)  5.03 us
    pallas_call x1, Pallas kernels, advance(): pl.pallas_call(advance_kernel, out_shape=(jax.ShapeDtypeStruct(conc.shape...  1.9 us
  transfers between devices with their start and end apart: 7, of which 3 were waited for; matrix products, arithmetic and copies ran while one was open for 0% of the time, Pallas kernels for 0%

profile of v2, /device:TPU:1, one launch (start us, length us, event | category | flops | bytes accessed | tf_op | source)
XLA Modules:
  0.0 80.4 jit_solution(13152220778825072638)
XLA Ops:
  0.6 0.0 copy-start
  0.6 1.6 %prepare.1 = (bf16[3,16,2048]{2,1,0:T(8,128)(2,1)S(1)}, bf16[3,16,2048]{2,1,0:T(8,128)(2,1)S(1)}, bf16[2,16,2048]{2,1,0:T(8,128)(2,1)S(1)}, f32[2,16,2048]{2,1,0...) custom-call(f32[2,16,2048]{2,1,0:T(8,128)} %perm_ref.1, ...), custom_call_target="tpu_custom_call" | custom-call | flops 2000000 | bytes 1600000 | tf_op jit(solution)/shard_map/prepare/pallas_call | solution.py:127
  2.2 4.0 %collective-permute-start = (bf16[3,16,2048]{2,1,0:T(8,128)(2,1)S(1)}, bf16[3,16,2048]{2,1,0:T(8,128)(2,1)S(1)}, u32[]{:S(2)}, u32[]{:S(2)}) collective-permute-start(bf16[3,16,2048]{2,1,0:T(8,128)(2,1)S(1)} %get-tuple-element.19), channel_id=1, source_target_pairs={{0,1},{1,2},{2,3},{3,4},{4,5},{5,6},{6,7},{7,8},{8,9},{9,10},{10,1... | collective-permute-start | bytes 589832 | tf_op jit(solution)/shard_map/ppermute | solution.py:261
  6.3 1.3 %collective-permute-start.1 = (bf16[3,16,2048]{2,1,0:T(8,128)(2,1)S(1)}, bf16[3,16,2048]{2,1,0:T(8,128)(2,1)S(1)}, u32[]{:S(2)}, u32[]{:S(2)}) collective-permute-start(bf16[3,16,2048]{2,1,0:T(8,128)(2,1)S(1)} %get-tuple-element.20), channel_id=1, source_target_pairs={{1,0},{2,1},{3,2},{4,3},{5,4},{6,5},{7,6},{8,7},{9,8},{10,9},{11,1... | collective-permute-start | bytes 589832 | tf_op jit(solution)/shard_map/ppermute | solution.py:261
  7.6 0.1 pad_add_fusion.place_ref
  7.7 1.2 %collective-permute-done.above_ref = bf16[3,16,2048]{2,1,0:T(8,128)(2,1)S(1)} collective-permute-done((bf16[3,16,2048]{2,1,0:T(8,128)(2,1)S(1)}, bf16[3,16,2048]{2,1,0:T(8,128)(2,1)S(1)}, u32[]{:S(2)}, u32[]{:S(2)}) %collective-permute-start) | collective-permute-done | bytes 196640 | tf_op jit(solution)/shard_map/ppermute | solution.py:261
  8.9 3.8 %collective-permute-done.1.below_ref = bf16[3,16,2048]{2,1,0:T(8,128)(2,1)S(1)} collective-permute-done((bf16[3,16,2048]{2,1,0:T(8,128)(2,1)S(1)}, bf16[3,16,2048]{2,1,0:T(8,128)(2,1)S(1)}, u32[]{:S(2)}, u32[]{:S(2)}) %collective-permute-start.1) | collective-permute-done | bytes 196640 | tf_op jit(solution)/shard_map/ppermute | solution.py:261
  12.7 0.0 copy-done
  12.7 1.9 %advance.1 = (f32[2,16,2048]{2,1,0:T(8,128)}, f32[32,16,128]{2,1,0:T(8,128)}) custom-call(s32[2]{0:T(128)S(1)} %pad_add_fusion.place_ref, f32[2,16,2048]{2,1,0:T(8,128)S(1)} %copy-done, f32[2,16,2048]{2,1,0:T(8,128)S(1)} %get-tuple-element.17.conduct_ref, f32[2,16,2048]{2,1,0:T(8,128)S(1)} %get-tuple-element.18.part_ref, ...), custom_call_target="tpu_custom_call" | custom-call | flops 60000000 | bytes 1800000 | tf_op jit(solution)/shard_map/advance/pallas_call | solution.py:199
  14.6 25.4 %all-to-all-start = ((f32[32,16,128]{2,1,0:T(8,128)}), f32[32,16,128]{2,1,0:T(8,128)S(1)}, u32[]{:S(2)}, u32[]{:S(2)}) async-start(f32[32,16,128]{2,1,0:T(8,128)} %get-tuple-element.26), calls=%async_computation | async-start | bytes 524288 | tf_op jit(solution)/shard_map/all_to_all | solution.py:276
  40.0 4.3 %collective-permute-start.4 = (bf16[2,16,2048]{2,1,0:T(8,128)(2,1)S(1)}, bf16[2,16,2048]{2,1,0:T(8,128)(2,1)S(1)}, u32[]{:S(2)}, u32[]{:S(2)}) collective-permute-start(bf16[2,16,2048]{2,1,0:T(8,128)(2,1)S(1)} %get-tuple-element.25), channel_id=1, source_target_pairs={{0,384},{128,256},{256,128},{384,0},{1,385},{129,257},{257,129},{3... | collective-permute-start | bytes 393224 | tf_op jit(solution)/shard_map/ppermute | solution.py:265
  44.3 1.9 %collective-permute-start.3 = (bf16[2,16,2048]{2,1,0:T(8,128)(2,1)S(1)}, bf16[2,16,2048]{2,1,0:T(8,128)(2,1)S(1)}, u32[]{:S(2)}, u32[]{:S(2)}) collective-permute-start(bf16[2,16,2048]{2,1,0:T(8,128)(2,1)S(1)} %get-tuple-element.25), channel_id=1, source_target_pairs={{0,256},{128,384},{256,0},{384,128},{1,257},{129,385},{257,1},{385... | collective-permute-start | bytes 393224 | tf_op jit(solution)/shard_map/ppermute | solution.py:265
  46.2 3.0 %collective-permute-start.2 = (bf16[2,16,2048]{2,1,0:T(8,128)(2,1)S(1)}, bf16[2,16,2048]{2,1,0:T(8,128)(2,1)S(1)}, u32[]{:S(2)}, u32[]{:S(2)}) collective-permute-start(bf16[2,16,2048]{2,1,0:T(8,128)(2,1)S(1)} %get-tuple-element.25), channel_id=1, source_target_pairs={{0,128},{128,0},{256,384},{384,256},{1,129},{129,1},{257,385},{385... | collective-permute-start | bytes 393224 | tf_op jit(solution)/shard_map/ppermute | solution.py:265
  49.3 0.0 collective-permute-done.4
  49.3 6.7 %collective-permute-done.3 = bf16[2,16,2048]{2,1,0:T(8,128)(2,1)S(1)} collective-permute-done((bf16[2,16,2048]{2,1,0:T(8,128)(2,1)S(1)}, bf16[2,16,2048]{2,1,0:T(8,128)(2,1)S(1)}, u32[]{:S(2)}, u32[]{:S(2)}) %collective-permute-start.3) | collective-permute-done | bytes 131104 | tf_op jit(solution)/shard_map/ppermute | solution.py:265
  56.0 0.0 collective-permute-done.2
  56.0 0.1 pad_maximum_fusion.even_ref
  56.1 0.0 copy-start.1
  56.1 0.0 all-to-all-done.found_ref
  56.1 4.3 %collective-permute-start.5 = (bf16[4,2,16,2048]{3,2,1,0:T(8,128)(2,1)S(1)}, bf16[4,2,16,2048]{3,2,1,0:T(8,128)(2,1)S(1)}, u32[]{:S(2)}, u32[]{:S(2)}) collective-permute-start(bf16[4,2,16,2048]{3,2,1,0:T(8,128)(2,1)S(1)} %pad_maximum_fusion.even_ref), channel_id=1, source_target_pairs={{0,64},{64,0},{1,65},{65,1},{2,66},{66,2},{3,67},{67,3},{4,68},{68... | collective-permute-start | bytes 1572872 | tf_op jit(solution)/shard_map/ppermute | solution.py:265
  60.4 12.9 %all_to_all.10.found_ref = f32[16,16,128]{2,1,0:T(8,128)S(1)} all-to-all(f32[16,16,128]{2,1,0:T(8,128)S(1)} %spread.1), channel_id=1, replica_groups=mesh['z_lo'=4,'core'=2,'z_hi'=2,'x'=4,'y'=8] {'z_lo','core','z_hi'}, dimensions={0} | all-to-all | bytes 262144 | tf_op jit(solution)/shard_map/all_to_all | solution.py:279
  73.3 0.0 collective-permute-done.5.odd_ref
  73.3 0.0 copy-done.1
  73.3 7.1 %update.1 = f32[2,16,2048]{2,1,0:T(8,128)} custom-call(s32[2]{0:T(128)S(1)} %pad_add_fusion.place_ref, f32[16,16,128]{2,1,0:T(8,128)S(1)} %all_to_all.10.found_ref, f32[16,128]{1,0:T(8,128)S(1)} %get-tuple-element.28.noise_ref, f32[1,128]{1,0:T(1,128)S(1)} %get-tuple-element.29.data_ref, f32[1,128]{1,0:T(1,128)S(1)} %get-tuple-element.30.var_ref, ...), custom_call_target="tpu_custom_call" | custom-call | flops 200000000 | bytes 1700000 | tf_op jit(solution)/shard_map/update/pallas_call | solution.py:238
  (1 shorter events, 0.0 us)
Async XLA Ops:
  0.6 12.1 %copy-start = (f32[2,16,2048]{2,1,0:T(8,128)S(1)}, f32[2,16,2048]{2,1,0:T(8,128)}, u32[]{:S(2)}) copy-start(f32[2,16,2048]{2,1,0:T(8,128)} %conc_ref.1) | copy-start | bytes 786436
  2.2 6.6 %collective-permute-start = (bf16[3,16,2048]{2,1,0:T(8,128)(2,1)S(1)}, bf16[3,16,2048]{2,1,0:T(8,128)(2,1)S(1)}, u32[]{:S(2)}, u32[]{:S(2)}) collective-permute-start(bf16[3,16,2048]{2,1,0:T(8,128)(2,1)S(1)} %get-tuple-element.19), channel_id=1, source_target_pairs={{0,1},{1,2},{2,3},{3,4},{4,5},{5,6},{6,7},{7,8},{8,9},{9,10},{10,1... | collective-permute-start | bytes 589832 | tf_op jit(solution)/shard_map/ppermute | solution.py:261
  6.3 6.4 %collective-permute-start.1 = (bf16[3,16,2048]{2,1,0:T(8,128)(2,1)S(1)}, bf16[3,16,2048]{2,1,0:T(8,128)(2,1)S(1)}, u32[]{:S(2)}, u32[]{:S(2)}) collective-permute-start(bf16[3,16,2048]{2,1,0:T(8,128)(2,1)S(1)} %get-tuple-element.20), channel_id=1, source_target_pairs={{1,0},{2,1},{3,2},{4,3},{5,4},{6,5},{7,6},{8,7},{9,8},{10,9},{11,1... | collective-permute-start | bytes 589832 | tf_op jit(solution)/shard_map/ppermute | solution.py:261
  14.6 41.5 %all-to-all-start = ((f32[32,16,128]{2,1,0:T(8,128)}), f32[32,16,128]{2,1,0:T(8,128)S(1)}, u32[]{:S(2)}, u32[]{:S(2)}) async-start(f32[32,16,128]{2,1,0:T(8,128)} %get-tuple-element.26), calls=%async_computation | async-start | bytes 524288 | tf_op jit(solution)/shard_map/all_to_all | solution.py:276
  40.0 9.3 %collective-permute-start.4 = (bf16[2,16,2048]{2,1,0:T(8,128)(2,1)S(1)}, bf16[2,16,2048]{2,1,0:T(8,128)(2,1)S(1)}, u32[]{:S(2)}, u32[]{:S(2)}) collective-permute-start(bf16[2,16,2048]{2,1,0:T(8,128)(2,1)S(1)} %get-tuple-element.25), channel_id=1, source_target_pairs={{0,384},{128,256},{256,128},{384,0},{1,385},{129,257},{257,129},{3... | collective-permute-start | bytes 393224 | tf_op jit(solution)/shard_map/ppermute | solution.py:265
  44.3 11.7 %collective-permute-start.3 = (bf16[2,16,2048]{2,1,0:T(8,128)(2,1)S(1)}, bf16[2,16,2048]{2,1,0:T(8,128)(2,1)S(1)}, u32[]{:S(2)}, u32[]{:S(2)}) collective-permute-start(bf16[2,16,2048]{2,1,0:T(8,128)(2,1)S(1)} %get-tuple-element.25), channel_id=1, source_target_pairs={{0,256},{128,384},{256,0},{384,128},{1,257},{129,385},{257,1},{385... | collective-permute-start | bytes 393224 | tf_op jit(solution)/shard_map/ppermute | solution.py:265
  46.2 9.8 %collective-permute-start.2 = (bf16[2,16,2048]{2,1,0:T(8,128)(2,1)S(1)}, bf16[2,16,2048]{2,1,0:T(8,128)(2,1)S(1)}, u32[]{:S(2)}, u32[]{:S(2)}) collective-permute-start(bf16[2,16,2048]{2,1,0:T(8,128)(2,1)S(1)} %get-tuple-element.25), channel_id=1, source_target_pairs={{0,128},{128,0},{256,384},{384,256},{1,129},{129,1},{257,385},{385... | collective-permute-start | bytes 393224 | tf_op jit(solution)/shard_map/ppermute | solution.py:265
  56.1 17.3 %copy-start.1 = (f32[2,16,2048]{2,1,0:T(8,128)S(1)}, f32[2,16,2048]{2,1,0:T(8,128)}, u32[]{:S(2)}) copy-start(f32[2,16,2048]{2,1,0:T(8,128)} %perm_ref.1) | copy-start | bytes 786436
  56.1 17.2 %collective-permute-start.5 = (bf16[4,2,16,2048]{3,2,1,0:T(8,128)(2,1)S(1)}, bf16[4,2,16,2048]{3,2,1,0:T(8,128)(2,1)S(1)}, u32[]{:S(2)}, u32[]{:S(2)}) collective-permute-start(bf16[4,2,16,2048]{3,2,1,0:T(8,128)(2,1)S(1)} %pad_maximum_fusion.even_ref), channel_id=1, source_target_pairs={{0,64},{64,0},{1,65},{65,1},{2,66},{66,2},{3,67},{67,3},{4,68},{68... | collective-permute-start | bytes 1572872 | tf_op jit(solution)/shard_map/ppermute | solution.py:265

commit v3 on v2

--- a/solution.py
+++ b/solution.py
@@ -1,3 +1,5 @@
+import functools
+
 import jax
 import jax.numpy as jnp
 from jax import lax
@@ -13,7 +15,7 @@
 PANEL = 16
 MEM = ("z_lo", "core")
 SPACE = ("z_hi", "x", "y")
-ORDER = (0, 2, 4, 6, 1, 3, 5, 7)
+SENT = ((1, 0), (1, 1), (1, 2), (0, 0), (0, 1), (2, 0), (2, 1))
 VMEM_LIMIT = 48 * 1024 * 1024
 
 def split3(x):
@@ -42,10 +44,10 @@
     return jnp.concatenate(tiles, axis=1)
 
 
-def weights_of(pred, own_noise, obs_data, obs_var, work, solved):
+def weights_of(pred, own, own_noise, obs_data, obs_var, work, solved):
     members = pred.shape[0]
     anomaly = pred - jnp.mean(pred, axis=0, keepdims=True)
-    innovation = obs_data + jnp.sqrt(inflation * obs_var) * own_noise - pred[:16]
+    innovation = obs_data + jnp.sqrt(inflation * obs_var) * own_noise - own
     cov = lax.dot_general(anomaly, anomaly, TN, precision=HIGH, preferred_element_type=F32) / (members - 1)
     r = lax.broadcasted_iota(jnp.int32, (128, 128), 0)
     c = lax.broadcasted_iota(jnp.int32, (128, 128), 1)
@@ -85,8 +87,8 @@
 
 
 def prepare_kernel(
-    perm_hbm, conc_hbm, wells_hbm, data_hbm, var_hbm, noise_hbm,
-    up_ref, down_ref, low_ref, part_ref, conduct_ref, wells_ref, data_ref, var_ref, noise_ref,
+    place_ref, perm_hbm, conc_hbm, wells_hbm, data_hbm, var_hbm, noise_hbm,
+    near_ref, far_ref, near_edge_ref, far_edge_ref, low_ref, part_ref, conduct_ref, here_ref, wells_ref, data_ref, var_ref, noise_ref,
     perm_ref, conc_ref, sem,
 ):
     main = [
@@ -113,22 +115,109 @@
     part0 = conc0 + time_step * (along_row(conc0, link_right(cond0), 0.5 * cond0) + between)
     part1 = conc1 + time_step * (along_row(conc1, link_right(cond1), 0.5 * cond1) - between)
     part_ref[0], part_ref[1] = part0, part1
-    down_ref[0], down_ref[1], down_ref[2] = conc0.astype(BF16), cond0.astype(BF16), part0.astype(BF16)
-    up_ref[0], up_ref[1], up_ref[2] = conc1.astype(BF16), cond1.astype(BF16), part1.astype(BF16)
+    even = lax.rem(place_ref[0], 2) == 0
+    edges = ((conc0, conc1), (cond0, cond1), (part0, part1))
+    for i, (low_edge, high_edge) in enumerate(edges):
+        near_edge_ref[i] = jnp.where(even, high_edge, low_edge).astype(BF16)
+        far_edge_ref[i] = jnp.where(even, low_edge, high_edge).astype(BF16)
     for copy in small:
         copy.wait()
-
-
-def prepare(log_perm, conc, wells, obs_data, obs_var, noise):
+    members, width = conc0.shape
+    pieces = []
+    for pair in edges:
+        for row in pair:
+            high = row.astype(BF16)
+            pieces += [high, (row - high.astype(F32)).astype(BF16)]
+    pieces = jnp.concatenate(pieces, axis=0)
+    column = lax.rem(wells_ref[...], width)
+    chunk = 256
+    total = [jnp.zeros((pieces.shape[0], 128), F32) for _ in range(3)]
+    for start in range(0, width, chunk):
+        position = lax.broadcasted_iota(jnp.int32, (chunk, 128), 0) + (start - column)
+        for side in range(3):
+            chosen = jnp.where(position == side - 1, 1.0, 0.0).astype(BF16)
+            total[side] = total[side] + jnp.dot(
+                pieces[:, start : start + chunk], chosen, preferred_element_type=F32
+            )
+    values = [
+        [t[2 * members * q : 2 * members * q + members] + t[2 * members * q + members : 2 * members * (q + 1)] for q in range(6)]
+        for t in total
+    ]
+    for side in range(3):
+        for quantity in range(6):
+            here_ref[6 * side + quantity] = values[side][quantity]
+    for slot, (side, quantity) in enumerate(SENT):
+        low_value, high_value = values[side][2 * quantity], values[side][2 * quantity + 1]
+        near_ref[slot] = jnp.where(even, high_value, low_value).astype(BF16)
+        far_ref[slot] = jnp.where(even, low_value, high_value).astype(BF16)
+
+
+def combine_kernel(width, place_ref, near_ref, far_ref, here_ref, wells_ref, out_ref):
+    strip = place_ref[0]
+    even = lax.rem(strip, 2) == 0
+    row = jnp.broadcast_to(wells_ref[...], here_ref.shape[1:]) // width
+    upper = lax.rem(row, 2) == 0
+    near = [near_ref[i].astype(F32) for i in range(len(SENT))]
+    far = [far_ref[i].astype(F32) for i in range(len(SENT))]
+    above = [jnp.where(even, f, n) for n, f in zip(near, far)]
+    below = [jnp.where(even, n, f) for n, f in zip(near, far)]
+    beside = [jnp.where(upper, a, b) for a, b in zip(above, below)]
+    beyond = [jnp.where(upper, b, a) for a, b in zip(above, below)]
+    conc_n, cond_n, part_n, conc_nl, cond_nl, conc_nr, cond_nr = beside
+    conc_f, cond_f = beyond[0], beyond[1]
+
+    def own(side, quantity):
+        return jnp.where(upper, here_ref[6 * side + 2 * quantity], here_ref[6 * side + 2 * quantity + 1])
+
+    def other(side, quantity):
+        return jnp.where(upper, here_ref[6 * side + 2 * quantity + 1], here_ref[6 * side + 2 * quantity])
+
+    half = 0.5 * time_step
+    conc, cond, part = own(1, 0), own(1, 1), own(1, 2)
+    conc_l, cond_l, part_l = own(0, 0), own(0, 1), own(0, 2)
+    conc_r, cond_r, part_r = own(2, 0), own(2, 1), own(2, 2)
+    conc_o, cond_o, part_o = other(1, 0), other(1, 1), other(1, 2)
+    gain = half * (cond + cond_n) * (conc_n - conc)
+    outside = (row == 0) | (row == 2 * STRIPS - 1)
+    once = part + gain
+    once_n = jnp.where(outside, 0.0, part_n - gain)
+    once_l = part_l + half * (cond_l + cond_nl) * (conc_nl - conc_l)
+    once_r = part_r + half * (cond_r + cond_nr) * (conc_nr - conc_r)
+    once_o = part_o + half * (cond_o + cond_f) * (conc_f - conc_o)
+    twice = once + half * (
+        (cond + cond_n) * (once_n - once)
+        + (cond + cond_o) * (once_o - once)
+        + (cond + cond_l) * (once_l - once)
+        + (cond + cond_r) * (once_r - once)
+    )
+    picked = jnp.where(row // 2 == strip, twice, 0.0)
+    for copy in range(out_ref.shape[0]):
+        out_ref[copy] = picked
+
+
+def combine(place, near, far, here, wells, width, copies):
+    return pl.pallas_call(
+        functools.partial(combine_kernel, width),
+        out_shape=jax.ShapeDtypeStruct((copies, *here.shape[1:]), F32),
+        in_specs=[pl.BlockSpec(memory_space=pltpu.SMEM)] + [pl.BlockSpec(memory_space=pltpu.VMEM)] * 4,
+        cost_estimate=pl.CostEstimate(flops=100_000, bytes_accessed=500_000, transcendentals=0),
+        compiler_params=pltpu.CompilerParams(vmem_limit_bytes=VMEM_LIMIT),
+        name="combine",
+    )(place, near, far, here, wells)
+
+
+def prepare(place, log_perm, conc, wells, obs_data, obs_var, noise):
     rows, members, width = log_perm.shape
     edge = jax.ShapeDtypeStruct((3, members, width), BF16)
     full = jax.ShapeDtypeStruct(log_perm.shape, F32)
+    sent = jax.ShapeDtypeStruct((len(SENT), members, 128), BF16)
+    here = jax.ShapeDtypeStruct((18, members, 128), F32)
     small = [jax.ShapeDtypeStruct(a.shape, a.dtype) for a in (wells, obs_data, obs_var, noise)]
     return pl.pallas_call(
         prepare_kernel,
-        out_shape=(edge, edge, jax.ShapeDtypeStruct(log_perm.shape, BF16), full, full, *small),
-        in_specs=[pl.BlockSpec(memory_space=pltpu.HBM)] * 6,
-        out_specs=[pl.BlockSpec(memory_space=pltpu.VMEM)] * 9,
+        out_shape=(sent, sent, edge, edge, jax.ShapeDtypeStruct(log_perm.shape, BF16), full, full, here, *small),
+        in_specs=[pl.BlockSpec(memory_space=pltpu.SMEM)] + [pl.BlockSpec(memory_space=pltpu.HBM)] * 6,
+        out_specs=[pl.BlockSpec(memory_space=pltpu.VMEM)] * 12,
         scratch_shapes=[
             pltpu.VMEM(log_perm.shape, F32),
             pltpu.VMEM(log_perm.shape, F32),
@@ -137,7 +226,7 @@
         cost_estimate=pl.CostEstimate(flops=2_000_000, bytes_accessed=1_600_000, transcendentals=65536),
         compiler_params=pltpu.CompilerParams(vmem_limit_bytes=VMEM_LIMIT),
         name="prepare",
-    )(*[pltpu.with_memory_space_constraint(a, pltpu.HBM) for a in (log_perm, conc, wells, obs_data, obs_var, noise)])
+    )(place, *[pltpu.with_memory_space_constraint(a, pltpu.HBM) for a in (log_perm, conc, wells, obs_data, obs_var, noise)])
 
 
 def spread_kernel(found_ref, out_ref):
@@ -158,12 +247,15 @@
     )(found)
 
 
-def advance_kernel(place_ref, conc_ref, conduct_ref, part_ref, above_ref, below_ref, wells_ref, out_ref, picked_ref):
+def advance_kernel(place_ref, conc_ref, conduct_ref, part_ref, near_ref, far_ref, out_ref):
     strip = place_ref[0]
     conc0, conc1 = conc_ref[0], conc_ref[1]
     cond0, cond1 = conduct_ref[0], conduct_ref[1]
-    conc_a, cond_a, part_a = [above_ref[i].astype(F32) for i in range(3)]
-    conc_b, cond_b, part_b = [below_ref[i].astype(F32) for i in range(3)]
+    even = lax.rem(strip, 2) == 0
+    near = [near_ref[i].astype(F32) for i in range(3)]
+    far = [far_ref[i].astype(F32) for i in range(3)]
+    conc_a, cond_a, part_a = [jnp.where(even, f, n) for n, f in zip(near, far)]
+    conc_b, cond_b, part_b = [jnp.where(even, n, f) for n, f in zip(near, far)]
     link_a = 0.5 * (cond0 + cond_a)
     link_b = 0.5 * (cond1 + cond_b)
     gain_a = time_step * (link_a * (conc_a - conc0))
@@ -179,35 +271,19 @@
         along_row(once1, link_right(cond1), 0.5 * cond1) - between + link_b * (once_b - once1)
     )
     out_ref[0], out_ref[1] = twice0, twice1
-    members, width = twice0.shape
-    chunk = 256
-    total = jnp.zeros((3 * members, 128), F32)
-    for row, values in enumerate((twice0, twice1)):
-        pieces = jnp.concatenate(split3(values), axis=0)
-        column = wells_ref[...] - (2 * strip + row) * width
-        for start in range(0, width, chunk):
-            here = lax.broadcasted_iota(jnp.int32, (chunk, 128), 0) + start
-            chosen = jnp.where(here == column, 1.0, 0.0).astype(BF16)
-            total = total + jnp.dot(pieces[:, start : start + chunk], chosen, preferred_element_type=F32)
-    picked = total[:members] + total[members : 2 * members] + total[2 * members :]
-    for copy in range(picked_ref.shape[0]):
-        picked_ref[copy] = picked
-
-
-def advance(place, conc, conduct, part, above, below, wells, copies):
+
+
+def advance(place, conc, conduct, part, near, far):
     vmem = pl.BlockSpec(memory_space=pltpu.VMEM)
     return pl.pallas_call(
         advance_kernel,
-        out_shape=(
-            jax.ShapeDtypeStruct(conc.shape, F32),
-            jax.ShapeDtypeStruct((copies, conc.shape[1], 128), F32),
-        ),
-        in_specs=[pl.BlockSpec(memory_space=pltpu.SMEM)] + [vmem] * 6,
-        out_specs=(vmem, vmem),
-        cost_estimate=pl.CostEstimate(flops=60_000_000, bytes_accessed=1_800_000, transcendentals=0),
+        out_shape=jax.ShapeDtypeStruct(conc.shape, F32),
+        in_specs=[pl.BlockSpec(memory_space=pltpu.SMEM)] + [vmem] * 5,
+        out_specs=vmem,
+        cost_estimate=pl.CostEstimate(flops=4_000_000, bytes_accessed=1_800_000, transcendentals=0),
         compiler_params=pltpu.CompilerParams(vmem_limit_bytes=VMEM_LIMIT),
         name="advance",
-    )(place, conc, conduct, part, above, below, wells)
+    )(place, conc, conduct, part, near, far)
 
 
 def update_kernel(place_ref, found_ref, noise_ref, data_ref, var_ref, perm_ref, even_ref, odd_ref, out_ref, pred, work, solved, low, sem):
@@ -221,10 +297,11 @@
             )
     for copy in copies:
         copy.start()
-    for position, flip in enumerate(ORDER):
-        block = lax.bitwise_xor(group, flip)
+    for position in range(8):
+        block = lax.bitwise_xor(group, 2 * position if position < 4 else 2 * position - 7)
         pred[pl.ds(position * 16, 16), :] = found_ref[2 * block] + found_ref[2 * block + 1]
-    centred = weights_of(pred[...], noise_ref[...], data_ref[...], var_ref[...], work, solved).astype(BF16)
+    own = found_ref[2 * group] + found_ref[2 * group + 1]
+    centred = weights_of(pred[...], own, noise_ref[...], data_ref[...], var_ref[...], work, solved).astype(BF16)
     for copy in copies:
         copy.wait()
     for row in range(2):
@@ -256,29 +333,34 @@
 STRIPS = 64
 
 
-def shifted(value, shift):
-    pairs = [(i, i + shift) for i in range(STRIPS) if 0 <= i + shift < STRIPS]
-    return lax.ppermute(value, SPACE, pairs)
-
-
-def swapped(value, axis, flip):
-    return lax.ppermute(value, axis, [(i, i ^ flip) for i in range(lax.axis_size(axis))])
+def swapped(value, axis, first, count):
+    pairs = [(i, i + 1) for i in range(first, count - 1, 2)]
+    return lax.ppermute(value, axis, pairs + [(high, low) for low, high in pairs])
+
+
+def crossed(value, flip):
+    return lax.ppermute(value, "z_lo", [(i, i ^ flip) for i in range(4)])
 
 
 def local(log_perm, concentration, well_cells, obs_data, obs_var, obs_noise):
     place = jnp.stack([lax.axis_index(SPACE), lax.axis_index(MEM)]).astype(jnp.int32)
-    up, down, low, part, conduct, wells, data, var, noise = prepare(
-        log_perm, concentration, well_cells[None], obs_data[None], obs_var[None], obs_noise
-    )
-    above, below = shifted(up, 1), shifted(down, -1)
-    tracer, picked = advance(place, concentration, conduct, part, above, below, wells, 32)
-    low, picked = lax.optimization_barrier((low, picked))
+    near, far, near_edge, far_edge, low, part, conduct, here, wells, data, var, noise = prepare(
+        place, log_perm, concentration, well_cells[None], obs_data[None], obs_var[None], obs_noise
+    )
+    far = swapped(far, SPACE, 1, STRIPS)
+    near = swapped(near, SPACE, 0, STRIPS)
+    picked = combine(place, near, far, here, wells, log_perm.shape[2], 32)
+    near_edge, far_edge, picked = lax.optimization_barrier((near_edge, far_edge, picked))
     found = lax.all_to_all(picked, ("x", "y"), 0, 0, tiled=True)
-    even = jnp.stack([low] + [swapped(low, "z_lo", flip) for flip in (1, 2, 3)])
+    far_edge = swapped(far_edge, SPACE, 1, STRIPS)
+    near_edge = swapped(near_edge, SPACE, 0, STRIPS)
+    even = jnp.stack([low] + [crossed(low, flip) for flip in (1, 2, 3)])
     even, found = lax.optimization_barrier((even, found))
     found = lax.all_to_all(spread(found, 16), ("z_lo", "core", "z_hi"), 0, 0, tiled=True)
-    odd = swapped(even, "core", 1)
+    odd = swapped(even, "core", 0, 2)
     updated = update(place, found, noise, data, var, log_perm, even, odd)
+    near_edge, far_edge, updated = lax.optimization_barrier((near_edge, far_edge, updated))
+    tracer = advance(place, concentration, conduct, part, near_edge, far_edge)
     return (tracer, updated)
 
 

time: 80.8 us -> 81.5 us (level)
  the two profiles are of different devices: /device:TPU:1 before, /device:TPU:62 now
where the time goes in v3:
time: 81.5 us; the launch traced here: 81 us
  starting transfers between devices  50.9 us (62%)
  waiting for transfers between devices  15.5 us (19%)
  Pallas kernels  13.6 us (17%)
    ppermute x5, starting transfers between devices, swapped(): lax.ppermute(value, axis, pairs + [(high, low) for low, high in pairs])  26.5 us
    ppermute x3, starting transfers between devices, crossed(): return lax.ppermute(value, 'z_lo', [(i, i ^ flip) for i in range(4)])  12.3 us
    ppermute x5, waiting for transfers between devices, swapped(): lax.ppermute(value, axis, pairs + [(high, low) for low, high in pairs])  10 us
    pallas_call x1, Pallas kernels, update(): pl.pallas_call(update_kernel, out_shape=jax.ShapeDtypeStruct(log_perm.sha...  7.06 us
    all_to_all x1, starting transfers between devices, local(): found = lax.all_to_all(picked, ('x', 'y'), 0, 0, tiled=True)  6.87 us
    ppermute x3, waiting for transfers between devices, crossed(): return lax.ppermute(value, 'z_lo', [(i, i ^ flip) for i in range(4)])  5.5 us
    all_to_all x1, starting transfers between devices, local(): lax.all_to_all(spread(found, 16), ('z_lo', 'core', 'z_hi'), 0, 0, tiled=T...  5.32 us
    pallas_call x1, Pallas kernels, prepare(): pl.pallas_call(prepare_kernel, out_shape=(sent, sent, edge, edge, jax.Sha...  2.88 us
  transfers between devices with their start and end apart: 10, of which 4 were waited for; matrix products, arithmetic and copies ran while one was open for 0% of the time, Pallas kernels for 10%

profile of v3, /device:TPU:62, one launch (start us, length us, event | category | flops | bytes accessed | tf_op | source)
XLA Modules:
  0.0 81.0 jit_solution(4194855810528130969)
XLA Ops:
  0.6 0.1 pad_add_fusion.place_ref
  0.7 2.9 %prepare.1 = (bf16[7,16,128]{2,1,0:T(8,128)(2,1)S(1)}, bf16[7,16,128]{2,1,0:T(8,128)(2,1)S(1)}, bf16[3,16,2048]{2,1,0:T(8,128)(2,1)S(1)}, bf16[3,16,2048]{2,1,0:...) custom-call(s32[2]{0:T(128)S(1)} %pad_add_fusion.place_ref, ...), custom_call_target="tpu_custom_call" | custom-call | flops 2000000 | bytes 1600000 | tf_op jit(solution)/shard_map/prepare/pallas_call | solution.py:216
  3.6 3.3 %collective-permute-start = (bf16[7,16,128]{2,1,0:T(8,128)(2,1)S(1)}, bf16[7,16,128]{2,1,0:T(8,128)(2,1)S(1)}, u32[]{:S(2)}, u32[]{:S(2)}) collective-permute-start(bf16[7,16,128]{2,1,0:T(8,128)(2,1)S(1)} %get-tuple-element.26), channel_id=1, source_target_pairs={{0,1},{2,3},{4,5},{6,7},{8,9},{10,11},{12,13},{14,15},{16,17},{18,... | collective-permute-start | bytes 86024 | tf_op jit(solution)/shard_map/ppermute | solution.py:338
  6.9 10.3 %collective-permute-start.1 = (bf16[7,16,128]{2,1,0:T(8,128)(2,1)S(1)}, bf16[7,16,128]{2,1,0:T(8,128)(2,1)S(1)}, u32[]{:S(2)}, u32[]{:S(2)}) collective-permute-start(bf16[7,16,128]{2,1,0:T(8,128)(2,1)S(1)} %get-tuple-element.27), channel_id=1, source_target_pairs={{1,2},{3,4},{5,6},{7,8},{9,10},{11,12},{13,14},{15,16},{17,18},{19... | collective-permute-start | bytes 86024 | tf_op jit(solution)/shard_map/ppermute | solution.py:338
  17.1 0.0 collective-permute-done.near_ref
  17.1 3.6 %collective-permute-done.1.far_ref = bf16[7,16,128]{2,1,0:T(8,128)(2,1)S(1)} collective-permute-done((bf16[7,16,128]{2,1,0:T(8,128)(2,1)S(1)}, bf16[7,16,128]{2,1,0:T(8,128)(2,1)S(1)}, u32[]{:S(2)}, u32[]{:S(2)}) %collective-permute-start.1) | collective-permute-done | bytes 28704 | tf_op jit(solution)/shard_map/ppermute | solution.py:338
  20.8 1.3 %combine.1 = f32[32,16,128]{2,1,0:T(8,128)} custom-call(s32[2]{0:T(128)S(1)} %pad_add_fusion.place_ref, bf16[7,16,128]{2,1,0:T(8,128)(2,1)S(1)} %collective-permute-done.near_ref, bf16[7,16,128]{2,1,0:T(8,128)(2,1)S(1)} %collective-permute-done.1.far_ref, f32[18,16,128]{2,1,0:T(8,128)S(1)} %get-tuple-element.28.here_ref, ...), custom_call_target="tpu_custom_call" | custom-call | flops 100000 | bytes 500000 | tf_op jit(solution)/shard_map/combine/pallas_call | solution.py:199
  22.1 6.9 %all-to-all-start = ((f32[32,16,128]{2,1,0:T(8,128)}), f32[32,16,128]{2,1,0:T(8,128)S(1)}, u32[]{:S(2)}, u32[]{:S(2)}) async-start(f32[32,16,128]{2,1,0:T(8,128)} %combine.1), calls=%async_computation | async-start | bytes 524288 | tf_op jit(solution)/shard_map/all_to_all | solution.py:354
  28.9 7.9 %collective-permute-start.6 = (bf16[2,16,2048]{2,1,0:T(8,128)(2,1)S(1)}, bf16[2,16,2048]{2,1,0:T(8,128)(2,1)S(1)}, u32[]{:S(2)}, u32[]{:S(2)}) collective-permute-start(bf16[2,16,2048]{2,1,0:T(8,128)(2,1)S(1)} %get-tuple-element.32), channel_id=1, source_target_pairs={{0,384},{128,256},{256,128},{384,0},{1,385},{129,257},{257,129},{3... | collective-permute-start | bytes 393224 | tf_op jit(solution)/shard_map/ppermute | solution.py:342
  36.8 1.9 %collective-permute-start.5 = (bf16[2,16,2048]{2,1,0:T(8,128)(2,1)S(1)}, bf16[2,16,2048]{2,1,0:T(8,128)(2,1)S(1)}, u32[]{:S(2)}, u32[]{:S(2)}) collective-permute-start(bf16[2,16,2048]{2,1,0:T(8,128)(2,1)S(1)} %get-tuple-element.32), channel_id=1, source_target_pairs={{0,256},{128,384},{256,0},{384,128},{1,257},{129,385},{257,1},{385... | collective-permute-start | bytes 393224 | tf_op jit(solution)/shard_map/ppermute | solution.py:342
  38.8 2.5 %collective-permute-start.4 = (bf16[2,16,2048]{2,1,0:T(8,128)(2,1)S(1)}, bf16[2,16,2048]{2,1,0:T(8,128)(2,1)S(1)}, u32[]{:S(2)}, u32[]{:S(2)}) collective-permute-start(bf16[2,16,2048]{2,1,0:T(8,128)(2,1)S(1)} %get-tuple-element.32), channel_id=1, source_target_pairs={{0,128},{128,0},{256,384},{384,256},{1,129},{129,1},{257,385},{385... | collective-permute-start | bytes 393224 | tf_op jit(solution)/shard_map/ppermute | solution.py:342
  41.3 4.2 %collective-permute-done.5 = bf16[2,16,2048]{2,1,0:T(8,128)(2,1)S(1)} collective-permute-done((bf16[2,16,2048]{2,1,0:T(8,128)(2,1)S(1)}, bf16[2,16,2048]{2,1,0:T(8,128)(2,1)S(1)}, u32[]{:S(2)}, u32[]{:S(2)}) %collective-permute-start.5) | collective-permute-done | bytes 131104 | tf_op jit(solution)/shard_map/ppermute | solution.py:342
  45.4 1.3 %collective-permute-done.4 = bf16[2,16,2048]{2,1,0:T(8,128)(2,1)S(1)} collective-permute-done((bf16[2,16,2048]{2,1,0:T(8,128)(2,1)S(1)}, bf16[2,16,2048]{2,1,0:T(8,128)(2,1)S(1)}, u32[]{:S(2)}, u32[]{:S(2)}) %collective-permute-start.4) | collective-permute-done | bytes 131104 | tf_op jit(solution)/shard_map/ppermute | solution.py:342
  46.8 0.1 pad_maximum_fusion.even_ref
  46.8 0.0 copy-start
  46.8 2.1 %collective-permute-start.7 = (bf16[4,2,16,2048]{3,2,1,0:T(8,128)(2,1)S(1)}, bf16[4,2,16,2048]{3,2,1,0:T(8,128)(2,1)S(1)}, u32[]{:S(2)}, u32[]{:S(2)}) collective-permute-start(bf16[4,2,16,2048]{3,2,1,0:T(8,128)(2,1)S(1)} %pad_maximum_fusion.even_ref), channel_id=1, source_target_pairs={{0,64},{64,0},{1,65},{65,1},{2,66},{66,2},{3,67},{67,3},{4,68},{68... | collective-permute-start | bytes 1572872 | tf_op jit(solution)/shard_map/ppermute | solution.py:338
  48.9 0.7 spread.1
  49.6 5.3 %all-to-all-start.1 = ((f32[16,16,128]{2,1,0:T(8,128)}), f32[16,16,128]{2,1,0:T(8,128)S(1)}, u32[]{:S(2)}, u32[]{:S(2)}) async-start(f32[16,16,128]{2,1,0:T(8,128)} %spread.1), calls=%async_computation.1 | async-start | bytes 262144 | tf_op jit(solution)/shard_map/all_to_all | solution.py:359
  54.9 3.4 %collective-permute-start.2 = (bf16[3,16,2048]{2,1,0:T(8,128)(2,1)S(1)}, bf16[3,16,2048]{2,1,0:T(8,128)(2,1)S(1)}, u32[]{:S(2)}, u32[]{:S(2)}) collective-permute-start(bf16[3,16,2048]{2,1,0:T(8,128)(2,1)S(1)} %get-tuple-element.30), channel_id=1, source_target_pairs={{0,1},{2,3},{4,5},{6,7},{8,9},{10,11},{12,13},{14,15},{16,17},{18,... | collective-permute-start | bytes 589832 | tf_op jit(solution)/shard_map/ppermute | solution.py:338
  58.3 7.5 %collective-permute-start.3 = (bf16[3,16,2048]{2,1,0:T(8,128)(2,1)S(1)}, bf16[3,16,2048]{2,1,0:T(8,128)(2,1)S(1)}, u32[]{:S(2)}, u32[]{:S(2)}) collective-permute-start(bf16[3,16,2048]{2,1,0:T(8,128)(2,1)S(1)} %get-tuple-element.31), channel_id=1, source_target_pairs={{1,2},{3,4},{5,6},{7,8},{9,10},{11,12},{13,14},{15,16},{17,18},{19... | collective-permute-start | bytes 589832 | tf_op jit(solution)/shard_map/ppermute | solution.py:338
  65.9 0.0 copy-start.1
  65.9 7.1 %update.1 = f32[2,16,2048]{2,1,0:T(8,128)} custom-call(s32[2]{0:T(128)S(1)} %pad_add_fusion.place_ref, f32[16,16,128]{2,1,0:T(8,128)S(1)} %all-to-all-done.1.found_ref, f32[16,128]{1,0:T(8,128)S(1)} %get-tuple-element.35.noise_ref, f32[1,128]{1,0:T(1,128)S(1)} %get-tuple-element.36.data_ref, f32[1,128]{1,0:T(1,128)S(1)} %get-tuple-element.37.var_ref, ...), custom_call_target="tpu_custom_call" | custom-call | flops 200000000 | bytes 1700000 | tf_op jit(solution)/shard_map/update/pallas_call | solution.py:315
  73.0 6.4 %collective-permute-done.3.far_ref = bf16[3,16,2048]{2,1,0:T(8,128)(2,1)S(1)} collective-permute-done((bf16[3,16,2048]{2,1,0:T(8,128)(2,1)S(1)}, bf16[3,16,2048]{2,1,0:T(8,128)(2,1)S(1)}, u32[]{:S(2)}, u32[]{:S(2)}) %collective-permute-start.3) | collective-permute-done | bytes 196640 | tf_op jit(solution)/shard_map/ppermute | solution.py:338
  79.4 1.7 %advance.1 = f32[2,16,2048]{2,1,0:T(8,128)} custom-call(s32[2]{0:T(128)S(1)} %pad_add_fusion.place_ref, f32[2,16,2048]{2,1,0:T(8,128)S(1)} %copy-done.1, f32[2,16,2048]{2,1,0:T(8,128)S(1)} %get-tuple-element.22.conduct_ref, f32[2,16,2048]{2,1,0:T(8,128)S(1)} %get-tuple-element.23.part_ref, bf16[3,16,2048]{2,1,0:T(8,128)(2,1)S(1)} %collective-permute-done.2.near_ref, ...), custom_call_target="tpu_custom_call" | custom-call | flops 4000000 | bytes 1800000 | tf_op jit(solution)/shard_map/advance/pallas_call | solution.py:278
  (7 shorter events, 0.0 us)
Async XLA Ops:
  3.6 13.5 %collective-permute-start = (bf16[7,16,128]{2,1,0:T(8,128)(2,1)S(1)}, bf16[7,16,128]{2,1,0:T(8,128)(2,1)S(1)}, u32[]{:S(2)}, u32[]{:S(2)}) collective-permute-start(bf16[7,16,128]{2,1,0:T(8,128)(2,1)S(1)} %get-tuple-element.26), channel_id=1, source_target_pairs={{0,1},{2,3},{4,5},{6,7},{8,9},{10,11},{12,13},{14,15},{16,17},{18,... | collective-permute-start | bytes 86024 | tf_op jit(solution)/shard_map/ppermute | solution.py:338
  6.9 13.9 %collective-permute-start.1 = (bf16[7,16,128]{2,1,0:T(8,128)(2,1)S(1)}, bf16[7,16,128]{2,1,0:T(8,128)(2,1)S(1)}, u32[]{:S(2)}, u32[]{:S(2)}) collective-permute-start(bf16[7,16,128]{2,1,0:T(8,128)(2,1)S(1)} %get-tuple-element.27), channel_id=1, source_target_pairs={{1,2},{3,4},{5,6},{7,8},{9,10},{11,12},{13,14},{15,16},{17,18},{19... | collective-permute-start | bytes 86024 | tf_op jit(solution)/shard_map/ppermute | solution.py:338
  22.1 24.8 %all-to-all-start = ((f32[32,16,128]{2,1,0:T(8,128)}), f32[32,16,128]{2,1,0:T(8,128)S(1)}, u32[]{:S(2)}, u32[]{:S(2)}) async-start(f32[32,16,128]{2,1,0:T(8,128)} %combine.1), calls=%async_computation | async-start | bytes 524288 | tf_op jit(solution)/shard_map/all_to_all | solution.py:354
  28.9 12.3 %collective-permute-start.6 = (bf16[2,16,2048]{2,1,0:T(8,128)(2,1)S(1)}, bf16[2,16,2048]{2,1,0:T(8,128)(2,1)S(1)}, u32[]{:S(2)}, u32[]{:S(2)}) collective-permute-start(bf16[2,16,2048]{2,1,0:T(8,128)(2,1)S(1)} %get-tuple-element.32), channel_id=1, source_target_pairs={{0,384},{128,256},{256,128},{384,0},{1,385},{129,257},{257,129},{3... | collective-permute-start | bytes 393224 | tf_op jit(solution)/shard_map/ppermute | solution.py:342
  36.8 8.6 %collective-permute-start.5 = (bf16[2,16,2048]{2,1,0:T(8,128)(2,1)S(1)}, bf16[2,16,2048]{2,1,0:T(8,128)(2,1)S(1)}, u32[]{:S(2)}, u32[]{:S(2)}) collective-permute-start(bf16[2,16,2048]{2,1,0:T(8,128)(2,1)S(1)} %get-tuple-element.32), channel_id=1, source_target_pairs={{0,256},{128,384},{256,0},{384,128},{1,257},{129,385},{257,1},{385... | collective-permute-start | bytes 393224 | tf_op jit(solution)/shard_map/ppermute | solution.py:342
  38.8 8.0 %collective-permute-start.4 = (bf16[2,16,2048]{2,1,0:T(8,128)(2,1)S(1)}, bf16[2,16,2048]{2,1,0:T(8,128)(2,1)S(1)}, u32[]{:S(2)}, u32[]{:S(2)}) collective-permute-start(bf16[2,16,2048]{2,1,0:T(8,128)(2,1)S(1)} %get-tuple-element.32), channel_id=1, source_target_pairs={{0,128},{128,0},{256,384},{384,256},{1,129},{129,1},{257,385},{385... | collective-permute-start | bytes 393224 | tf_op jit(solution)/shard_map/ppermute | solution.py:342
  46.8 19.0 %copy-start = (f32[2,16,2048]{2,1,0:T(8,128)S(1)}, f32[2,16,2048]{2,1,0:T(8,128)}, u32[]{:S(2)}) copy-start(f32[2,16,2048]{2,1,0:T(8,128)} %perm_ref.1) | copy-start | bytes 786436
  46.8 19.0 %collective-permute-start.7 = (bf16[4,2,16,2048]{3,2,1,0:T(8,128)(2,1)S(1)}, bf16[4,2,16,2048]{3,2,1,0:T(8,128)(2,1)S(1)}, u32[]{:S(2)}, u32[]{:S(2)}) collective-permute-start(bf16[4,2,16,2048]{3,2,1,0:T(8,128)(2,1)S(1)} %pad_maximum_fusion.even_ref), channel_id=1, source_target_pairs={{0,64},{64,0},{1,65},{65,1},{2,66},{66,2},{3,67},{67,3},{4,68},{68... | collective-permute-start | bytes 1572872 | tf_op jit(solution)/shard_map/ppermute | solution.py:338
  49.6 16.2 %all-to-all-start.1 = ((f32[16,16,128]{2,1,0:T(8,128)}), f32[16,16,128]{2,1,0:T(8,128)S(1)}, u32[]{:S(2)}, u32[]{:S(2)}) async-start(f32[16,16,128]{2,1,0:T(8,128)} %spread.1), calls=%async_computation.1 | async-start | bytes 262144 | tf_op jit(solution)/shard_map/all_to_all | solution.py:359
  54.9 18.0 %collective-permute-start.2 = (bf16[3,16,2048]{2,1,0:T(8,128)(2,1)S(1)}, bf16[3,16,2048]{2,1,0:T(8,128)(2,1)S(1)}, u32[]{:S(2)}, u32[]{:S(2)}) collective-permute-start(bf16[3,16,2048]{2,1,0:T(8,128)(2,1)S(1)} %get-tuple-element.30), channel_id=1, source_target_pairs={{0,1},{2,3},{4,5},{6,7},{8,9},{10,11},{12,13},{14,15},{16,17},{18,... | collective-permute-start | bytes 589832 | tf_op jit(solution)/shard_map/ppermute | solution.py:338
  58.3 21.1 %collective-permute-start.3 = (bf16[3,16,2048]{2,1,0:T(8,128)(2,1)S(1)}, bf16[3,16,2048]{2,1,0:T(8,128)(2,1)S(1)}, u32[]{:S(2)}, u32[]{:S(2)}) collective-permute-start(bf16[3,16,2048]{2,1,0:T(8,128)(2,1)S(1)} %get-tuple-element.31), channel_id=1, source_target_pairs={{1,2},{3,4},{5,6},{7,8},{9,10},{11,12},{13,14},{15,16},{17,18},{19... | collective-permute-start | bytes 589832 | tf_op jit(solution)/shard_map/ppermute | solution.py:338
  65.9 13.5 %copy-start.1 = (f32[2,16,2048]{2,1,0:T(8,128)S(1)}, f32[2,16,2048]{2,1,0:T(8,128)}, u32[]{:S(2)}) copy-start(f32[2,16,2048]{2,1,0:T(8,128)} %conc_ref.1) | copy-start | bytes 786436

commit v4 on v2

--- a/solution.py
+++ b/solution.py
@@ -42,10 +42,10 @@
     return jnp.concatenate(tiles, axis=1)
 
 
-def weights_of(pred, own_noise, obs_data, obs_var, work, solved):
+def weights_of(pred, own, own_noise, obs_data, obs_var, work, solved):
     members = pred.shape[0]
     anomaly = pred - jnp.mean(pred, axis=0, keepdims=True)
-    innovation = obs_data + jnp.sqrt(inflation * obs_var) * own_noise - pred[:16]
+    innovation = obs_data + jnp.sqrt(inflation * obs_var) * own_noise - own
     cov = lax.dot_general(anomaly, anomaly, TN, precision=HIGH, preferred_element_type=F32) / (members - 1)
     r = lax.broadcasted_iota(jnp.int32, (128, 128), 0)
     c = lax.broadcasted_iota(jnp.int32, (128, 128), 1)
@@ -85,8 +85,8 @@
 
 
 def prepare_kernel(
-    perm_hbm, conc_hbm, wells_hbm, data_hbm, var_hbm, noise_hbm,
-    up_ref, down_ref, low_ref, part_ref, conduct_ref, wells_ref, data_ref, var_ref, noise_ref,
+    place_ref, perm_hbm, conc_hbm, wells_hbm, data_hbm, var_hbm, noise_hbm,
+    near_ref, far_ref, low_ref, part_ref, conduct_ref, wells_ref, data_ref, var_ref, noise_ref,
     perm_ref, conc_ref, sem,
 ):
     main = [
@@ -113,13 +113,15 @@
     part0 = conc0 + time_step * (along_row(conc0, link_right(cond0), 0.5 * cond0) + between)
     part1 = conc1 + time_step * (along_row(conc1, link_right(cond1), 0.5 * cond1) - between)
     part_ref[0], part_ref[1] = part0, part1
-    down_ref[0], down_ref[1], down_ref[2] = conc0.astype(BF16), cond0.astype(BF16), part0.astype(BF16)
-    up_ref[0], up_ref[1], up_ref[2] = conc1.astype(BF16), cond1.astype(BF16), part1.astype(BF16)
+    even = lax.rem(place_ref[0], 2) == 0
+    for i, (low_edge, high_edge) in enumerate(((conc0, conc1), (cond0, cond1), (part0, part1))):
+        near_ref[i] = jnp.where(even, high_edge, low_edge).astype(BF16)
+        far_ref[i] = jnp.where(even, low_edge, high_edge).astype(BF16)
     for copy in small:
         copy.wait()
 
 
-def prepare(log_perm, conc, wells, obs_data, obs_var, noise):
+def prepare(place, log_perm, conc, wells, obs_data, obs_var, noise):
     rows, members, width = log_perm.shape
     edge = jax.ShapeDtypeStruct((3, members, width), BF16)
     full = jax.ShapeDtypeStruct(log_perm.shape, F32)
@@ -127,7 +129,7 @@
     return pl.pallas_call(
         prepare_kernel,
         out_shape=(edge, edge, jax.ShapeDtypeStruct(log_perm.shape, BF16), full, full, *small),
-        in_specs=[pl.BlockSpec(memory_space=pltpu.HBM)] * 6,
+        in_specs=[pl.BlockSpec(memory_space=pltpu.SMEM)] + [pl.BlockSpec(memory_space=pltpu.HBM)] * 6,
         out_specs=[pl.BlockSpec(memory_space=pltpu.VMEM)] * 9,
         scratch_shapes=[
             pltpu.VMEM(log_perm.shape, F32),
@@ -137,7 +139,7 @@
         cost_estimate=pl.CostEstimate(flops=2_000_000, bytes_accessed=1_600_000, transcendentals=65536),
         compiler_params=pltpu.CompilerParams(vmem_limit_bytes=VMEM_LIMIT),
         name="prepare",
-    )(*[pltpu.with_memory_space_constraint(a, pltpu.HBM) for a in (log_perm, conc, wells, obs_data, obs_var, noise)])
+    )(place, *[pltpu.with_memory_space_constraint(a, pltpu.HBM) for a in (log_perm, conc, wells, obs_data, obs_var, noise)])
 
 
 def spread_kernel(found_ref, out_ref):
@@ -158,12 +160,15 @@
     )(found)
 
 
-def advance_kernel(place_ref, conc_ref, conduct_ref, part_ref, above_ref, below_ref, wells_ref, out_ref, picked_ref):
+def advance_kernel(place_ref, conc_ref, conduct_ref, part_ref, far_ref, near_ref, wells_ref, out_ref, picked_ref):
     strip = place_ref[0]
     conc0, conc1 = conc_ref[0], conc_ref[1]
     cond0, cond1 = conduct_ref[0], conduct_ref[1]
-    conc_a, cond_a, part_a = [above_ref[i].astype(F32) for i in range(3)]
-    conc_b, cond_b, part_b = [below_ref[i].astype(F32) for i in range(3)]
+    even = lax.rem(strip, 2) == 0
+    near = [near_ref[i].astype(F32) for i in range(3)]
+    far = [far_ref[i].astype(F32) for i in range(3)]
+    conc_a, cond_a, part_a = [jnp.where(even, f, n) for n, f in zip(near, far)]
+    conc_b, cond_b, part_b = [jnp.where(even, n, f) for n, f in zip(near, far)]
     link_a = 0.5 * (cond0 + cond_a)
     link_b = 0.5 * (cond1 + cond_b)
     gain_a = time_step * (link_a * (conc_a - conc0))
@@ -194,7 +199,7 @@
         picked_ref[copy] = picked
 
 
-def advance(place, conc, conduct, part, above, below, wells, copies):
+def advance(place, conc, conduct, part, far, near, wells, copies):
     vmem = pl.BlockSpec(memory_space=pltpu.VMEM)
     return pl.pallas_call(
         advance_kernel,
@@ -207,78 +212,80 @@
         cost_estimate=pl.CostEstimate(flops=60_000_000, bytes_accessed=1_800_000, transcendentals=0),
         compiler_params=pltpu.CompilerParams(vmem_limit_bytes=VMEM_LIMIT),
         name="advance",
-    )(place, conc, conduct, part, above, below, wells)
-
-
-def update_kernel(place_ref, found_ref, noise_ref, data_ref, var_ref, perm_ref, even_ref, odd_ref, out_ref, pred, work, solved, low, sem):
+    )(place, conc, conduct, part, far, near, wells)
+
+
+def solve_kernel(place_ref, found_ref, noise_ref, data_ref, var_ref, out_ref, pred, work, solved):
     group = place_ref[1]
-    copies = []
-    for position in range(8):
-        source = (even_ref if position < 4 else odd_ref).at[position % 4]
-        for row in range(2):
-            copies.append(
-                pltpu.make_async_copy(source.at[row], low.at[row, pl.ds(position * 16, 16)], sem.at[position, row])
-            )
-    for copy in copies:
-        copy.start()
     for position, flip in enumerate(ORDER):
         block = lax.bitwise_xor(group, flip)
         pred[pl.ds(position * 16, 16), :] = found_ref[2 * block] + found_ref[2 * block + 1]
-    centred = weights_of(pred[...], noise_ref[...], data_ref[...], var_ref[...], work, solved).astype(BF16)
-    for copy in copies:
-        copy.wait()
-    for row in range(2):
-        out_ref[row] = perm_ref[row] + jnp.dot(centred, low[row], preferred_element_type=F32)
-
-
-def update(place, found, noise, obs_data, obs_var, log_perm, even, odd):
+    centred = weights_of(pred[...], pred[0:16], noise_ref[...], data_ref[...], var_ref[...], work, solved)
+    out_ref[...] = centred.astype(BF16)
+
+
+def solve(place, found, noise, obs_data, obs_var):
     vmem = pl.BlockSpec(memory_space=pltpu.VMEM)
-    anywhere = pl.BlockSpec(memory_space=pl.ANY)
-    rows, members, width = log_perm.shape
-    return pl.pallas_call(
-        update_kernel,
-        out_shape=jax.ShapeDtypeStruct(log_perm.shape, F32),
-        in_specs=[pl.BlockSpec(memory_space=pltpu.SMEM)] + [vmem] * 5 + [anywhere] * 2,
+    return pl.pallas_call(
+        solve_kernel,
+        out_shape=jax.ShapeDtypeStruct((16, 128), BF16),
+        in_specs=[pl.BlockSpec(memory_space=pltpu.SMEM)] + [vmem] * 4,
         out_specs=vmem,
         scratch_shapes=[
             pltpu.VMEM((128, 128), F32),
             pltpu.VMEM((128, 384), F32),
             pltpu.VMEM((128, 256), F32),
-            pltpu.VMEM((rows, 128, width), BF16),
-            pltpu.SemaphoreType.DMA((8, 2)),
         ],
-        cost_estimate=pl.CostEstimate(flops=200_000_000, bytes_accessed=1_700_000, transcendentals=128),
-        compiler_params=pltpu.CompilerParams(vmem_limit_bytes=VMEM_LIMIT),
-        name="update",
-    )(place, found, noise, obs_data, obs_var, log_perm, even, odd)
+        cost_estimate=pl.CostEstimate(flops=50_000_000, bytes_accessed=18_000_000, transcendentals=128),
+        compiler_params=pltpu.CompilerParams(vmem_limit_bytes=VMEM_LIMIT),
+        name="solve",
+    )(place, found, noise, obs_data, obs_var)
+
+
+def increment_kernel(weights_ref, perm_ref, *refs):
+    *pieces, odd_ref, out_ref = refs
+    for row in range(2):
+        members = [piece[row] for piece in pieces] + [odd_ref[i, row] for i in range(odd_ref.shape[0])]
+        stacked = jnp.concatenate(members, axis=0)
+        out_ref[row] = perm_ref[row] + jnp.dot(weights_ref[...], stacked, preferred_element_type=F32)
+
+
+def increment(weights, log_perm, pieces, odd):
+    return pl.pallas_call(
+        increment_kernel,
+        out_shape=jax.ShapeDtypeStruct(log_perm.shape, F32),
+        cost_estimate=pl.CostEstimate(flops=20_000_000, bytes_accessed=1_700_000, transcendentals=0),
+        compiler_params=pltpu.CompilerParams(vmem_limit_bytes=VMEM_LIMIT),
+        name="increment",
+    )(weights, log_perm, *pieces, odd)
 
 
 STRIPS = 64
 
 
-def shifted(value, shift):
-    pairs = [(i, i + shift) for i in range(STRIPS) if 0 <= i + shift < STRIPS]
-    return lax.ppermute(value, SPACE, pairs)
-
-
-def swapped(value, axis, flip):
-    return lax.ppermute(value, axis, [(i, i ^ flip) for i in range(lax.axis_size(axis))])
+def swapped(value, axis, first, count):
+    pairs = [(i, i + 1) for i in range(first, count - 1, 2)]
+    return lax.ppermute(value, axis, pairs + [(high, low) for low, high in pairs])
+
+
+def crossed(value, flip):
+    return lax.ppermute(value, "z_lo", [(i, i ^ flip) for i in range(4)])
 
 
 def local(log_perm, concentration, well_cells, obs_data, obs_var, obs_noise):
     place = jnp.stack([lax.axis_index(SPACE), lax.axis_index(MEM)]).astype(jnp.int32)
-    up, down, low, part, conduct, wells, data, var, noise = prepare(
-        log_perm, concentration, well_cells[None], obs_data[None], obs_var[None], obs_noise
+    near, far, low, part, conduct, wells, data, var, noise = prepare(
+        place, log_perm, concentration, well_cells[None], obs_data[None], obs_var[None], obs_noise
     )
-    above, below = shifted(up, 1), shifted(down, -1)
-    tracer, picked = advance(place, concentration, conduct, part, above, below, wells, 32)
-    low, picked = lax.optimization_barrier((low, picked))
+    far = swapped(far, SPACE, 1, STRIPS)
+    near = swapped(near, SPACE, 0, STRIPS)
+    tracer, picked = advance(place, concentration, conduct, part, far, near, wells, 32)
     found = lax.all_to_all(picked, ("x", "y"), 0, 0, tiled=True)
-    even = jnp.stack([low] + [swapped(low, "z_lo", flip) for flip in (1, 2, 3)])
-    even, found = lax.optimization_barrier((even, found))
+    even = [low] + [crossed(low, flip) for flip in (1, 2, 3)]
     found = lax.all_to_all(spread(found, 16), ("z_lo", "core", "z_hi"), 0, 0, tiled=True)
-    odd = swapped(even, "core", 1)
-    updated = update(place, found, noise, data, var, log_perm, even, odd)
+    odd = swapped(jnp.stack(even), "core", 0, 2)
+    weights = solve(place, found, noise, data, var)
+    updated = increment(weights, log_perm, even, odd)
     return (tracer, updated)
 
 

time: 80.8 us -> 68.1 us (0.84)
  starting transfers between devices: 44.2 us -> 34.3 us
  waiting for transfers between devices: 11.8 us -> 5.29 us
  blocking collectives: 12.9 us -> 17.7 us
  Pallas kernels: 10.6 us -> 9.57 us
    all_to_all x1, starting transfers between devices: 25.4 us -> 11 us  [local(): found = lax.all_to_all(picked, ('x', 'y'), 0, 0, tiled=True)]
    ppermute x6, waiting for transfers between devices: 11.8 us -> 0.02 us  [the longest x3 0.01 us: swapped(): lax.ppermute(value, axis, pairs + [(high, low) for low, high in pairs])]
    all_to_all x1, waiting for transfers between devices: 0.01 us -> 5.28 us  [local(): found = lax.all_to_all(picked, ('x', 'y'), 0, 0, tiled=True)]
    all_to_all x1, blocking collectives: 12.9 us -> 17.7 us  [local(): lax.all_to_all(spread(found, 16), ('z_lo', 'core', 'z_hi'), 0, 0, tiled=T...]
    ppermute x6, starting transfers between devices: 18.9 us -> 23.2 us  [the longest x3 11.7 us: crossed(): return lax.ppermute(value, 'z_lo', [(i, i ^ flip) for i in range(4)])]
    pallas_call x1 -> x2, Pallas kernels: 7.06 us -> 5.46 us  [the longest x1 4.5 us: solve(): pl.pallas_call(solve_kernel, out_shape=jax.ShapeDtypeStruct((16, 128), BF...]
  transfers between devices with their start and end apart: 7 -> 7, of which waited for: 3 -> 1; matrix products, arithmetic and copies ran while one was open for 0% -> 0% of each run, Pallas kernels for 0% -> 10%
where the time goes in v4:
time: 68.1 us; the launch traced here: 67.7 us
  starting transfers between devices  34.3 us (50%)
  blocking collectives  17.7 us (26%)
  Pallas kernels  9.57 us (14%)
  waiting for transfers between devices  5.29 us (8%)
  between operations  0.78 us (1%)
    all_to_all x1, blocking collectives, local(): lax.all_to_all(spread(found, 16), ('z_lo', 'core', 'z_hi'), 0, 0, tiled=T...  17.7 us
    ppermute x3, starting transfers between devices, crossed(): return lax.ppermute(value, 'z_lo', [(i, i ^ flip) for i in range(4)])  11.7 us
    ppermute x3, starting transfers between devices, swapped(): lax.ppermute(value, axis, pairs + [(high, low) for low, high in pairs])  11.5 us
    all_to_all x1, starting transfers between devices, local(): found = lax.all_to_all(picked, ('x', 'y'), 0, 0, tiled=True)  11 us
    all_to_all x1, waiting for transfers between devices, local(): found = lax.all_to_all(picked, ('x', 'y'), 0, 0, tiled=True)  5.28 us
    pallas_call x1, Pallas kernels, solve(): pl.pallas_call(solve_kernel, out_shape=jax.ShapeDtypeStruct((16, 128), BF...  4.5 us
    pallas_call x1, Pallas kernels, prepare(): pl.pallas_call(prepare_kernel, out_shape=(edge, edge, jax.ShapeDtypeStruc...  2.09 us
    pallas_call x1, Pallas kernels, advance(): pl.pallas_call(advance_kernel, out_shape=(jax.ShapeDtypeStruct(conc.shape...  1.98 us
  transfers between devices with their start and end apart: 7, of which 1 were waited for; matrix products, arithmetic and copies ran while one was open for 0% of the time, Pallas kernels for 10%

profile of v4, /device:TPU:1, one launch (start us, length us, event | category | flops | bytes accessed | tf_op | source)
XLA Modules:
  0.0 67.7 jit_solution(10935864590965328640)
XLA Ops:
  0.6 0.1 pad_add_fusion.place_ref
  0.7 2.1 %prepare.1 = (bf16[3,16,2048]{2,1,0:T(8,128)(2,1)S(1)}, bf16[3,16,2048]{2,1,0:T(8,128)(2,1)S(1)}, bf16[2,16,2048]{2,1,0:T(8,128)(2,1)S(1)}, f32[2,16,2048]{2,1,0...) custom-call(s32[2]{0:T(128)S(1)} %pad_add_fusion.place_ref, ...), custom_call_target="tpu_custom_call" | custom-call | flops 2000000 | bytes 1600000 | tf_op jit(solution)/shard_map/prepare/pallas_call | solution.py:129
  2.8 0.7 collective-permute-start
  3.5 6.6 %collective-permute-start.1 = (bf16[3,16,2048]{2,1,0:T(8,128)(2,1)S(1)}, bf16[3,16,2048]{2,1,0:T(8,128)(2,1)S(1)}, u32[]{:S(2)}, u32[]{:S(2)}) collective-permute-start(bf16[3,16,2048]{2,1,0:T(8,128)(2,1)S(1)} %get-tuple-element.16), channel_id=1, source_target_pairs={{0,1},{2,3},{4,5},{6,7},{8,9},{10,11},{12,13},{14,15},{16,17},{18,... | collective-permute-start | bytes 589832 | tf_op jit(solution)/shard_map/ppermute | solution.py:268
  10.1 4.0 %collective-permute-start.2 = (bf16[2,16,2048]{2,1,0:T(8,128)(2,1)S(1)}, bf16[2,16,2048]{2,1,0:T(8,128)(2,1)S(1)}, u32[]{:S(2)}, u32[]{:S(2)}) collective-permute-start(bf16[2,16,2048]{2,1,0:T(8,128)(2,1)S(1)} %get-tuple-element.23.refs_0_), channel_id=1, source_target_pairs={{0,128},{128,0},{256,384},{384,256},{1,129},{129,1},{257,385},{385... | collective-permute-start | bytes 393224 | tf_op jit(solution)/shard_map/ppermute | solution.py:272
  14.1 5.8 %collective-permute-start.3 = (bf16[2,16,2048]{2,1,0:T(8,128)(2,1)S(1)}, bf16[2,16,2048]{2,1,0:T(8,128)(2,1)S(1)}, u32[]{:S(2)}, u32[]{:S(2)}) collective-permute-start(bf16[2,16,2048]{2,1,0:T(8,128)(2,1)S(1)} %get-tuple-element.23.refs_0_), channel_id=1, source_target_pairs={{0,256},{128,384},{256,0},{384,128},{1,257},{129,385},{257,1},{385... | collective-permute-start | bytes 393224 | tf_op jit(solution)/shard_map/ppermute | solution.py:272
  19.9 1.9 %collective-permute-start.4 = (bf16[2,16,2048]{2,1,0:T(8,128)(2,1)S(1)}, bf16[2,16,2048]{2,1,0:T(8,128)(2,1)S(1)}, u32[]{:S(2)}, u32[]{:S(2)}) collective-permute-start(bf16[2,16,2048]{2,1,0:T(8,128)(2,1)S(1)} %get-tuple-element.23.refs_0_), channel_id=1, source_target_pairs={{0,384},{128,256},{256,128},{384,0},{1,385},{129,257},{257,129},{3... | collective-permute-start | bytes 393224 | tf_op jit(solution)/shard_map/ppermute | solution.py:272
  21.8 0.0 collective-permute-done.far_ref
  21.8 0.0 collective-permute-done.1.near_ref
  21.8 0.0 copy-done
  21.9 2.0 %advance.1 = (f32[2,16,2048]{2,1,0:T(8,128)}, f32[32,16,128]{2,1,0:T(8,128)}) custom-call(s32[2]{0:T(128)S(1)} %pad_add_fusion.place_ref, f32[2,16,2048]{2,1,0:T(8,128)S(1)} %copy-done, f32[2,16,2048]{2,1,0:T(8,128)S(1)} %get-tuple-element.13.conduct_ref, f32[2,16,2048]{2,1,0:T(8,128)S(1)} %get-tuple-element.14.part_ref, ...), custom_call_target="tpu_custom_call" | custom-call | flops 60000000 | bytes 1800000 | tf_op jit(solution)/shard_map/advance/pallas_call | solution.py:204
  23.8 11.0 %all-to-all-start = ((f32[32,16,128]{2,1,0:T(8,128)}), f32[32,16,128]{2,1,0:T(8,128)S(1)}, u32[]{:S(2)}, u32[]{:S(2)}) async-start(f32[32,16,128]{2,1,0:T(8,128)} %get-tuple-element.19), calls=%async_computation | async-start | bytes 524288 | tf_op jit(solution)/shard_map/all_to_all | solution.py:283
  34.9 0.0 collective-permute-done.2.refs_1_
  34.9 0.0 collective-permute-done.3.refs_2_
  34.9 0.0 collective-permute-done.4.refs_3_
  34.9 0.1 pad_maximum_fusion
  35.0 4.3 %collective-permute-start.5 = (bf16[4,2,16,2048]{3,2,1,0:T(8,128)(2,1)S(1)}, bf16[4,2,16,2048]{3,2,1,0:T(8,128)(2,1)S(1)}, u32[]{:S(2)}, u32[]{:S(2)}) collective-permute-start(bf16[4,2,16,2048]{3,2,1,0:T(8,128)(2,1)S(1)} %pad_maximum_fusion), channel_id=1, source_target_pairs={{0,64},{64,0},{1,65},{65,1},{2,66},{66,2},{3,67},{67,3},{4,68},{68... | collective-permute-start | bytes 1572872 | tf_op jit(solution)/shard_map/ppermute | solution.py:268
  39.3 5.3 %all-to-all-done.found_ref = f32[32,16,128]{2,1,0:T(8,128)S(1)} async-done(((f32[32,16,128]{2,1,0:T(8,128)}), f32[32,16,128]{2,1,0:T(8,128)S(1)}, u32[]{:S(2)}, u32[]{:S(2)}) %all-to-all-start) | async-done | bytes 262176 | tf_op jit(solution)/shard_map/all_to_all | solution.py:283
  44.6 0.0 copy-start.1
  44.6 17.7 %all_to_all.10.found_ref = f32[16,16,128]{2,1,0:T(8,128)S(1)} all-to-all(f32[16,16,128]{2,1,0:T(8,128)S(1)} %spread.1), channel_id=1, replica_groups=mesh['z_lo'=4,'core'=2,'z_hi'=2,'x'=4,'y'=8] {'z_lo','core','z_hi'}, dimensions={0} | all-to-all | bytes 262144 | tf_op jit(solution)/shard_map/all_to_all | solution.py:285
  62.3 4.5 %solve.1.weights_ref = bf16[16,128]{1,0:T(8,128)(2,1)S(1)} custom-call(s32[2]{0:T(128)S(1)} %pad_add_fusion.place_ref, f32[16,16,128]{2,1,0:T(8,128)S(1)} %all_to_all.10.found_ref, f32[16,128]{1,0:T(8,128)S(1)} %get-tuple-element.20.noise_ref, f32[1,128]{1,0:T(1,128)S(1)} %get-tuple-element.21.data_ref, f32[1,128]{1,0:T(1,128)S(1)} %get-tuple-element.22.var_ref), custom_call_target="tpu_custom_call" | custom-call | flops 50000000 | bytes 18000000 | tf_op jit(solution)/shard_map/solve/pallas_call | solution.py:229
  66.8 0.0 collective-permute-done.5.refs_4_
  66.8 0.0 copy-done.1
  66.8 1.0 %increment.1 = f32[2,16,2048]{2,1,0:T(8,128)} custom-call(bf16[16,128]{1,0:T(8,128)(2,1)S(1)} %solve.1.weights_ref, f32[2,16,2048]{2,1,0:T(8,128)S(1)} %copy-done.1, bf16[2,16,2048]{2,1,0:T(8,128)(2,1)S(1)} %get-tuple-element.23.refs_0_, bf16[2,16,2048]{2,1,0:T(8,128)(2,1)S(1)} %collective-permute-done.2.refs_1_, ...), custom_call_target="tpu_custom_call" | custom-call | flops 20000000 | bytes 1700000 | tf_op jit(solution)/shard_map/increment/pallas_call | solution.py:254
  (2 shorter events, 0.0 us)
Async XLA Ops:
  0.7 21.1 %copy-start = (f32[2,16,2048]{2,1,0:T(8,128)S(1)}, f32[2,16,2048]{2,1,0:T(8,128)}, u32[]{:S(2)}) copy-start(f32[2,16,2048]{2,1,0:T(8,128)} %conc_ref.1) | copy-start | bytes 786436
  2.8 19.0 %collective-permute-start = (bf16[3,16,2048]{2,1,0:T(8,128)(2,1)S(1)}, bf16[3,16,2048]{2,1,0:T(8,128)(2,1)S(1)}, u32[]{:S(2)}, u32[]{:S(2)}) collective-permute-start(bf16[3,16,2048]{2,1,0:T(8,128)(2,1)S(1)} %get-tuple-element.15), channel_id=1, source_target_pairs={{1,2},{3,4},{5,6},{7,8},{9,10},{11,12},{13,14},{15,16},{17,18},{19... | collective-permute-start | bytes 589832 | tf_op jit(solution)/shard_map/ppermute | solution.py:268
  3.5 18.3 %collective-permute-start.1 = (bf16[3,16,2048]{2,1,0:T(8,128)(2,1)S(1)}, bf16[3,16,2048]{2,1,0:T(8,128)(2,1)S(1)}, u32[]{:S(2)}, u32[]{:S(2)}) collective-permute-start(bf16[3,16,2048]{2,1,0:T(8,128)(2,1)S(1)} %get-tuple-element.16), channel_id=1, source_target_pairs={{0,1},{2,3},{4,5},{6,7},{8,9},{10,11},{12,13},{14,15},{16,17},{18,... | collective-permute-start | bytes 589832 | tf_op jit(solution)/shard_map/ppermute | solution.py:268
  10.1 24.8 %collective-permute-start.2 = (bf16[2,16,2048]{2,1,0:T(8,128)(2,1)S(1)}, bf16[2,16,2048]{2,1,0:T(8,128)(2,1)S(1)}, u32[]{:S(2)}, u32[]{:S(2)}) collective-permute-start(bf16[2,16,2048]{2,1,0:T(8,128)(2,1)S(1)} %get-tuple-element.23.refs_0_), channel_id=1, source_target_pairs={{0,128},{128,0},{256,384},{384,256},{1,129},{129,1},{257,385},{385... | collective-permute-start | bytes 393224 | tf_op jit(solution)/shard_map/ppermute | solution.py:272
  14.1 20.8 %collective-permute-start.3 = (bf16[2,16,2048]{2,1,0:T(8,128)(2,1)S(1)}, bf16[2,16,2048]{2,1,0:T(8,128)(2,1)S(1)}, u32[]{:S(2)}, u32[]{:S(2)}) collective-permute-start(bf16[2,16,2048]{2,1,0:T(8,128)(2,1)S(1)} %get-tuple-element.23.refs_0_), channel_id=1, source_target_pairs={{0,256},{128,384},{256,0},{384,128},{1,257},{129,385},{257,1},{385... | collective-permute-start | bytes 393224 | tf_op jit(solution)/shard_map/ppermute | solution.py:272
  19.9 15.0 %collective-permute-start.4 = (bf16[2,16,2048]{2,1,0:T(8,128)(2,1)S(1)}, bf16[2,16,2048]{2,1,0:T(8,128)(2,1)S(1)}, u32[]{:S(2)}, u32[]{:S(2)}) collective-permute-start(bf16[2,16,2048]{2,1,0:T(8,128)(2,1)S(1)} %get-tuple-element.23.refs_0_), channel_id=1, source_target_pairs={{0,384},{128,256},{256,128},{384,0},{1,385},{129,257},{257,129},{3... | collective-permute-start | bytes 393224 | tf_op jit(solution)/shard_map/ppermute | solution.py:272
  23.8 20.7 %all-to-all-start = ((f32[32,16,128]{2,1,0:T(8,128)}), f32[32,16,128]{2,1,0:T(8,128)S(1)}, u32[]{:S(2)}, u32[]{:S(2)}) async-start(f32[32,16,128]{2,1,0:T(8,128)} %get-tuple-element.19), calls=%async_computation | async-start | bytes 524288 | tf_op jit(solution)/shard_map/all_to_all | solution.py:283
  35.0 31.8 %collective-permute-start.5 = (bf16[4,2,16,2048]{3,2,1,0:T(8,128)(2,1)S(1)}, bf16[4,2,16,2048]{3,2,1,0:T(8,128)(2,1)S(1)}, u32[]{:S(2)}, u32[]{:S(2)}) collective-permute-start(bf16[4,2,16,2048]{3,2,1,0:T(8,128)(2,1)S(1)} %pad_maximum_fusion), channel_id=1, source_target_pairs={{0,64},{64,0},{1,65},{65,1},{2,66},{66,2},{3,67},{67,3},{4,68},{68... | collective-permute-start | bytes 1572872 | tf_op jit(solution)/shard_map/ppermute | solution.py:268
  44.6 22.2 %copy-start.1 = (f32[2,16,2048]{2,1,0:T(8,128)S(1)}, f32[2,16,2048]{2,1,0:T(8,128)}, u32[]{:S(2)}) copy-start(f32[2,16,2048]{2,1,0:T(8,128)} %perm_ref.1) | copy-start | bytes 786436

commit v5 on v4

--- a/solution.py
+++ b/solution.py
@@ -11,9 +11,10 @@
 HIGH = lax.Precision.HIGHEST
 TN = (((0,), (0,)), ((), ()))
 PANEL = 16
+GRAIN = 32000 / 6
 MEM = ("z_lo", "core")
 SPACE = ("z_hi", "x", "y")
-ORDER = (0, 2, 4, 6, 1, 3, 5, 7)
+ORDER = (0, 4, 6, 2, 1, 5, 7, 3)
 VMEM_LIMIT = 48 * 1024 * 1024
 
 def split3(x):
@@ -85,7 +86,7 @@
 
 
 def prepare_kernel(
-    place_ref, perm_hbm, conc_hbm, wells_hbm, data_hbm, var_hbm, noise_hbm,
+    perm_hbm, conc_hbm, wells_hbm, data_hbm, var_hbm, noise_hbm,
     near_ref, far_ref, low_ref, part_ref, conduct_ref, wells_ref, data_ref, var_ref, noise_ref,
     perm_ref, conc_ref, sem,
 ):
@@ -113,7 +114,7 @@
     part0 = conc0 + time_step * (along_row(conc0, link_right(cond0), 0.5 * cond0) + between)
     part1 = conc1 + time_step * (along_row(conc1, link_right(cond1), 0.5 * cond1) - between)
     part_ref[0], part_ref[1] = part0, part1
-    even = lax.rem(place_ref[0], 2) == 0
+    even = lax.rem(lax.axis_index(SPACE), 2) == 0
     for i, (low_edge, high_edge) in enumerate(((conc0, conc1), (cond0, cond1), (part0, part1))):
         near_ref[i] = jnp.where(even, high_edge, low_edge).astype(BF16)
         far_ref[i] = jnp.where(even, low_edge, high_edge).astype(BF16)
@@ -121,7 +122,7 @@
         copy.wait()
 
 
-def prepare(place, log_perm, conc, wells, obs_data, obs_var, noise):
+def prepare(log_perm, conc, wells, obs_data, obs_var, noise):
     rows, members, width = log_perm.shape
     edge = jax.ShapeDtypeStruct((3, members, width), BF16)
     full = jax.ShapeDtypeStruct(log_perm.shape, F32)
@@ -129,7 +130,7 @@
     return pl.pallas_call(
         prepare_kernel,
         out_shape=(edge, edge, jax.ShapeDtypeStruct(log_perm.shape, BF16), full, full, *small),
-        in_specs=[pl.BlockSpec(memory_space=pltpu.SMEM)] + [pl.BlockSpec(memory_space=pltpu.HBM)] * 6,
+        in_specs=[pl.BlockSpec(memory_space=pltpu.HBM)] * 6,
         out_specs=[pl.BlockSpec(memory_space=pltpu.VMEM)] * 9,
         scratch_shapes=[
             pltpu.VMEM(log_perm.shape, F32),
@@ -139,7 +140,7 @@
         cost_estimate=pl.CostEstimate(flops=2_000_000, bytes_accessed=1_600_000, transcendentals=65536),
         compiler_params=pltpu.CompilerParams(vmem_limit_bytes=VMEM_LIMIT),
         name="prepare",
-    )(place, *[pltpu.with_memory_space_constraint(a, pltpu.HBM) for a in (log_perm, conc, wells, obs_data, obs_var, noise)])
+    )(*[pltpu.with_memory_space_constraint(a, pltpu.HBM) for a in (log_perm, conc, wells, obs_data, obs_var, noise)])
 
 
 def spread_kernel(found_ref, out_ref):
@@ -153,15 +154,15 @@
 def spread(found, copies):
     return pl.pallas_call(
         spread_kernel,
-        out_shape=jax.ShapeDtypeStruct((copies, *found.shape[1:]), F32),
+        out_shape=jax.ShapeDtypeStruct((copies, *found.shape[1:]), found.dtype),
         cost_estimate=pl.CostEstimate(flops=65536, bytes_accessed=400_000, transcendentals=0),
         compiler_params=pltpu.CompilerParams(vmem_limit_bytes=VMEM_LIMIT),
         name="spread",
     )(found)
 
 
-def advance_kernel(place_ref, conc_ref, conduct_ref, part_ref, far_ref, near_ref, wells_ref, out_ref, picked_ref):
-    strip = place_ref[0]
+def advance_kernel(conc_ref, conduct_ref, part_ref, far_ref, near_ref, wells_ref, out_ref, picked_ref):
+    strip = lax.axis_index(SPACE)
     conc0, conc1 = conc_ref[0], conc_ref[1]
     cond0, cond1 = conduct_ref[0], conduct_ref[1]
     even = lax.rem(strip, 2) == 0
@@ -186,50 +187,56 @@
     out_ref[0], out_ref[1] = twice0, twice1
     members, width = twice0.shape
     chunk = 256
-    total = jnp.zeros((3 * members, 128), F32)
-    for row, values in enumerate((twice0, twice1)):
-        pieces = jnp.concatenate(split3(values), axis=0)
-        column = wells_ref[...] - (2 * strip + row) * width
-        for start in range(0, width, chunk):
-            here = lax.broadcasted_iota(jnp.int32, (chunk, 128), 0) + start
-            chosen = jnp.where(here == column, 1.0, 0.0).astype(BF16)
-            total = total + jnp.dot(pieces[:, start : start + chunk], chosen, preferred_element_type=F32)
-    picked = total[:members] + total[members : 2 * members] + total[2 * members :]
+    pieces = jnp.concatenate([*split3(twice0), *split3(twice1)], axis=0)
+    cell = wells_ref[...] - 2 * strip * width
+    column = jnp.where(cell >= width, cell - width, cell)
+    total = jnp.zeros((6 * members, 128), F32)
+    for start in range(0, width, chunk):
+        here = lax.broadcasted_iota(jnp.int32, (chunk, 128), 0) + start
+        chosen = jnp.where(here == column, 1.0, 0.0).astype(BF16)
+        total = total + jnp.dot(pieces[:, start : start + chunk], chosen, preferred_element_type=F32)
+    upper, lower = [
+        total[i : i + members] + total[i + members : i + 2 * members] + total[i + 2 * members : i + 3 * members]
+        for i in (0, 3 * members)
+    ]
+    picked = jnp.where(jnp.broadcast_to(cell, upper.shape) >= width, lower, upper)
+    picked = jnp.round(picked * GRAIN).astype(jnp.int32).astype(jnp.int16)
     for copy in range(picked_ref.shape[0]):
         picked_ref[copy] = picked
 
 
-def advance(place, conc, conduct, part, far, near, wells, copies):
+def advance(conc, conduct, part, far, near, wells, copies):
     vmem = pl.BlockSpec(memory_space=pltpu.VMEM)
     return pl.pallas_call(
         advance_kernel,
         out_shape=(
             jax.ShapeDtypeStruct(conc.shape, F32),
-            jax.ShapeDtypeStruct((copies, conc.shape[1], 128), F32),
+            jax.ShapeDtypeStruct((copies, conc.shape[1], 128), jnp.int16),
         ),
-        in_specs=[pl.BlockSpec(memory_space=pltpu.SMEM)] + [vmem] * 6,
+        in_specs=[vmem] * 6,
         out_specs=(vmem, vmem),
         cost_estimate=pl.CostEstimate(flops=60_000_000, bytes_accessed=1_800_000, transcendentals=0),
         compiler_params=pltpu.CompilerParams(vmem_limit_bytes=VMEM_LIMIT),
         name="advance",
-    )(place, conc, conduct, part, far, near, wells)
-
-
-def solve_kernel(place_ref, found_ref, noise_ref, data_ref, var_ref, out_ref, pred, work, solved):
-    group = place_ref[1]
+    )(conc, conduct, part, far, near, wells)
+
+
+def solve_kernel(found_ref, noise_ref, data_ref, var_ref, out_ref, pred, work, solved):
+    group = lax.axis_index(MEM)
     for position, flip in enumerate(ORDER):
         block = lax.bitwise_xor(group, flip)
-        pred[pl.ds(position * 16, 16), :] = found_ref[2 * block] + found_ref[2 * block + 1]
+        code = found_ref[2 * block].astype(jnp.int32) + found_ref[2 * block + 1].astype(jnp.int32)
+        pred[pl.ds(position * 16, 16), :] = code.astype(F32) * (1 / GRAIN)
     centred = weights_of(pred[...], pred[0:16], noise_ref[...], data_ref[...], var_ref[...], work, solved)
     out_ref[...] = centred.astype(BF16)
 
 
-def solve(place, found, noise, obs_data, obs_var):
+def solve(found, noise, obs_data, obs_var):
     vmem = pl.BlockSpec(memory_space=pltpu.VMEM)
     return pl.pallas_call(
         solve_kernel,
         out_shape=jax.ShapeDtypeStruct((16, 128), BF16),
-        in_specs=[pl.BlockSpec(memory_space=pltpu.SMEM)] + [vmem] * 4,
+        in_specs=[vmem] * 4,
         out_specs=vmem,
         scratch_shapes=[
             pltpu.VMEM((128, 128), F32),
@@ -239,28 +246,29 @@
         cost_estimate=pl.CostEstimate(flops=50_000_000, bytes_accessed=18_000_000, transcendentals=128),
         compiler_params=pltpu.CompilerParams(vmem_limit_bytes=VMEM_LIMIT),
         name="solve",
-    )(place, found, noise, obs_data, obs_var)
+    )(found, noise, obs_data, obs_var)
 
 
 def increment_kernel(weights_ref, perm_ref, *refs):
-    *pieces, odd_ref, out_ref = refs
+    *pieces, out_ref = refs
     for row in range(2):
-        members = [piece[row] for piece in pieces] + [odd_ref[i, row] for i in range(odd_ref.shape[0])]
+        members = [piece[i, row] for piece in pieces for i in range(piece.shape[0])]
         stacked = jnp.concatenate(members, axis=0)
         out_ref[row] = perm_ref[row] + jnp.dot(weights_ref[...], stacked, preferred_element_type=F32)
 
 
-def increment(weights, log_perm, pieces, odd):
+def increment(weights, log_perm, pieces):
     return pl.pallas_call(
         increment_kernel,
         out_shape=jax.ShapeDtypeStruct(log_perm.shape, F32),
         cost_estimate=pl.CostEstimate(flops=20_000_000, bytes_accessed=1_700_000, transcendentals=0),
         compiler_params=pltpu.CompilerParams(vmem_limit_bytes=VMEM_LIMIT),
         name="increment",
-    )(weights, log_perm, *pieces, odd)
+    )(weights, log_perm, *pieces)
 
 
 STRIPS = 64
+PLANES = [list(range(STRIPS // 2 - 1, -1, -1)), list(range(STRIPS // 2, STRIPS))]
 
 
 def swapped(value, axis, first, count):
@@ -273,19 +281,20 @@
 
 
 def local(log_perm, concentration, well_cells, obs_data, obs_var, obs_noise):
-    place = jnp.stack([lax.axis_index(SPACE), lax.axis_index(MEM)]).astype(jnp.int32)
     near, far, low, part, conduct, wells, data, var, noise = prepare(
-        place, log_perm, concentration, well_cells[None], obs_data[None], obs_var[None], obs_noise
+        log_perm, concentration, well_cells[None], obs_data[None], obs_var[None], obs_noise
     )
     far = swapped(far, SPACE, 1, STRIPS)
     near = swapped(near, SPACE, 0, STRIPS)
-    tracer, picked = advance(place, concentration, conduct, part, far, near, wells, 32)
-    found = lax.all_to_all(picked, ("x", "y"), 0, 0, tiled=True)
-    even = [low] + [crossed(low, flip) for flip in (1, 2, 3)]
+    tracer, picked = advance(concentration, conduct, part, far, near, wells, 32)
+    last, *pair = [crossed(low, flip) for flip in (1, 2, 3)]
+    pair = jnp.stack(pair)
+    found = lax.all_to_all(picked, SPACE, 0, 0, axis_index_groups=PLANES, tiled=True)
     found = lax.all_to_all(spread(found, 16), ("z_lo", "core", "z_hi"), 0, 0, tiled=True)
-    odd = swapped(jnp.stack(even), "core", 0, 2)
-    weights = solve(place, found, noise, data, var)
-    updated = increment(weights, log_perm, even, odd)
+    mine = [low[None], pair, last[None]]
+    pieces = mine + [swapped(piece, "core", 0, 2) for piece in mine]
+    weights = solve(found, noise, data, var)
+    updated = increment(weights, log_perm, pieces)
     return (tracer, updated)
 
 

time: 68.1 us -> 64 us (0.940)
  waiting for transfers between devices: 5.29 us -> 0.03 us
  starting transfers between devices: 34.3 us -> 39.3 us
  blocking collectives: 17.7 us -> 15.5 us
  Pallas kernels: 9.57 us -> 7.87 us
    all_to_all x1, waiting for transfers between devices: 5.28 us -> 0.01 us  [local(): lax.all_to_all(picked, SPACE, 0, 0, axis_index_groups=PLANES, tiled=True)]
    ppermute x3 -> x5, starting transfers between devices: 11.5 us -> 15.7 us  [swapped(): lax.ppermute(value, axis, pairs + [(high, low) for low, high in pairs])]
    all_to_all x1, blocking collectives: 17.7 us -> 15.5 us  [local(): lax.all_to_all(spread(found, 16), ('z_lo', 'core', 'z_hi'), 0, 0, tiled=T...]
    all_to_all x1, starting transfers between devices: 11 us -> 11.9 us  [local(): lax.all_to_all(picked, SPACE, 0, 0, axis_index_groups=PLANES, tiled=True)]
  transfers between devices with their start and end apart: 7 -> 9, of which waited for: 1 -> 0; matrix products, arithmetic and copies ran while one was open for 0% -> 0% of each run, Pallas kernels for 10% -> 8%
where the time goes in v5:
time: 64 us; the launch traced here: 63.5 us
  starting transfers between devices  39.3 us (61%)
  blocking collectives  15.5 us (24%)
  Pallas kernels  7.87 us (12%)
  between operations  0.82 us (1%)
    ppermute x5, starting transfers between devices, swapped(): lax.ppermute(value, axis, pairs + [(high, low) for low, high in pairs])  15.7 us
    all_to_all x1, blocking collectives, local(): lax.all_to_all(spread(found, 16), ('z_lo', 'core', 'z_hi'), 0, 0, tiled=T...  15.5 us
    all_to_all x1, starting transfers between devices, local(): lax.all_to_all(picked, SPACE, 0, 0, axis_index_groups=PLANES, tiled=True)  11.9 us
    ppermute x3, starting transfers between devices, crossed(): return lax.ppermute(value, 'z_lo', [(i, i ^ flip) for i in range(4)])  11.7 us
    pallas_call x1, Pallas kernels, solve(): pl.pallas_call(solve_kernel, out_shape=jax.ShapeDtypeStruct((16, 128), BF...  3.96 us
    pallas_call x1, Pallas kernels, prepare(): pl.pallas_call(prepare_kernel, out_shape=(edge, edge, jax.ShapeDtypeStruc...  1.59 us
    pallas_call x1, Pallas kernels, advance(): pl.pallas_call(advance_kernel, out_shape=(jax.ShapeDtypeStruct(conc.shape...  1.32 us
  transfers between devices with their start and end apart: 9, of which 0 were waited for; matrix products, arithmetic and copies ran while one was open for 0% of the time, Pallas kernels for 8%

profile of v5, /device:TPU:1, one launch (start us, length us, event | category | flops | bytes accessed | tf_op | source)
XLA Modules:
  0.0 63.5 jit_solution(6979852360604642999)
XLA Ops:
  0.6 1.6 %prepare.1 = (bf16[3,16,2048]{2,1,0:T(8,128)(2,1)S(1)}, bf16[3,16,2048]{2,1,0:T(8,128)(2,1)S(1)}, bf16[2,16,2048]{2,1,0:T(8,128)(2,1)S(1)}, f32[2,16,2048]{2,1,0...) custom-call(f32[2,16,2048]{2,1,0:T(8,128)} %perm_ref.1, ...), custom_call_target="tpu_custom_call" | custom-call | flops 2000000 | bytes 1600000 | tf_op jit(solution)/shard_map/prepare/pallas_call | solution.py:130
  2.2 0.7 %collective-permute-start = (bf16[3,16,2048]{2,1,0:T(8,128)(2,1)S(1)}, bf16[3,16,2048]{2,1,0:T(8,128)(2,1)S(1)}, u32[]{:S(2)}, u32[]{:S(2)}) collective-permute-start(bf16[3,16,2048]{2,1,0:T(8,128)(2,1)S(1)} %get-tuple-element.15), channel_id=1, source_target_pairs={{1,2},{3,4},{5,6},{7,8},{9,10},{11,12},{13,14},{15,16},{17,18},{19... | collective-permute-start | bytes 589832 | tf_op jit(solution)/shard_map/ppermute | solution.py:276
  2.9 6.6 %collective-permute-start.1 = (bf16[3,16,2048]{2,1,0:T(8,128)(2,1)S(1)}, bf16[3,16,2048]{2,1,0:T(8,128)(2,1)S(1)}, u32[]{:S(2)}, u32[]{:S(2)}) collective-permute-start(bf16[3,16,2048]{2,1,0:T(8,128)(2,1)S(1)} %get-tuple-element.16), channel_id=1, source_target_pairs={{0,1},{2,3},{4,5},{6,7},{8,9},{10,11},{12,13},{14,15},{16,17},{18,... | collective-permute-start | bytes 589832 | tf_op jit(solution)/shard_map/ppermute | solution.py:276
  9.5 7.6 %collective-permute-start.3 = (bf16[2,16,2048]{2,1,0:T(8,128)(2,1)S(1)}, bf16[2,16,2048]{2,1,0:T(8,128)(2,1)S(1)}, u32[]{:S(2)}, u32[]{:S(2)}) collective-permute-start(bf16[2,16,2048]{2,1,0:T(8,128)(2,1)S(1)} %get-tuple-element.23), channel_id=1, source_target_pairs={{0,384},{128,256},{256,128},{384,0},{1,385},{129,257},{257,129},{3... | collective-permute-start | bytes 393224 | tf_op jit(solution)/shard_map/ppermute | solution.py:280
  17.1 1.9 %collective-permute-start.2 = (bf16[2,16,2048]{2,1,0:T(8,128)(2,1)S(1)}, bf16[2,16,2048]{2,1,0:T(8,128)(2,1)S(1)}, u32[]{:S(2)}, u32[]{:S(2)}) collective-permute-start(bf16[2,16,2048]{2,1,0:T(8,128)(2,1)S(1)} %get-tuple-element.23), channel_id=1, source_target_pairs={{0,256},{128,384},{256,0},{384,128},{1,257},{129,385},{257,1},{385... | collective-permute-start | bytes 393224 | tf_op jit(solution)/shard_map/ppermute | solution.py:280
  19.0 2.2 %collective-permute-start.4 = (bf16[2,16,2048]{2,1,0:T(8,128)(2,1)S(1)}, bf16[2,16,2048]{2,1,0:T(8,128)(2,1)S(1)}, u32[]{:S(2)}, u32[]{:S(2)}) collective-permute-start(bf16[2,16,2048]{2,1,0:T(8,128)(2,1)S(1)} %get-tuple-element.23), channel_id=1, source_target_pairs={{0,128},{128,0},{256,384},{384,256},{1,129},{129,1},{257,385},{385... | collective-permute-start | bytes 393224 | tf_op jit(solution)/shard_map/ppermute | solution.py:280
  21.2 0.0 collective-permute-done.far_ref
  21.3 0.0 collective-permute-done.1.near_ref
  21.3 1.3 %advance.1 = (f32[2,16,2048]{2,1,0:T(8,128)}, s16[32,16,128]{2,1,0:T(8,128)(2,1)}) custom-call(f32[2,16,2048]{2,1,0:T(8,128)S(1)} %copy-done, f32[2,16,2048]{2,1,0:T(8,128)S(1)} %get-tuple-element.13.conduct_ref, f32[2,16,2048]{2,1,0:T(8,128)S(1)} %get-tuple-element.14.part_ref, bf16[3,16,2048]{2,1,0:T(8,128)(2,1)S(1)} %collective-permute-done.far_ref, ...), custom_call_target="tpu_custom_call" | custom-call | flops 60000000 | bytes 1800000 | tf_op jit(solution)/shard_map/advance/pallas_call | solution.py:210
  22.6 11.9 %all-to-all-start = ((s16[32,16,128]{2,1,0:T(8,128)(2,1)}), s16[32,16,128]{2,1,0:T(8,128)(2,1)S(1)}, u32[]{:S(2)}, u32[]{:S(2)}) async-start(s16[32,16,128]{2,1,0:T(8,128)(2,1)} %get-tuple-element.19), calls=%async_computation | async-start | bytes 262144 | tf_op jit(solution)/shard_map/all_to_all | solution.py:292
  34.5 0.0 collective-permute-done.3
  34.5 0.0 collective-permute-done.2
  34.6 0.0 copy-start.1
  34.6 4.1 %collective-permute-start.6 = (bf16[2,2,16,2048]{3,2,1,0:T(8,128)(2,1)S(1)}, bf16[2,2,16,2048]{3,2,1,0:T(8,128)(2,1)S(1)}, u32[]{:S(2)}, u32[]{:S(2)}) collective-permute-start(bf16[2,2,16,2048]{3,2,1,0:T(8,128)(2,1)S(1)} %pad_maximum_fusion.refs_1_), channel_id=1, source_target_pairs={{0,64},{64,0},{1,65},{65,1},{2,66},{66,2},{3,67},{67,3},{4,68},{68... | collective-permute-start | bytes 786440 | tf_op jit(solution)/shard_map/ppermute | solution.py:276
  38.7 1.9 %collective-permute-start.5 = (bf16[1,2,16,2048]{3,2,1,0:T(8,128)(2,1)S(1)}, bf16[1,2,16,2048]{3,2,1,0:T(8,128)(2,1)S(1)}, u32[]{:S(2)}, u32[]{:S(2)}) collective-permute-start(bf16[1,2,16,2048]{3,2,1,0:T(8,128)(2,1)S(1)} %bitcast.7), channel_id=1, source_target_pairs={{0,64},{64,0},{1,65},{65,1},{2,66},{66,2},{3,67},{67,3},{4,68},{68... | collective-permute-start | bytes 393224 | tf_op jit(solution)/shard_map/ppermute | solution.py:276
  40.6 0.0 collective-permute-done.4
  40.6 2.4 %collective-permute-start.7 = (bf16[1,2,16,2048]{3,2,1,0:T(8,128)(2,1)S(1)}, bf16[1,2,16,2048]{3,2,1,0:T(8,128)(2,1)S(1)}, u32[]{:S(2)}, u32[]{:S(2)}) collective-permute-start(bf16[1,2,16,2048]{3,2,1,0:T(8,128)(2,1)S(1)} %bitcast.9), channel_id=1, source_target_pairs={{0,64},{64,0},{1,65},{65,1},{2,66},{66,2},{3,67},{67,3},{4,68},{68... | collective-permute-start | bytes 393224 | tf_op jit(solution)/shard_map/ppermute | solution.py:276
  43.1 0.0 all-to-all-done.found_ref
  43.1 15.5 %all_to_all.10.found_ref = s16[16,16,128]{2,1,0:T(8,128)(2,1)S(1)} all-to-all(s16[16,16,128]{2,1,0:T(8,128)(2,1)S(1)} %spread.1), channel_id=1, replica_groups=mesh['z_lo'=4,'core'=2,'z_hi'=2,'x'=4,'y'=8] {'z_lo','core','z_hi'}, dimensions={0} | all-to-all | bytes 131072 | tf_op jit(solution)/shard_map/all_to_all | solution.py:293
  58.6 4.0 %solve.1.weights_ref = bf16[16,128]{1,0:T(8,128)(2,1)S(1)} custom-call(s16[16,16,128]{2,1,0:T(8,128)(2,1)S(1)} %all_to_all.10.found_ref, f32[16,128]{1,0:T(8,128)S(1)} %get-tuple-element.20.noise_ref, f32[1,128]{1,0:T(1,128)S(1)} %get-tuple-element.21.data_ref, f32[1,128]{1,0:T(1,128)S(1)} %get-tuple-element.22.var_ref), custom_call_target="tpu_custom_call" | custom-call | flops 50000000 | bytes 18000000 | tf_op jit(solution)/shard_map/solve/pallas_call | solution.py:236
  62.5 0.0 collective-permute-done.5.refs_3_
  62.5 0.0 collective-permute-done.7.refs_5_
  62.6 0.0 collective-permute-done.6.refs_4_
  62.6 1.0 %increment.1 = f32[2,16,2048]{2,1,0:T(8,128)} custom-call(bf16[16,128]{1,0:T(8,128)(2,1)S(1)} %solve.1.weights_ref, f32[2,16,2048]{2,1,0:T(8,128)S(1)} %copy-done.1, bf16[1,2,16,2048]{3,2,1,0:T(8,128)(2,1)S(1)} %bitcast.8, bf16[2,2,16,2048]{3,2,1,0:T(8,128)(2,1)S(1)} %pad_maximum_fusion.refs_1_, bf16[1,2,16,2048]{3,2,1,0:T(8,128)(2,1)S(1)} %bitcast.10, ...), custom_call_target="tpu_custom_call" | custom-call | flops 20000000 | bytes 1700000 | tf_op jit(solution)/shard_map/increment/pallas_call | solution.py:261
  (5 shorter events, 0.1 us)
Async XLA Ops:
  0.6 20.6 %copy-start = (f32[2,16,2048]{2,1,0:T(8,128)S(1)}, f32[2,16,2048]{2,1,0:T(8,128)}, u32[]{:S(2)}) copy-start(f32[2,16,2048]{2,1,0:T(8,128)} %conc_ref.1) | copy-start | bytes 786436
  2.2 19.0 %collective-permute-start = (bf16[3,16,2048]{2,1,0:T(8,128)(2,1)S(1)}, bf16[3,16,2048]{2,1,0:T(8,128)(2,1)S(1)}, u32[]{:S(2)}, u32[]{:S(2)}) collective-permute-start(bf16[3,16,2048]{2,1,0:T(8,128)(2,1)S(1)} %get-tuple-element.15), channel_id=1, source_target_pairs={{1,2},{3,4},{5,6},{7,8},{9,10},{11,12},{13,14},{15,16},{17,18},{19... | collective-permute-start | bytes 589832 | tf_op jit(solution)/shard_map/ppermute | solution.py:276
  2.9 18.3 %collective-permute-start.1 = (bf16[3,16,2048]{2,1,0:T(8,128)(2,1)S(1)}, bf16[3,16,2048]{2,1,0:T(8,128)(2,1)S(1)}, u32[]{:S(2)}, u32[]{:S(2)}) collective-permute-start(bf16[3,16,2048]{2,1,0:T(8,128)(2,1)S(1)} %get-tuple-element.16), channel_id=1, source_target_pairs={{0,1},{2,3},{4,5},{6,7},{8,9},{10,11},{12,13},{14,15},{16,17},{18,... | collective-permute-start | bytes 589832 | tf_op jit(solution)/shard_map/ppermute | solution.py:276
  9.5 25.0 %collective-permute-start.3 = (bf16[2,16,2048]{2,1,0:T(8,128)(2,1)S(1)}, bf16[2,16,2048]{2,1,0:T(8,128)(2,1)S(1)}, u32[]{:S(2)}, u32[]{:S(2)}) collective-permute-start(bf16[2,16,2048]{2,1,0:T(8,128)(2,1)S(1)} %get-tuple-element.23), channel_id=1, source_target_pairs={{0,384},{128,256},{256,128},{384,0},{1,385},{129,257},{257,129},{3... | collective-permute-start | bytes 393224 | tf_op jit(solution)/shard_map/ppermute | solution.py:280
  17.1 17.4 %collective-permute-start.2 = (bf16[2,16,2048]{2,1,0:T(8,128)(2,1)S(1)}, bf16[2,16,2048]{2,1,0:T(8,128)(2,1)S(1)}, u32[]{:S(2)}, u32[]{:S(2)}) collective-permute-start(bf16[2,16,2048]{2,1,0:T(8,128)(2,1)S(1)} %get-tuple-element.23), channel_id=1, source_target_pairs={{0,256},{128,384},{256,0},{384,128},{1,257},{129,385},{257,1},{385... | collective-permute-start | bytes 393224 | tf_op jit(solution)/shard_map/ppermute | solution.py:280
  19.0 21.6 %collective-permute-start.4 = (bf16[2,16,2048]{2,1,0:T(8,128)(2,1)S(1)}, bf16[2,16,2048]{2,1,0:T(8,128)(2,1)S(1)}, u32[]{:S(2)}, u32[]{:S(2)}) collective-permute-start(bf16[2,16,2048]{2,1,0:T(8,128)(2,1)S(1)} %get-tuple-element.23), channel_id=1, source_target_pairs={{0,128},{128,0},{256,384},{384,256},{1,129},{129,1},{257,385},{385... | collective-permute-start | bytes 393224 | tf_op jit(solution)/shard_map/ppermute | solution.py:280
  22.6 20.5 %all-to-all-start = ((s16[32,16,128]{2,1,0:T(8,128)(2,1)}), s16[32,16,128]{2,1,0:T(8,128)(2,1)S(1)}, u32[]{:S(2)}, u32[]{:S(2)}) async-start(s16[32,16,128]{2,1,0:T(8,128)(2,1)} %get-tuple-element.19), calls=%async_computation | async-start | bytes 262144 | tf_op jit(solution)/shard_map/all_to_all | solution.py:292
  34.6 28.0 %copy-start.1 = (f32[2,16,2048]{2,1,0:T(8,128)S(1)}, f32[2,16,2048]{2,1,0:T(8,128)}, u32[]{:S(2)}) copy-start(f32[2,16,2048]{2,1,0:T(8,128)} %perm_ref.1) | copy-start | bytes 786436
  34.6 28.0 %collective-permute-start.6 = (bf16[2,2,16,2048]{3,2,1,0:T(8,128)(2,1)S(1)}, bf16[2,2,16,2048]{3,2,1,0:T(8,128)(2,1)S(1)}, u32[]{:S(2)}, u32[]{:S(2)}) collective-permute-start(bf16[2,2,16,2048]{3,2,1,0:T(8,128)(2,1)S(1)} %pad_maximum_fusion.refs_1_), channel_id=1, source_target_pairs={{0,64},{64,0},{1,65},{65,1},{2,66},{66,2},{3,67},{67,3},{4,68},{68... | collective-permute-start | bytes 786440 | tf_op jit(solution)/shard_map/ppermute | solution.py:276
  38.7 23.8 %collective-permute-start.5 = (bf16[1,2,16,2048]{3,2,1,0:T(8,128)(2,1)S(1)}, bf16[1,2,16,2048]{3,2,1,0:T(8,128)(2,1)S(1)}, u32[]{:S(2)}, u32[]{:S(2)}) collective-permute-start(bf16[1,2,16,2048]{3,2,1,0:T(8,128)(2,1)S(1)} %bitcast.7), channel_id=1, source_target_pairs={{0,64},{64,0},{1,65},{65,1},{2,66},{66,2},{3,67},{67,3},{4,68},{68... | collective-permute-start | bytes 393224 | tf_op jit(solution)/shard_map/ppermute | solution.py:276
  40.6 21.9 %collective-permute-start.7 = (bf16[1,2,16,2048]{3,2,1,0:T(8,128)(2,1)S(1)}, bf16[1,2,16,2048]{3,2,1,0:T(8,128)(2,1)S(1)}, u32[]{:S(2)}, u32[]{:S(2)}) collective-permute-start(bf16[1,2,16,2048]{3,2,1,0:T(8,128)(2,1)S(1)} %bitcast.9), channel_id=1, source_target_pairs={{0,64},{64,0},{1,65},{65,1},{2,66},{66,2},{3,67},{67,3},{4,68},{68... | collective-permute-start | bytes 393224 | tf_op jit(solution)/shard_map/ppermute | solution.py:276

commit v6 on v5

--- a/solution.py
+++ b/solution.py
@@ -10,7 +10,7 @@
 inflation = 4.0
 HIGH = lax.Precision.HIGHEST
 TN = (((0,), (0,)), ((), ()))
-PANEL = 16
+PANEL = 32
 GRAIN = 32000 / 6
 MEM = ("z_lo", "core")
 SPACE = ("z_hi", "x", "y")
@@ -225,7 +225,8 @@
     group = lax.axis_index(MEM)
     for position, flip in enumerate(ORDER):
         block = lax.bitwise_xor(group, flip)
-        code = found_ref[2 * block].astype(jnp.int32) + found_ref[2 * block + 1].astype(jnp.int32)
+        place = 8 * lax.rem(block, 2) + block // 2
+        code = found_ref[place].astype(jnp.int32) + found_ref[place + 4].astype(jnp.int32)
         pred[pl.ds(position * 16, 16), :] = code.astype(F32) * (1 / GRAIN)
     centred = weights_of(pred[...], pred[0:16], noise_ref[...], data_ref[...], var_ref[...], work, solved)
     out_ref[...] = centred.astype(BF16)
@@ -290,7 +291,7 @@
     last, *pair = [crossed(low, flip) for flip in (1, 2, 3)]
     pair = jnp.stack(pair)
     found = lax.all_to_all(picked, SPACE, 0, 0, axis_index_groups=PLANES, tiled=True)
-    found = lax.all_to_all(spread(found, 16), ("z_lo", "core", "z_hi"), 0, 0, tiled=True)
+    found = lax.all_to_all(spread(found, 16), ("core", "z_hi", "z_lo"), 0, 0, tiled=True)
     mine = [low[None], pair, last[None]]
     pieces = mine + [swapped(piece, "core", 0, 2) for piece in mine]
     weights = solve(found, noise, data, var)

time: 64 us -> 63.3 us (0.989)
  no operation moved by 1% of the time
where the time goes in v6:
time: 63.3 us; the launch traced here: 62.9 us
  starting transfers between devices  39.3 us (62%)
  blocking collectives  15 us (24%)
  Pallas kernels  7.7 us (12%)
  between operations  0.82 us (1%)
    ppermute x5, starting transfers between devices, swapped(): lax.ppermute(value, axis, pairs + [(high, low) for low, high in pairs])  15.7 us
    all_to_all x1, blocking collectives, local(): lax.all_to_all(spread(found, 16), ('core', 'z_hi', 'z_lo'), 0, 0, tiled=T...  15 us
    all_to_all x1, starting transfers between devices, local(): lax.all_to_all(picked, SPACE, 0, 0, axis_index_groups=PLANES, tiled=True)  11.9 us
    ppermute x3, starting transfers between devices, crossed(): return lax.ppermute(value, 'z_lo', [(i, i ^ flip) for i in range(4)])  11.7 us
    pallas_call x1, Pallas kernels, solve(): pl.pallas_call(solve_kernel, out_shape=jax.ShapeDtypeStruct((16, 128), BF...  3.79 us
    pallas_call x1, Pallas kernels, prepare(): pl.pallas_call(prepare_kernel, out_shape=(edge, edge, jax.ShapeDtypeStruc...  1.59 us
    pallas_call x1, Pallas kernels, advance(): pl.pallas_call(advance_kernel, out_shape=(jax.ShapeDtypeStruct(conc.shape...  1.32 us
  transfers between devices with their start and end apart: 9, of which 0 were waited for; matrix products, arithmetic and copies ran while one was open for 0% of the time, Pallas kernels for 8%

profile of v6, /device:TPU:1, one launch (start us, length us, event | category | flops | bytes accessed | tf_op | source)
XLA Modules:
  0.0 62.9 jit_solution(16985384735385672261)
XLA Ops:
  0.6 1.6 %prepare.1 = (bf16[3,16,2048]{2,1,0:T(8,128)(2,1)S(1)}, bf16[3,16,2048]{2,1,0:T(8,128)(2,1)S(1)}, bf16[2,16,2048]{2,1,0:T(8,128)(2,1)S(1)}, f32[2,16,2048]{2,1,0...) custom-call(f32[2,16,2048]{2,1,0:T(8,128)} %perm_ref.1, ...), custom_call_target="tpu_custom_call" | custom-call | flops 2000000 | bytes 1600000 | tf_op jit(solution)/shard_map/prepare/pallas_call | solution.py:130
  2.2 0.7 %collective-permute-start = (bf16[3,16,2048]{2,1,0:T(8,128)(2,1)S(1)}, bf16[3,16,2048]{2,1,0:T(8,128)(2,1)S(1)}, u32[]{:S(2)}, u32[]{:S(2)}) collective-permute-start(bf16[3,16,2048]{2,1,0:T(8,128)(2,1)S(1)} %get-tuple-element.15), channel_id=1, source_target_pairs={{1,2},{3,4},{5,6},{7,8},{9,10},{11,12},{13,14},{15,16},{17,18},{19... | collective-permute-start | bytes 589832 | tf_op jit(solution)/shard_map/ppermute | solution.py:277
  2.9 6.6 %collective-permute-start.1 = (bf16[3,16,2048]{2,1,0:T(8,128)(2,1)S(1)}, bf16[3,16,2048]{2,1,0:T(8,128)(2,1)S(1)}, u32[]{:S(2)}, u32[]{:S(2)}) collective-permute-start(bf16[3,16,2048]{2,1,0:T(8,128)(2,1)S(1)} %get-tuple-element.16), channel_id=1, source_target_pairs={{0,1},{2,3},{4,5},{6,7},{8,9},{10,11},{12,13},{14,15},{16,17},{18,... | collective-permute-start | bytes 589832 | tf_op jit(solution)/shard_map/ppermute | solution.py:277
  9.5 7.6 %collective-permute-start.3 = (bf16[2,16,2048]{2,1,0:T(8,128)(2,1)S(1)}, bf16[2,16,2048]{2,1,0:T(8,128)(2,1)S(1)}, u32[]{:S(2)}, u32[]{:S(2)}) collective-permute-start(bf16[2,16,2048]{2,1,0:T(8,128)(2,1)S(1)} %get-tuple-element.23), channel_id=1, source_target_pairs={{0,384},{128,256},{256,128},{384,0},{1,385},{129,257},{257,129},{3... | collective-permute-start | bytes 393224 | tf_op jit(solution)/shard_map/ppermute | solution.py:281
  17.1 1.9 %collective-permute-start.2 = (bf16[2,16,2048]{2,1,0:T(8,128)(2,1)S(1)}, bf16[2,16,2048]{2,1,0:T(8,128)(2,1)S(1)}, u32[]{:S(2)}, u32[]{:S(2)}) collective-permute-start(bf16[2,16,2048]{2,1,0:T(8,128)(2,1)S(1)} %get-tuple-element.23), channel_id=1, source_target_pairs={{0,256},{128,384},{256,0},{384,128},{1,257},{129,385},{257,1},{385... | collective-permute-start | bytes 393224 | tf_op jit(solution)/shard_map/ppermute | solution.py:281
  19.0 2.2 %collective-permute-start.4 = (bf16[2,16,2048]{2,1,0:T(8,128)(2,1)S(1)}, bf16[2,16,2048]{2,1,0:T(8,128)(2,1)S(1)}, u32[]{:S(2)}, u32[]{:S(2)}) collective-permute-start(bf16[2,16,2048]{2,1,0:T(8,128)(2,1)S(1)} %get-tuple-element.23), channel_id=1, source_target_pairs={{0,128},{128,0},{256,384},{384,256},{1,129},{129,1},{257,385},{385... | collective-permute-start | bytes 393224 | tf_op jit(solution)/shard_map/ppermute | solution.py:281
  21.2 0.0 collective-permute-done.far_ref
  21.3 0.0 collective-permute-done.1.near_ref
  21.3 1.3 %advance.1 = (f32[2,16,2048]{2,1,0:T(8,128)}, s16[32,16,128]{2,1,0:T(8,128)(2,1)}) custom-call(f32[2,16,2048]{2,1,0:T(8,128)S(1)} %copy-done, f32[2,16,2048]{2,1,0:T(8,128)S(1)} %get-tuple-element.13.conduct_ref, f32[2,16,2048]{2,1,0:T(8,128)S(1)} %get-tuple-element.14.part_ref, bf16[3,16,2048]{2,1,0:T(8,128)(2,1)S(1)} %collective-permute-done.far_ref, ...), custom_call_target="tpu_custom_call" | custom-call | flops 60000000 | bytes 1800000 | tf_op jit(solution)/shard_map/advance/pallas_call | solution.py:210
  22.6 11.9 %all-to-all-start = ((s16[32,16,128]{2,1,0:T(8,128)(2,1)}), s16[32,16,128]{2,1,0:T(8,128)(2,1)S(1)}, u32[]{:S(2)}, u32[]{:S(2)}) async-start(s16[32,16,128]{2,1,0:T(8,128)(2,1)} %get-tuple-element.19), calls=%async_computation | async-start | bytes 262144 | tf_op jit(solution)/shard_map/all_to_all | solution.py:293
  34.5 0.0 collective-permute-done.3
  34.5 0.0 collective-permute-done.2
  34.6 0.0 copy-start.1
  34.6 4.1 %collective-permute-start.6 = (bf16[2,2,16,2048]{3,2,1,0:T(8,128)(2,1)S(1)}, bf16[2,2,16,2048]{3,2,1,0:T(8,128)(2,1)S(1)}, u32[]{:S(2)}, u32[]{:S(2)}) collective-permute-start(bf16[2,2,16,2048]{3,2,1,0:T(8,128)(2,1)S(1)} %pad_maximum_fusion.refs_1_), channel_id=1, source_target_pairs={{0,64},{64,0},{1,65},{65,1},{2,66},{66,2},{3,67},{67,3},{4,68},{68... | collective-permute-start | bytes 786440 | tf_op jit(solution)/shard_map/ppermute | solution.py:277
  38.7 1.9 %collective-permute-start.5 = (bf16[1,2,16,2048]{3,2,1,0:T(8,128)(2,1)S(1)}, bf16[1,2,16,2048]{3,2,1,0:T(8,128)(2,1)S(1)}, u32[]{:S(2)}, u32[]{:S(2)}) collective-permute-start(bf16[1,2,16,2048]{3,2,1,0:T(8,128)(2,1)S(1)} %bitcast.7), channel_id=1, source_target_pairs={{0,64},{64,0},{1,65},{65,1},{2,66},{66,2},{3,67},{67,3},{4,68},{68... | collective-permute-start | bytes 393224 | tf_op jit(solution)/shard_map/ppermute | solution.py:277
  40.6 0.0 collective-permute-done.4
  40.6 2.4 %collective-permute-start.7 = (bf16[1,2,16,2048]{3,2,1,0:T(8,128)(2,1)S(1)}, bf16[1,2,16,2048]{3,2,1,0:T(8,128)(2,1)S(1)}, u32[]{:S(2)}, u32[]{:S(2)}) collective-permute-start(bf16[1,2,16,2048]{3,2,1,0:T(8,128)(2,1)S(1)} %bitcast.9), channel_id=1, source_target_pairs={{0,64},{64,0},{1,65},{65,1},{2,66},{66,2},{3,67},{67,3},{4,68},{68... | collective-permute-start | bytes 393224 | tf_op jit(solution)/shard_map/ppermute | solution.py:277
  43.1 0.0 all-to-all-done.found_ref
  43.1 15.0 %all_to_all.10.found_ref = s16[16,16,128]{2,1,0:T(8,128)(2,1)S(1)} all-to-all(s16[16,16,128]{2,1,0:T(8,128)(2,1)S(1)} %spread.1), channel_id=1, replica_groups=mesh['z_lo'=4,'core'=2,'z_hi'=2,'x'=4,'y'=8] {'core','z_hi','z_lo'}, dimensions={0} | all-to-all | bytes 131072 | tf_op jit(solution)/shard_map/all_to_all | solution.py:294
  58.1 3.8 %solve.1.weights_ref = bf16[16,128]{1,0:T(8,128)(2,1)S(1)} custom-call(s16[16,16,128]{2,1,0:T(8,128)(2,1)S(1)} %all_to_all.10.found_ref, f32[16,128]{1,0:T(8,128)S(1)} %get-tuple-element.20.noise_ref, f32[1,128]{1,0:T(1,128)S(1)} %get-tuple-element.21.data_ref, f32[1,128]{1,0:T(1,128)S(1)} %get-tuple-element.22.var_ref), custom_call_target="tpu_custom_call" | custom-call | flops 50000000 | bytes 18000000 | tf_op jit(solution)/shard_map/solve/pallas_call | solution.py:237
  61.9 0.0 collective-permute-done.5.refs_3_
  61.9 0.0 collective-permute-done.7.refs_5_
  61.9 0.0 collective-permute-done.6.refs_4_
  61.9 1.0 %increment.1 = f32[2,16,2048]{2,1,0:T(8,128)} custom-call(bf16[16,128]{1,0:T(8,128)(2,1)S(1)} %solve.1.weights_ref, f32[2,16,2048]{2,1,0:T(8,128)S(1)} %copy-done.1, bf16[1,2,16,2048]{3,2,1,0:T(8,128)(2,1)S(1)} %bitcast.8, bf16[2,2,16,2048]{3,2,1,0:T(8,128)(2,1)S(1)} %pad_maximum_fusion.refs_1_, bf16[1,2,16,2048]{3,2,1,0:T(8,128)(2,1)S(1)} %bitcast.10, ...), custom_call_target="tpu_custom_call" | custom-call | flops 20000000 | bytes 1700000 | tf_op jit(solution)/shard_map/increment/pallas_call | solution.py:262
  (5 shorter events, 0.1 us)
Async XLA Ops:
  0.6 20.6 %copy-start = (f32[2,16,2048]{2,1,0:T(8,128)S(1)}, f32[2,16,2048]{2,1,0:T(8,128)}, u32[]{:S(2)}) copy-start(f32[2,16,2048]{2,1,0:T(8,128)} %conc_ref.1) | copy-start | bytes 786436
  2.2 19.0 %collective-permute-start = (bf16[3,16,2048]{2,1,0:T(8,128)(2,1)S(1)}, bf16[3,16,2048]{2,1,0:T(8,128)(2,1)S(1)}, u32[]{:S(2)}, u32[]{:S(2)}) collective-permute-start(bf16[3,16,2048]{2,1,0:T(8,128)(2,1)S(1)} %get-tuple-element.15), channel_id=1, source_target_pairs={{1,2},{3,4},{5,6},{7,8},{9,10},{11,12},{13,14},{15,16},{17,18},{19... | collective-permute-start | bytes 589832 | tf_op jit(solution)/shard_map/ppermute | solution.py:277
  2.9 18.3 %collective-permute-start.1 = (bf16[3,16,2048]{2,1,0:T(8,128)(2,1)S(1)}, bf16[3,16,2048]{2,1,0:T(8,128)(2,1)S(1)}, u32[]{:S(2)}, u32[]{:S(2)}) collective-permute-start(bf16[3,16,2048]{2,1,0:T(8,128)(2,1)S(1)} %get-tuple-element.16), channel_id=1, source_target_pairs={{0,1},{2,3},{4,5},{6,7},{8,9},{10,11},{12,13},{14,15},{16,17},{18,... | collective-permute-start | bytes 589832 | tf_op jit(solution)/shard_map/ppermute | solution.py:277
  9.5 25.0 %collective-permute-start.3 = (bf16[2,16,2048]{2,1,0:T(8,128)(2,1)S(1)}, bf16[2,16,2048]{2,1,0:T(8,128)(2,1)S(1)}, u32[]{:S(2)}, u32[]{:S(2)}) collective-permute-start(bf16[2,16,2048]{2,1,0:T(8,128)(2,1)S(1)} %get-tuple-element.23), channel_id=1, source_target_pairs={{0,384},{128,256},{256,128},{384,0},{1,385},{129,257},{257,129},{3... | collective-permute-start | bytes 393224 | tf_op jit(solution)/shard_map/ppermute | solution.py:281
  17.1 17.4 %collective-permute-start.2 = (bf16[2,16,2048]{2,1,0:T(8,128)(2,1)S(1)}, bf16[2,16,2048]{2,1,0:T(8,128)(2,1)S(1)}, u32[]{:S(2)}, u32[]{:S(2)}) collective-permute-start(bf16[2,16,2048]{2,1,0:T(8,128)(2,1)S(1)} %get-tuple-element.23), channel_id=1, source_target_pairs={{0,256},{128,384},{256,0},{384,128},{1,257},{129,385},{257,1},{385... | collective-permute-start | bytes 393224 | tf_op jit(solution)/shard_map/ppermute | solution.py:281
  19.0 21.6 %collective-permute-start.4 = (bf16[2,16,2048]{2,1,0:T(8,128)(2,1)S(1)}, bf16[2,16,2048]{2,1,0:T(8,128)(2,1)S(1)}, u32[]{:S(2)}, u32[]{:S(2)}) collective-permute-start(bf16[2,16,2048]{2,1,0:T(8,128)(2,1)S(1)} %get-tuple-element.23), channel_id=1, source_target_pairs={{0,128},{128,0},{256,384},{384,256},{1,129},{129,1},{257,385},{385... | collective-permute-start | bytes 393224 | tf_op jit(solution)/shard_map/ppermute | solution.py:281
  22.6 20.5 %all-to-all-start = ((s16[32,16,128]{2,1,0:T(8,128)(2,1)}), s16[32,16,128]{2,1,0:T(8,128)(2,1)S(1)}, u32[]{:S(2)}, u32[]{:S(2)}) async-start(s16[32,16,128]{2,1,0:T(8,128)(2,1)} %get-tuple-element.19), calls=%async_computation | async-start | bytes 262144 | tf_op jit(solution)/shard_map/all_to_all | solution.py:293
  34.6 27.4 %copy-start.1 = (f32[2,16,2048]{2,1,0:T(8,128)S(1)}, f32[2,16,2048]{2,1,0:T(8,128)}, u32[]{:S(2)}) copy-start(f32[2,16,2048]{2,1,0:T(8,128)} %perm_ref.1) | copy-start | bytes 786436
  34.6 27.3 %collective-permute-start.6 = (bf16[2,2,16,2048]{3,2,1,0:T(8,128)(2,1)S(1)}, bf16[2,2,16,2048]{3,2,1,0:T(8,128)(2,1)S(1)}, u32[]{:S(2)}, u32[]{:S(2)}) collective-permute-start(bf16[2,2,16,2048]{3,2,1,0:T(8,128)(2,1)S(1)} %pad_maximum_fusion.refs_1_), channel_id=1, source_target_pairs={{0,64},{64,0},{1,65},{65,1},{2,66},{66,2},{3,67},{67,3},{4,68},{68... | collective-permute-start | bytes 786440 | tf_op jit(solution)/shard_map/ppermute | solution.py:277
  38.7 23.2 %collective-permute-start.5 = (bf16[1,2,16,2048]{3,2,1,0:T(8,128)(2,1)S(1)}, bf16[1,2,16,2048]{3,2,1,0:T(8,128)(2,1)S(1)}, u32[]{:S(2)}, u32[]{:S(2)}) collective-permute-start(bf16[1,2,16,2048]{3,2,1,0:T(8,128)(2,1)S(1)} %bitcast.7), channel_id=1, source_target_pairs={{0,64},{64,0},{1,65},{65,1},{2,66},{66,2},{3,67},{67,3},{4,68},{68... | collective-permute-start | bytes 393224 | tf_op jit(solution)/shard_map/ppermute | solution.py:277
  40.6 21.3 %collective-permute-start.7 = (bf16[1,2,16,2048]{3,2,1,0:T(8,128)(2,1)S(1)}, bf16[1,2,16,2048]{3,2,1,0:T(8,128)(2,1)S(1)}, u32[]{:S(2)}, u32[]{:S(2)}) collective-permute-start(bf16[1,2,16,2048]{3,2,1,0:T(8,128)(2,1)S(1)} %bitcast.9), channel_id=1, source_target_pairs={{0,64},{64,0},{1,65},{65,1},{2,66},{66,2},{3,67},{67,3},{4,68},{68... | collective-permute-start | bytes 393224 | tf_op jit(solution)/shard_map/ppermute | solution.py:277

commit v7 on v6

--- a/solution.py
+++ b/solution.py
@@ -225,8 +225,8 @@
     group = lax.axis_index(MEM)
     for position, flip in enumerate(ORDER):
         block = lax.bitwise_xor(group, flip)
-        place = 8 * lax.rem(block, 2) + block // 2
-        code = found_ref[place].astype(jnp.int32) + found_ref[place + 4].astype(jnp.int32)
+        place = 4 * lax.rem(block, 2) + block // 2
+        code = found_ref[place].astype(jnp.int32) + found_ref[place + 8].astype(jnp.int32)
         pred[pl.ds(position * 16, 16), :] = code.astype(F32) * (1 / GRAIN)
     centred = weights_of(pred[...], pred[0:16], noise_ref[...], data_ref[...], var_ref[...], work, solved)
     out_ref[...] = centred.astype(BF16)
@@ -269,6 +269,10 @@
 
 
 STRIPS = 64
+COLUMNS = [
+    [128 * z + 64 * core + 32 * half + column for half in (1, 0) for core in (0, 1) for z in range(4)]
+    for column in range(STRIPS // 2)
+]
 PLANES = [list(range(STRIPS // 2 - 1, -1, -1)), list(range(STRIPS // 2, STRIPS))]
 
 
@@ -291,7 +295,7 @@
     last, *pair = [crossed(low, flip) for flip in (1, 2, 3)]
     pair = jnp.stack(pair)
     found = lax.all_to_all(picked, SPACE, 0, 0, axis_index_groups=PLANES, tiled=True)
-    found = lax.all_to_all(spread(found, 16), ("core", "z_hi", "z_lo"), 0, 0, tiled=True)
+    found = lax.all_to_all(spread(found, 16), MEM + SPACE, 0, 0, axis_index_groups=COLUMNS, tiled=True)
     mine = [low[None], pair, last[None]]
     pieces = mine + [swapped(piece, "core", 0, 2) for piece in mine]
     weights = solve(found, noise, data, var)

time: 63.3 us -> 61.9 us (0.978)
  blocking collectives: 15 us -> 13.6 us
    all_to_all x1, blocking collectives: 15 us -> 13.6 us  [local(): lax.all_to_all(spread(found, 16), MEM + SPACE, 0, 0, axis_index_groups=CO...]
where the time goes in v7:
time: 61.9 us; the launch traced here: 61.5 us
  starting transfers between devices  39.3 us (63%)
  blocking collectives  13.6 us (22%)
  Pallas kernels  7.7 us (12%)
  between operations  0.82 us (1%)
    ppermute x5, starting transfers between devices, swapped(): lax.ppermute(value, axis, pairs + [(high, low) for low, high in pairs])  15.7 us
    all_to_all x1, blocking collectives, local(): lax.all_to_all(spread(found, 16), MEM + SPACE, 0, 0, axis_index_groups=CO...  13.6 us
    all_to_all x1, starting transfers between devices, local(): lax.all_to_all(picked, SPACE, 0, 0, axis_index_groups=PLANES, tiled=True)  11.9 us
    ppermute x3, starting transfers between devices, crossed(): return lax.ppermute(value, 'z_lo', [(i, i ^ flip) for i in range(4)])  11.7 us
    pallas_call x1, Pallas kernels, solve(): pl.pallas_call(solve_kernel, out_shape=jax.ShapeDtypeStruct((16, 128), BF...  3.8 us
    pallas_call x1, Pallas kernels, prepare(): pl.pallas_call(prepare_kernel, out_shape=(edge, edge, jax.ShapeDtypeStruc...  1.59 us
    pallas_call x1, Pallas kernels, advance(): pl.pallas_call(advance_kernel, out_shape=(jax.ShapeDtypeStruct(conc.shape...  1.32 us
  transfers between devices with their start and end apart: 9, of which 0 were waited for; matrix products, arithmetic and copies ran while one was open for 0% of the time, Pallas kernels for 8%

profile of v7, /device:TPU:1, one launch (start us, length us, event | category | flops | bytes accessed | tf_op | source)
XLA Modules:
  0.0 61.5 jit_solution(7406893831778904203)
XLA Ops:
  0.6 1.6 %prepare.1 = (bf16[3,16,2048]{2,1,0:T(8,128)(2,1)S(1)}, bf16[3,16,2048]{2,1,0:T(8,128)(2,1)S(1)}, bf16[2,16,2048]{2,1,0:T(8,128)(2,1)S(1)}, f32[2,16,2048]{2,1,0...) custom-call(f32[2,16,2048]{2,1,0:T(8,128)} %perm_ref.1, ...), custom_call_target="tpu_custom_call" | custom-call | flops 2000000 | bytes 1600000 | tf_op jit(solution)/shard_map/prepare/pallas_call | solution.py:130
  2.2 0.7 %collective-permute-start = (bf16[3,16,2048]{2,1,0:T(8,128)(2,1)S(1)}, bf16[3,16,2048]{2,1,0:T(8,128)(2,1)S(1)}, u32[]{:S(2)}, u32[]{:S(2)}) collective-permute-start(bf16[3,16,2048]{2,1,0:T(8,128)(2,1)S(1)} %get-tuple-element.15), channel_id=1, source_target_pairs={{1,2},{3,4},{5,6},{7,8},{9,10},{11,12},{13,14},{15,16},{17,18},{19... | collective-permute-start | bytes 589832 | tf_op jit(solution)/shard_map/ppermute | solution.py:281
  2.9 6.6 %collective-permute-start.1 = (bf16[3,16,2048]{2,1,0:T(8,128)(2,1)S(1)}, bf16[3,16,2048]{2,1,0:T(8,128)(2,1)S(1)}, u32[]{:S(2)}, u32[]{:S(2)}) collective-permute-start(bf16[3,16,2048]{2,1,0:T(8,128)(2,1)S(1)} %get-tuple-element.16), channel_id=1, source_target_pairs={{0,1},{2,3},{4,5},{6,7},{8,9},{10,11},{12,13},{14,15},{16,17},{18,... | collective-permute-start | bytes 589832 | tf_op jit(solution)/shard_map/ppermute | solution.py:281
  9.5 7.6 %collective-permute-start.3 = (bf16[2,16,2048]{2,1,0:T(8,128)(2,1)S(1)}, bf16[2,16,2048]{2,1,0:T(8,128)(2,1)S(1)}, u32[]{:S(2)}, u32[]{:S(2)}) collective-permute-start(bf16[2,16,2048]{2,1,0:T(8,128)(2,1)S(1)} %get-tuple-element.23), channel_id=1, source_target_pairs={{0,384},{128,256},{256,128},{384,0},{1,385},{129,257},{257,129},{3... | collective-permute-start | bytes 393224 | tf_op jit(solution)/shard_map/ppermute | solution.py:285
  17.1 1.9 %collective-permute-start.2 = (bf16[2,16,2048]{2,1,0:T(8,128)(2,1)S(1)}, bf16[2,16,2048]{2,1,0:T(8,128)(2,1)S(1)}, u32[]{:S(2)}, u32[]{:S(2)}) collective-permute-start(bf16[2,16,2048]{2,1,0:T(8,128)(2,1)S(1)} %get-tuple-element.23), channel_id=1, source_target_pairs={{0,256},{128,384},{256,0},{384,128},{1,257},{129,385},{257,1},{385... | collective-permute-start | bytes 393224 | tf_op jit(solution)/shard_map/ppermute | solution.py:285
  19.0 2.2 %collective-permute-start.4 = (bf16[2,16,2048]{2,1,0:T(8,128)(2,1)S(1)}, bf16[2,16,2048]{2,1,0:T(8,128)(2,1)S(1)}, u32[]{:S(2)}, u32[]{:S(2)}) collective-permute-start(bf16[2,16,2048]{2,1,0:T(8,128)(2,1)S(1)} %get-tuple-element.23), channel_id=1, source_target_pairs={{0,128},{128,0},{256,384},{384,256},{1,129},{129,1},{257,385},{385... | collective-permute-start | bytes 393224 | tf_op jit(solution)/shard_map/ppermute | solution.py:285
  21.2 0.0 collective-permute-done.far_ref
  21.3 0.0 collective-permute-done.1.near_ref
  21.3 1.3 %advance.1 = (f32[2,16,2048]{2,1,0:T(8,128)}, s16[32,16,128]{2,1,0:T(8,128)(2,1)}) custom-call(f32[2,16,2048]{2,1,0:T(8,128)S(1)} %copy-done, f32[2,16,2048]{2,1,0:T(8,128)S(1)} %get-tuple-element.13.conduct_ref, f32[2,16,2048]{2,1,0:T(8,128)S(1)} %get-tuple-element.14.part_ref, bf16[3,16,2048]{2,1,0:T(8,128)(2,1)S(1)} %collective-permute-done.far_ref, ...), custom_call_target="tpu_custom_call" | custom-call | flops 60000000 | bytes 1800000 | tf_op jit(solution)/shard_map/advance/pallas_call | solution.py:210
  22.6 11.9 %all-to-all-start = ((s16[32,16,128]{2,1,0:T(8,128)(2,1)}), s16[32,16,128]{2,1,0:T(8,128)(2,1)S(1)}, u32[]{:S(2)}, u32[]{:S(2)}) async-start(s16[32,16,128]{2,1,0:T(8,128)(2,1)} %get-tuple-element.19), calls=%async_computation | async-start | bytes 262144 | tf_op jit(solution)/shard_map/all_to_all | solution.py:297
  34.5 0.0 collective-permute-done.3
  34.5 0.0 collective-permute-done.2
  34.6 0.0 copy-start.1
  34.6 4.1 %collective-permute-start.6 = (bf16[2,2,16,2048]{3,2,1,0:T(8,128)(2,1)S(1)}, bf16[2,2,16,2048]{3,2,1,0:T(8,128)(2,1)S(1)}, u32[]{:S(2)}, u32[]{:S(2)}) collective-permute-start(bf16[2,2,16,2048]{3,2,1,0:T(8,128)(2,1)S(1)} %pad_maximum_fusion.refs_1_), channel_id=1, source_target_pairs={{0,64},{64,0},{1,65},{65,1},{2,66},{66,2},{3,67},{67,3},{4,68},{68... | collective-permute-start | bytes 786440 | tf_op jit(solution)/shard_map/ppermute | solution.py:281
  38.7 1.9 %collective-permute-start.5 = (bf16[1,2,16,2048]{3,2,1,0:T(8,128)(2,1)S(1)}, bf16[1,2,16,2048]{3,2,1,0:T(8,128)(2,1)S(1)}, u32[]{:S(2)}, u32[]{:S(2)}) collective-permute-start(bf16[1,2,16,2048]{3,2,1,0:T(8,128)(2,1)S(1)} %bitcast.7), channel_id=1, source_target_pairs={{0,64},{64,0},{1,65},{65,1},{2,66},{66,2},{3,67},{67,3},{4,68},{68... | collective-permute-start | bytes 393224 | tf_op jit(solution)/shard_map/ppermute | solution.py:281
  40.6 0.0 collective-permute-done.4
  40.6 2.4 %collective-permute-start.7 = (bf16[1,2,16,2048]{3,2,1,0:T(8,128)(2,1)S(1)}, bf16[1,2,16,2048]{3,2,1,0:T(8,128)(2,1)S(1)}, u32[]{:S(2)}, u32[]{:S(2)}) collective-permute-start(bf16[1,2,16,2048]{3,2,1,0:T(8,128)(2,1)S(1)} %bitcast.9), channel_id=1, source_target_pairs={{0,64},{64,0},{1,65},{65,1},{2,66},{66,2},{3,67},{67,3},{4,68},{68... | collective-permute-start | bytes 393224 | tf_op jit(solution)/shard_map/ppermute | solution.py:281
  43.1 0.0 all-to-all-done.found_ref
  43.1 13.6 %all_to_all.10.found_ref = s16[16,16,128]{2,1,0:T(8,128)(2,1)S(1)} all-to-all(s16[16,16,128]{2,1,0:T(8,128)(2,1)S(1)} %spread.1), channel_id=1, replica_groups={{32,160,288,416,96,224,352,480,0,128,256,384,64,192,320,448},{33,161,28..., dimensions={0} | all-to-all | bytes 131072 | tf_op jit(solution)/shard_map/all_to_all | solution.py:298
  56.7 3.8 %solve.1.weights_ref = bf16[16,128]{1,0:T(8,128)(2,1)S(1)} custom-call(s16[16,16,128]{2,1,0:T(8,128)(2,1)S(1)} %all_to_all.10.found_ref, f32[16,128]{1,0:T(8,128)S(1)} %get-tuple-element.20.noise_ref, f32[1,128]{1,0:T(1,128)S(1)} %get-tuple-element.21.data_ref, f32[1,128]{1,0:T(1,128)S(1)} %get-tuple-element.22.var_ref), custom_call_target="tpu_custom_call" | custom-call | flops 50000000 | bytes 18000000 | tf_op jit(solution)/shard_map/solve/pallas_call | solution.py:237
  60.5 0.0 collective-permute-done.5.refs_3_
  60.5 0.0 collective-permute-done.7.refs_5_
  60.5 0.0 collective-permute-done.6.refs_4_
  60.5 1.0 %increment.1 = f32[2,16,2048]{2,1,0:T(8,128)} custom-call(bf16[16,128]{1,0:T(8,128)(2,1)S(1)} %solve.1.weights_ref, f32[2,16,2048]{2,1,0:T(8,128)S(1)} %copy-done.1, bf16[1,2,16,2048]{3,2,1,0:T(8,128)(2,1)S(1)} %bitcast.8, bf16[2,2,16,2048]{3,2,1,0:T(8,128)(2,1)S(1)} %pad_maximum_fusion.refs_1_, bf16[1,2,16,2048]{3,2,1,0:T(8,128)(2,1)S(1)} %bitcast.10, ...), custom_call_target="tpu_custom_call" | custom-call | flops 20000000 | bytes 1700000 | tf_op jit(solution)/shard_map/increment/pallas_call | solution.py:262
  (5 shorter events, 0.1 us)
Async XLA Ops:
  0.6 20.6 %copy-start = (f32[2,16,2048]{2,1,0:T(8,128)S(1)}, f32[2,16,2048]{2,1,0:T(8,128)}, u32[]{:S(2)}) copy-start(f32[2,16,2048]{2,1,0:T(8,128)} %conc_ref.1) | copy-start | bytes 786436
  2.2 19.0 %collective-permute-start = (bf16[3,16,2048]{2,1,0:T(8,128)(2,1)S(1)}, bf16[3,16,2048]{2,1,0:T(8,128)(2,1)S(1)}, u32[]{:S(2)}, u32[]{:S(2)}) collective-permute-start(bf16[3,16,2048]{2,1,0:T(8,128)(2,1)S(1)} %get-tuple-element.15), channel_id=1, source_target_pairs={{1,2},{3,4},{5,6},{7,8},{9,10},{11,12},{13,14},{15,16},{17,18},{19... | collective-permute-start | bytes 589832 | tf_op jit(solution)/shard_map/ppermute | solution.py:281
  2.9 18.3 %collective-permute-start.1 = (bf16[3,16,2048]{2,1,0:T(8,128)(2,1)S(1)}, bf16[3,16,2048]{2,1,0:T(8,128)(2,1)S(1)}, u32[]{:S(2)}, u32[]{:S(2)}) collective-permute-start(bf16[3,16,2048]{2,1,0:T(8,128)(2,1)S(1)} %get-tuple-element.16), channel_id=1, source_target_pairs={{0,1},{2,3},{4,5},{6,7},{8,9},{10,11},{12,13},{14,15},{16,17},{18,... | collective-permute-start | bytes 589832 | tf_op jit(solution)/shard_map/ppermute | solution.py:281
  9.5 25.0 %collective-permute-start.3 = (bf16[2,16,2048]{2,1,0:T(8,128)(2,1)S(1)}, bf16[2,16,2048]{2,1,0:T(8,128)(2,1)S(1)}, u32[]{:S(2)}, u32[]{:S(2)}) collective-permute-start(bf16[2,16,2048]{2,1,0:T(8,128)(2,1)S(1)} %get-tuple-element.23), channel_id=1, source_target_pairs={{0,384},{128,256},{256,128},{384,0},{1,385},{129,257},{257,129},{3... | collective-permute-start | bytes 393224 | tf_op jit(solution)/shard_map/ppermute | solution.py:285
  17.1 17.4 %collective-permute-start.2 = (bf16[2,16,2048]{2,1,0:T(8,128)(2,1)S(1)}, bf16[2,16,2048]{2,1,0:T(8,128)(2,1)S(1)}, u32[]{:S(2)}, u32[]{:S(2)}) collective-permute-start(bf16[2,16,2048]{2,1,0:T(8,128)(2,1)S(1)} %get-tuple-element.23), channel_id=1, source_target_pairs={{0,256},{128,384},{256,0},{384,128},{1,257},{129,385},{257,1},{385... | collective-permute-start | bytes 393224 | tf_op jit(solution)/shard_map/ppermute | solution.py:285
  19.0 21.6 %collective-permute-start.4 = (bf16[2,16,2048]{2,1,0:T(8,128)(2,1)S(1)}, bf16[2,16,2048]{2,1,0:T(8,128)(2,1)S(1)}, u32[]{:S(2)}, u32[]{:S(2)}) collective-permute-start(bf16[2,16,2048]{2,1,0:T(8,128)(2,1)S(1)} %get-tuple-element.23), channel_id=1, source_target_pairs={{0,128},{128,0},{256,384},{384,256},{1,129},{129,1},{257,385},{385... | collective-permute-start | bytes 393224 | tf_op jit(solution)/shard_map/ppermute | solution.py:285
  22.6 20.5 %all-to-all-start = ((s16[32,16,128]{2,1,0:T(8,128)(2,1)}), s16[32,16,128]{2,1,0:T(8,128)(2,1)S(1)}, u32[]{:S(2)}, u32[]{:S(2)}) async-start(s16[32,16,128]{2,1,0:T(8,128)(2,1)} %get-tuple-element.19), calls=%async_computation | async-start | bytes 262144 | tf_op jit(solution)/shard_map/all_to_all | solution.py:297
  34.6 26.0 %copy-start.1 = (f32[2,16,2048]{2,1,0:T(8,128)S(1)}, f32[2,16,2048]{2,1,0:T(8,128)}, u32[]{:S(2)}) copy-start(f32[2,16,2048]{2,1,0:T(8,128)} %perm_ref.1) | copy-start | bytes 786436
  34.6 25.9 %collective-permute-start.6 = (bf16[2,2,16,2048]{3,2,1,0:T(8,128)(2,1)S(1)}, bf16[2,2,16,2048]{3,2,1,0:T(8,128)(2,1)S(1)}, u32[]{:S(2)}, u32[]{:S(2)}) collective-permute-start(bf16[2,2,16,2048]{3,2,1,0:T(8,128)(2,1)S(1)} %pad_maximum_fusion.refs_1_), channel_id=1, source_target_pairs={{0,64},{64,0},{1,65},{65,1},{2,66},{66,2},{3,67},{67,3},{4,68},{68... | collective-permute-start | bytes 786440 | tf_op jit(solution)/shard_map/ppermute | solution.py:281
  38.7 21.8 %collective-permute-start.5 = (bf16[1,2,16,2048]{3,2,1,0:T(8,128)(2,1)S(1)}, bf16[1,2,16,2048]{3,2,1,0:T(8,128)(2,1)S(1)}, u32[]{:S(2)}, u32[]{:S(2)}) collective-permute-start(bf16[1,2,16,2048]{3,2,1,0:T(8,128)(2,1)S(1)} %bitcast.7), channel_id=1, source_target_pairs={{0,64},{64,0},{1,65},{65,1},{2,66},{66,2},{3,67},{67,3},{4,68},{68... | collective-permute-start | bytes 393224 | tf_op jit(solution)/shard_map/ppermute | solution.py:281
  40.6 19.9 %collective-permute-start.7 = (bf16[1,2,16,2048]{3,2,1,0:T(8,128)(2,1)S(1)}, bf16[1,2,16,2048]{3,2,1,0:T(8,128)(2,1)S(1)}, u32[]{:S(2)}, u32[]{:S(2)}) collective-permute-start(bf16[1,2,16,2048]{3,2,1,0:T(8,128)(2,1)S(1)} %bitcast.9), channel_id=1, source_target_pairs={{0,64},{64,0},{1,65},{65,1},{2,66},{66,2},{3,67},{67,3},{4,68},{68... | collective-permute-start | bytes 393224 | tf_op jit(solution)/shard_map/ppermute | solution.py:281

commit v8 on v7

--- a/solution.py
+++ b/solution.py
@@ -14,7 +14,7 @@
 GRAIN = 32000 / 6
 MEM = ("z_lo", "core")
 SPACE = ("z_hi", "x", "y")
-ORDER = (0, 4, 6, 2, 1, 5, 7, 3)
+ORDER = (0, 2, 4, 6, 1, 3, 5, 7)
 VMEM_LIMIT = 48 * 1024 * 1024
 
 def split3(x):
@@ -292,7 +292,7 @@
     far = swapped(far, SPACE, 1, STRIPS)
     near = swapped(near, SPACE, 0, STRIPS)
     tracer, picked = advance(concentration, conduct, part, far, near, wells, 32)
-    last, *pair = [crossed(low, flip) for flip in (1, 2, 3)]
+    last, *pair = [crossed(low, flip) for flip in (3, 1, 2)]
     pair = jnp.stack(pair)
     found = lax.all_to_all(picked, SPACE, 0, 0, axis_index_groups=PLANES, tiled=True)
     found = lax.all_to_all(spread(found, 16), MEM + SPACE, 0, 0, axis_index_groups=COLUMNS, tiled=True)

time: 61.9 us -> 61.9 us (level)
  no operation moved by 1% of the time
where the time goes in v8:
time: 61.9 us; the launch traced here: 61.5 us
  starting transfers between devices  39.3 us (63%)
  blocking collectives  13.6 us (22%)
  Pallas kernels  7.7 us (12%)
  between operations  0.82 us (1%)
    ppermute x5, starting transfers between devices, swapped(): lax.ppermute(value, axis, pairs + [(high, low) for low, high in pairs])  15.7 us
    all_to_all x1, blocking collectives, local(): lax.all_to_all(spread(found, 16), MEM + SPACE, 0, 0, axis_index_groups=CO...  13.6 us
    all_to_all x1, starting transfers between devices, local(): lax.all_to_all(picked, SPACE, 0, 0, axis_index_groups=PLANES, tiled=True)  11.9 us
    ppermute x3, starting transfers between devices, crossed(): return lax.ppermute(value, 'z_lo', [(i, i ^ flip) for i in range(4)])  11.7 us
    pallas_call x1, Pallas kernels, solve(): pl.pallas_call(solve_kernel, out_shape=jax.ShapeDtypeStruct((16, 128), BF...  3.8 us
    pallas_call x1, Pallas kernels, prepare(): pl.pallas_call(prepare_kernel, out_shape=(edge, edge, jax.ShapeDtypeStruc...  1.59 us
    pallas_call x1, Pallas kernels, advance(): pl.pallas_call(advance_kernel, out_shape=(jax.ShapeDtypeStruct(conc.shape...  1.32 us
  transfers between devices with their start and end apart: 9, of which 0 were waited for; matrix products, arithmetic and copies ran while one was open for 0% of the time, Pallas kernels for 8%

profile of v8, /device:TPU:1, one launch (start us, length us, event | category | flops | bytes accessed | tf_op | source)
XLA Modules:
  0.0 61.5 jit_solution(17463553459514741615)
XLA Ops:
  0.6 1.6 %prepare.1 = (bf16[3,16,2048]{2,1,0:T(8,128)(2,1)S(1)}, bf16[3,16,2048]{2,1,0:T(8,128)(2,1)S(1)}, bf16[2,16,2048]{2,1,0:T(8,128)(2,1)S(1)}, f32[2,16,2048]{2,1,0...) custom-call(f32[2,16,2048]{2,1,0:T(8,128)} %perm_ref.1, ...), custom_call_target="tpu_custom_call" | custom-call | flops 2000000 | bytes 1600000 | tf_op jit(solution)/shard_map/prepare/pallas_call | solution.py:130
  2.2 0.7 %collective-permute-start = (bf16[3,16,2048]{2,1,0:T(8,128)(2,1)S(1)}, bf16[3,16,2048]{2,1,0:T(8,128)(2,1)S(1)}, u32[]{:S(2)}, u32[]{:S(2)}) collective-permute-start(bf16[3,16,2048]{2,1,0:T(8,128)(2,1)S(1)} %get-tuple-element.15), channel_id=1, source_target_pairs={{1,2},{3,4},{5,6},{7,8},{9,10},{11,12},{13,14},{15,16},{17,18},{19... | collective-permute-start | bytes 589832 | tf_op jit(solution)/shard_map/ppermute | solution.py:281
  2.9 6.6 %collective-permute-start.1 = (bf16[3,16,2048]{2,1,0:T(8,128)(2,1)S(1)}, bf16[3,16,2048]{2,1,0:T(8,128)(2,1)S(1)}, u32[]{:S(2)}, u32[]{:S(2)}) collective-permute-start(bf16[3,16,2048]{2,1,0:T(8,128)(2,1)S(1)} %get-tuple-element.16), channel_id=1, source_target_pairs={{0,1},{2,3},{4,5},{6,7},{8,9},{10,11},{12,13},{14,15},{16,17},{18,... | collective-permute-start | bytes 589832 | tf_op jit(solution)/shard_map/ppermute | solution.py:281
  9.5 5.8 %collective-permute-start.3 = (bf16[2,16,2048]{2,1,0:T(8,128)(2,1)S(1)}, bf16[2,16,2048]{2,1,0:T(8,128)(2,1)S(1)}, u32[]{:S(2)}, u32[]{:S(2)}) collective-permute-start(bf16[2,16,2048]{2,1,0:T(8,128)(2,1)S(1)} %get-tuple-element.23), channel_id=1, source_target_pairs={{0,256},{128,384},{256,0},{384,128},{1,257},{129,385},{257,1},{385... | collective-permute-start | bytes 393224 | tf_op jit(solution)/shard_map/ppermute | solution.py:285
  15.3 4.0 %collective-permute-start.2 = (bf16[2,16,2048]{2,1,0:T(8,128)(2,1)S(1)}, bf16[2,16,2048]{2,1,0:T(8,128)(2,1)S(1)}, u32[]{:S(2)}, u32[]{:S(2)}) collective-permute-start(bf16[2,16,2048]{2,1,0:T(8,128)(2,1)S(1)} %get-tuple-element.23), channel_id=1, source_target_pairs={{0,128},{128,0},{256,384},{384,256},{1,129},{129,1},{257,385},{385... | collective-permute-start | bytes 393224 | tf_op jit(solution)/shard_map/ppermute | solution.py:285
  19.3 1.9 %collective-permute-start.4 = (bf16[2,16,2048]{2,1,0:T(8,128)(2,1)S(1)}, bf16[2,16,2048]{2,1,0:T(8,128)(2,1)S(1)}, u32[]{:S(2)}, u32[]{:S(2)}) collective-permute-start(bf16[2,16,2048]{2,1,0:T(8,128)(2,1)S(1)} %get-tuple-element.23), channel_id=1, source_target_pairs={{0,384},{128,256},{256,128},{384,0},{1,385},{129,257},{257,129},{3... | collective-permute-start | bytes 393224 | tf_op jit(solution)/shard_map/ppermute | solution.py:285
  21.2 0.0 collective-permute-done.far_ref
  21.3 0.0 collective-permute-done.1.near_ref
  21.3 1.3 %advance.1 = (f32[2,16,2048]{2,1,0:T(8,128)}, s16[32,16,128]{2,1,0:T(8,128)(2,1)}) custom-call(f32[2,16,2048]{2,1,0:T(8,128)S(1)} %copy-done, f32[2,16,2048]{2,1,0:T(8,128)S(1)} %get-tuple-element.13.conduct_ref, f32[2,16,2048]{2,1,0:T(8,128)S(1)} %get-tuple-element.14.part_ref, bf16[3,16,2048]{2,1,0:T(8,128)(2,1)S(1)} %collective-permute-done.far_ref, ...), custom_call_target="tpu_custom_call" | custom-call | flops 60000000 | bytes 1800000 | tf_op jit(solution)/shard_map/advance/pallas_call | solution.py:210
  22.6 11.9 %all-to-all-start = ((s16[32,16,128]{2,1,0:T(8,128)(2,1)}), s16[32,16,128]{2,1,0:T(8,128)(2,1)S(1)}, u32[]{:S(2)}, u32[]{:S(2)}) async-start(s16[32,16,128]{2,1,0:T(8,128)(2,1)} %get-tuple-element.19), calls=%async_computation | async-start | bytes 262144 | tf_op jit(solution)/shard_map/all_to_all | solution.py:297
  34.5 0.0 collective-permute-done.3
  34.5 0.0 collective-permute-done.2
  34.6 0.0 copy-start.1
  34.6 4.1 %collective-permute-start.6 = (bf16[2,2,16,2048]{3,2,1,0:T(8,128)(2,1)S(1)}, bf16[2,2,16,2048]{3,2,1,0:T(8,128)(2,1)S(1)}, u32[]{:S(2)}, u32[]{:S(2)}) collective-permute-start(bf16[2,2,16,2048]{3,2,1,0:T(8,128)(2,1)S(1)} %pad_maximum_fusion.refs_1_), channel_id=1, source_target_pairs={{0,64},{64,0},{1,65},{65,1},{2,66},{66,2},{3,67},{67,3},{4,68},{68... | collective-permute-start | bytes 786440 | tf_op jit(solution)/shard_map/ppermute | solution.py:281
  38.7 1.9 %collective-permute-start.5 = (bf16[1,2,16,2048]{3,2,1,0:T(8,128)(2,1)S(1)}, bf16[1,2,16,2048]{3,2,1,0:T(8,128)(2,1)S(1)}, u32[]{:S(2)}, u32[]{:S(2)}) collective-permute-start(bf16[1,2,16,2048]{3,2,1,0:T(8,128)(2,1)S(1)} %bitcast.7), channel_id=1, source_target_pairs={{0,64},{64,0},{1,65},{65,1},{2,66},{66,2},{3,67},{67,3},{4,68},{68... | collective-permute-start | bytes 393224 | tf_op jit(solution)/shard_map/ppermute | solution.py:281
  40.6 0.0 collective-permute-done.4
  40.6 2.4 %collective-permute-start.7 = (bf16[1,2,16,2048]{3,2,1,0:T(8,128)(2,1)S(1)}, bf16[1,2,16,2048]{3,2,1,0:T(8,128)(2,1)S(1)}, u32[]{:S(2)}, u32[]{:S(2)}) collective-permute-start(bf16[1,2,16,2048]{3,2,1,0:T(8,128)(2,1)S(1)} %bitcast.9), channel_id=1, source_target_pairs={{0,64},{64,0},{1,65},{65,1},{2,66},{66,2},{3,67},{67,3},{4,68},{68... | collective-permute-start | bytes 393224 | tf_op jit(solution)/shard_map/ppermute | solution.py:281
  43.1 0.0 all-to-all-done.found_ref
  43.1 13.6 %all_to_all.10.found_ref = s16[16,16,128]{2,1,0:T(8,128)(2,1)S(1)} all-to-all(s16[16,16,128]{2,1,0:T(8,128)(2,1)S(1)} %spread.1), channel_id=1, replica_groups={{32,160,288,416,96,224,352,480,0,128,256,384,64,192,320,448},{33,161,28..., dimensions={0} | all-to-all | bytes 131072 | tf_op jit(solution)/shard_map/all_to_all | solution.py:298
  56.7 3.8 %solve.1.weights_ref = bf16[16,128]{1,0:T(8,128)(2,1)S(1)} custom-call(s16[16,16,128]{2,1,0:T(8,128)(2,1)S(1)} %all_to_all.10.found_ref, f32[16,128]{1,0:T(8,128)S(1)} %get-tuple-element.20.noise_ref, f32[1,128]{1,0:T(1,128)S(1)} %get-tuple-element.21.data_ref, f32[1,128]{1,0:T(1,128)S(1)} %get-tuple-element.22.var_ref), custom_call_target="tpu_custom_call" | custom-call | flops 50000000 | bytes 18000000 | tf_op jit(solution)/shard_map/solve/pallas_call | solution.py:237
  60.5 0.0 collective-permute-done.5.refs_3_
  60.5 0.0 collective-permute-done.7.refs_5_
  60.5 0.0 collective-permute-done.6.refs_4_
  60.5 1.0 %increment.1 = f32[2,16,2048]{2,1,0:T(8,128)} custom-call(bf16[16,128]{1,0:T(8,128)(2,1)S(1)} %solve.1.weights_ref, f32[2,16,2048]{2,1,0:T(8,128)S(1)} %copy-done.1, bf16[1,2,16,2048]{3,2,1,0:T(8,128)(2,1)S(1)} %bitcast.8, bf16[2,2,16,2048]{3,2,1,0:T(8,128)(2,1)S(1)} %pad_maximum_fusion.refs_1_, bf16[1,2,16,2048]{3,2,1,0:T(8,128)(2,1)S(1)} %bitcast.10, ...), custom_call_target="tpu_custom_call" | custom-call | flops 20000000 | bytes 1700000 | tf_op jit(solution)/shard_map/increment/pallas_call | solution.py:262
  (5 shorter events, 0.1 us)
Async XLA Ops:
  0.6 20.6 %copy-start = (f32[2,16,2048]{2,1,0:T(8,128)S(1)}, f32[2,16,2048]{2,1,0:T(8,128)}, u32[]{:S(2)}) copy-start(f32[2,16,2048]{2,1,0:T(8,128)} %conc_ref.1) | copy-start | bytes 786436
  2.2 19.0 %collective-permute-start = (bf16[3,16,2048]{2,1,0:T(8,128)(2,1)S(1)}, bf16[3,16,2048]{2,1,0:T(8,128)(2,1)S(1)}, u32[]{:S(2)}, u32[]{:S(2)}) collective-permute-start(bf16[3,16,2048]{2,1,0:T(8,128)(2,1)S(1)} %get-tuple-element.15), channel_id=1, source_target_pairs={{1,2},{3,4},{5,6},{7,8},{9,10},{11,12},{13,14},{15,16},{17,18},{19... | collective-permute-start | bytes 589832 | tf_op jit(solution)/shard_map/ppermute | solution.py:281
  2.9 18.3 %collective-permute-start.1 = (bf16[3,16,2048]{2,1,0:T(8,128)(2,1)S(1)}, bf16[3,16,2048]{2,1,0:T(8,128)(2,1)S(1)}, u32[]{:S(2)}, u32[]{:S(2)}) collective-permute-start(bf16[3,16,2048]{2,1,0:T(8,128)(2,1)S(1)} %get-tuple-element.16), channel_id=1, source_target_pairs={{0,1},{2,3},{4,5},{6,7},{8,9},{10,11},{12,13},{14,15},{16,17},{18,... | collective-permute-start | bytes 589832 | tf_op jit(solution)/shard_map/ppermute | solution.py:281
  9.5 25.0 %collective-permute-start.3 = (bf16[2,16,2048]{2,1,0:T(8,128)(2,1)S(1)}, bf16[2,16,2048]{2,1,0:T(8,128)(2,1)S(1)}, u32[]{:S(2)}, u32[]{:S(2)}) collective-permute-start(bf16[2,16,2048]{2,1,0:T(8,128)(2,1)S(1)} %get-tuple-element.23), channel_id=1, source_target_pairs={{0,256},{128,384},{256,0},{384,128},{1,257},{129,385},{257,1},{385... | collective-permute-start | bytes 393224 | tf_op jit(solution)/shard_map/ppermute | solution.py:285
  15.3 19.2 %collective-permute-start.2 = (bf16[2,16,2048]{2,1,0:T(8,128)(2,1)S(1)}, bf16[2,16,2048]{2,1,0:T(8,128)(2,1)S(1)}, u32[]{:S(2)}, u32[]{:S(2)}) collective-permute-start(bf16[2,16,2048]{2,1,0:T(8,128)(2,1)S(1)} %get-tuple-element.23), channel_id=1, source_target_pairs={{0,128},{128,0},{256,384},{384,256},{1,129},{129,1},{257,385},{385... | collective-permute-start | bytes 393224 | tf_op jit(solution)/shard_map/ppermute | solution.py:285
  19.3 21.3 %collective-permute-start.4 = (bf16[2,16,2048]{2,1,0:T(8,128)(2,1)S(1)}, bf16[2,16,2048]{2,1,0:T(8,128)(2,1)S(1)}, u32[]{:S(2)}, u32[]{:S(2)}) collective-permute-start(bf16[2,16,2048]{2,1,0:T(8,128)(2,1)S(1)} %get-tuple-element.23), channel_id=1, source_target_pairs={{0,384},{128,256},{256,128},{384,0},{1,385},{129,257},{257,129},{3... | collective-permute-start | bytes 393224 | tf_op jit(solution)/shard_map/ppermute | solution.py:285
  22.6 20.5 %all-to-all-start = ((s16[32,16,128]{2,1,0:T(8,128)(2,1)}), s16[32,16,128]{2,1,0:T(8,128)(2,1)S(1)}, u32[]{:S(2)}, u32[]{:S(2)}) async-start(s16[32,16,128]{2,1,0:T(8,128)(2,1)} %get-tuple-element.19), calls=%async_computation | async-start | bytes 262144 | tf_op jit(solution)/shard_map/all_to_all | solution.py:297
  34.6 26.0 %copy-start.1 = (f32[2,16,2048]{2,1,0:T(8,128)S(1)}, f32[2,16,2048]{2,1,0:T(8,128)}, u32[]{:S(2)}) copy-start(f32[2,16,2048]{2,1,0:T(8,128)} %perm_ref.1) | copy-start | bytes 786436
  34.6 25.9 %collective-permute-start.6 = (bf16[2,2,16,2048]{3,2,1,0:T(8,128)(2,1)S(1)}, bf16[2,2,16,2048]{3,2,1,0:T(8,128)(2,1)S(1)}, u32[]{:S(2)}, u32[]{:S(2)}) collective-permute-start(bf16[2,2,16,2048]{3,2,1,0:T(8,128)(2,1)S(1)} %pad_maximum_fusion.refs_1_), channel_id=1, source_target_pairs={{0,64},{64,0},{1,65},{65,1},{2,66},{66,2},{3,67},{67,3},{4,68},{68... | collective-permute-start | bytes 786440 | tf_op jit(solution)/shard_map/ppermute | solution.py:281
  38.7 21.8 %collective-permute-start.5 = (bf16[1,2,16,2048]{3,2,1,0:T(8,128)(2,1)S(1)}, bf16[1,2,16,2048]{3,2,1,0:T(8,128)(2,1)S(1)}, u32[]{:S(2)}, u32[]{:S(2)}) collective-permute-start(bf16[1,2,16,2048]{3,2,1,0:T(8,128)(2,1)S(1)} %bitcast.7), channel_id=1, source_target_pairs={{0,64},{64,0},{1,65},{65,1},{2,66},{66,2},{3,67},{67,3},{4,68},{68... | collective-permute-start | bytes 393224 | tf_op jit(solution)/shard_map/ppermute | solution.py:281
  40.6 19.9 %collective-permute-start.7 = (bf16[1,2,16,2048]{3,2,1,0:T(8,128)(2,1)S(1)}, bf16[1,2,16,2048]{3,2,1,0:T(8,128)(2,1)S(1)}, u32[]{:S(2)}, u32[]{:S(2)}) collective-permute-start(bf16[1,2,16,2048]{3,2,1,0:T(8,128)(2,1)S(1)} %bitcast.9), channel_id=1, source_target_pairs={{0,64},{64,0},{1,65},{65,1},{2,66},{66,2},{3,67},{67,3},{4,68},{68... | collective-permute-start | bytes 393224 | tf_op jit(solution)/shard_map/ppermute | solution.py:281
